TPU v7x, 128 devices: a whole 4x4x4 slice. The times are simulated.
128 devices in a mesh: depth: 2 (over core), lat: 64 (over z, y, x).
Axes of the slice: x: 4, y: 4, z: 4, core: 2. Of those that a mesh axis runs over, the one named last changes fastest.
Arguments:
- object_slices: float32 [2, 2, 16384, 2048], P('depth', None, 'lat'), may hold values from -1.1 to 1.1, as said below
- probe: float32 [2, 256, 256], replicated, may hold values from -6 to 6
- measured: float32 [256, 256, 256], P('lat'), may hold values from 0.2 to 3
- positions: int32 [256, 2], P('lat'), may hold values from 0 to 1792, as said below
- counts: int32 [64], P('lat'), may hold values from 1 to 4, 160 in all
Outputs:
- object_gradient: float32 [2, 2, 16384, 2048], P('depth', None, 'lat')
Inputs may be any that keep to these rules, and one draw needn't show every extreme that they name: `object_slices`: each transmission value has modulus at most 1.1. `positions`: column 0 is a row offset within the slot's own tile, from 0 to 255; column 1 is a column offset from 0 to 1792; both ends are reached. `counts`: every tile uses at least one slot; some tile uses all 4.
All inputs are finite; a program needn't handle non-finite values. No bound on the sum of `counts` on one device may be relied on, other than what follows from the above.
Results may differ from a plain program's by a relative error of at most 0.0003.
Values sent between devices are 32-bit elements; how exact they have to be, the bound alone decides.
A program may use at most 128 MiB of HBM per device.

v0:
```python
import math

import jax
import jax.numpy as jnp
from jax import lax
from jax.sharding import PartitionSpec as P

fresnel_strength = 8.0


def from_behind(value, axis, by):
    length = lax.axis_size(axis)
    return lax.ppermute(value, axis, [(i, (i + by) % length) for i in range(length)])


def from_behind_2(value, axis, steps):
    count = lax.axis_size(axis)
    initial, last = (max(0, -steps), min(count, count - steps))
    return lax.ppermute(value, axis, [(source, source + steps) for source in range(initial, last)])


def dft_tables(length):
    index = jnp.arange(length, dtype=jnp.int32)
    product = index[:, None] * index[None, :] % length
    angle = 2.0 * math.pi / length * product.astype(jnp.float32)
    scale = 1.0 / math.sqrt(length)
    return (jnp.cos(angle) * scale, jnp.sin(angle) * scale)


def kernel_tables(length):
    index = jnp.arange(length, dtype=jnp.int32)
    centred = (index - length * (index >= length // 2).astype(jnp.int32)).astype(
        jnp.float32
    ) / length
    phase = math.pi * fresnel_strength * (centred[:, None] ** 2 + centred[None, :] ** 2)
    return (jnp.cos(phase), jnp.sin(phase))


def left_product(matrix, values):
    return jnp.einsum("jk,...kl->...jl", matrix, values, precision=lax.Precision.HIGHEST)


def right_product(values, matrix):
    return jnp.einsum("...jk,kl->...jl", values, matrix, precision=lax.Precision.HIGHEST)


def transform(values, tables, sign):
    cosine, sine = tables
    sine = sine * sign
    left_real = left_product(cosine, values[0]) - left_product(sine, values[1])
    left_imaginary = left_product(cosine, values[1]) + left_product(sine, values[0])
    out_real = right_product(left_real, cosine) - right_product(left_imaginary, sine)
    out_imaginary = right_product(left_imaginary, cosine) + right_product(left_real, sine)
    return jnp.stack([out_real, out_imaginary])


def complex_product(first, second):
    return jnp.stack(
        [first[0] * second[0] - first[1] * second[1], first[0] * second[1] + first[1] * second[0]]
    )


def conj_product(first, second):
    return jnp.stack(
        [first[0] * second[0] + first[1] * second[1], first[0] * second[1] - first[1] * second[0]]
    )


def propagate(values, tables, kernel, sign):
    spectrum = transform(values, tables, -1.0)
    turned = complex_product(spectrum, jnp.stack([kernel[0], sign * kernel[1]]))
    return transform(turned, tables, 1.0)


def forward_group(wave, windows, tables, kernel):
    inputs = [wave]
    slab = jnp.moveaxis(windows[:, 0], 1, 0)
    wave = propagate(complex_product(wave, slab), tables, kernel, 1.0)
    return (wave, jnp.stack(inputs))


def backward_group(back, windows, stored, tables, kernel):
    layers = windows.shape[1]
    pieces = [None] * layers
    for layer in reversed(range(layers)):
        adjoint = propagate(back, tables, kernel, -1.0)
        pieces[layer] = conj_product(stored[layer], adjoint)
        slab = jnp.moveaxis(windows[:, layer], 1, 0)
        back = conj_product(slab, adjoint)
    return (back, jnp.stack(pieces))


def detector(wave, measured, live, tables):
    far = transform(wave, tables, -1.0)
    factor = live[:, None, None] * (
        1.0 - measured / jnp.sqrt(far[0] * far[0] + far[1] * far[1] + 1.0)
    )
    return transform(far * factor, tables, 1.0)


def shards(object_slices, probe, measured, positions, counts):
    layers = object_slices.shape[0]
    tile_rows = object_slices.shape[2]
    columns = object_slices.shape[3]
    width = probe.shape[1]
    slots = positions.shape[0]
    tables = dft_tables(width)
    kernel = kernel_tables(width)
    live = (jnp.arange(slots, dtype=jnp.int32) < counts[0]).astype(jnp.float32)
    depth_index = lax.axis_index("depth")
    groups = lax.axis_size("depth")
    last = groups - 1
    rim = from_behind(object_slices, "lat", -1)
    extended = jnp.concatenate([object_slices, rim], axis=2)

    def cut_window(place):
        return lax.dynamic_slice(extended, (0, 0, place[0], place[1]), (layers, 2, width, width))

    windows = jax.vmap(cut_window)(positions)
    entering = jnp.broadcast_to(probe[:, None], (2, slots, width, width))
    stored = jnp.zeros((layers, 2, slots, width, width), jnp.float32)
    wave = entering

    def run_forward(wave_now, stored_now):
        return forward_group(wave_now, windows, tables, kernel)

    def skip_forward(wave_now, stored_now):
        return (wave_now, stored_now)

    for section in range(groups):
        leaving, stored = lax.cond(depth_index == section, run_forward, skip_forward, wave, stored)
        if section + 1 < groups:
            moved = from_behind_2(leaving, "depth", 1)
            wave = jnp.where(depth_index == 0, entering, moved)

    def run_detector(wave_now):
        return detector(wave_now, measured, live, tables)

    def skip_detector(wave_now):
        return jnp.zeros_like(wave_now)

    start = lax.cond(depth_index == last, run_detector, skip_detector, leaving)
    grads = jnp.zeros((layers, 2, slots, width, width), jnp.float32)
    back = start

    def run_backward(back_now, grads_now):
        return backward_group(back_now, windows, stored, tables, kernel)

    def skip_backward(back_now, grads_now):
        return (back_now, grads_now)

    for section in reversed(range(groups)):
        returned, grads = lax.cond(depth_index == section, run_backward, skip_backward, back, grads)
        if section > 0:
            moved = from_behind_2(returned, "depth", -1)
            back = jnp.where(depth_index == last, start, moved)
    widened = jnp.zeros((layers, 2, tile_rows + width, columns), jnp.float32)

    def add_window(slot_number, total):
        place = positions[slot_number]
        piece = lax.dynamic_index_in_dim(grads, slot_number, 2, keepdims=False)
        corner = (0, 0, place[0], place[1])
        current = lax.dynamic_slice(total, corner, piece.shape)
        return lax.dynamic_update_slice(total, current + piece, corner)

    widened = lax.fori_loop(0, slots, add_window, widened)
    spill = from_behind(widened[:, :, tile_rows:, :], "lat", 1)
    result = widened[:, :, :tile_rows, :]
    result = result.at[:, :, :width, :].add(spill)
    return result


def solution(mesh):
    return jax.shard_map(
        shards,
        mesh=mesh,
        in_specs=(
            P("depth", None, "lat", None),
            P(),
            P("lat", None, None),
            P("lat", None),
            P("lat"),
        ),
        out_specs=P("depth", None, "lat", None),
        check_vma=False,
    )
```

profile of v0, /device:TPU:0, one launch (start us, length us, event | category | flops | bytes accessed | tf_op | source)
XLA Modules:
  0.0 461.5 jit_solution(8915416454014389791)
XLA Ops:
  0.0 8.8 %collective-permute-start = (f32[1,2,256,2048]{3,2,1,0:T(8,128)}, f32[1,2,256,2048]{3,2,1,0:T(8,128)}, u32[]{:S(2)}, u32[]{:S(2)}) collective-permute-start(f32[1,2,256,2048]{3,2,1,0:T(8,128)} %param.21), channel_id=1, source_target_pairs={{0,63},{1,0},{2,1},{3,2},{4,3},{5,4},{6,5},{7,6},{8,7},{9,8},{10,9... | collective-permute-start | bytes 12582920 | tf_op jit(solution)/shard_map/ppermute | solution.py:13
  13.9 85.0 %collective-permute-done = f32[1,2,256,2048]{3,2,1,0:T(8,128)} collective-permute-done((f32[1,2,256,2048]{3,2,1,0:T(8,128)}, f32[1,2,256,2048]{3,2,1,0:T(8,128)}, u32[]{:S(2)}, u32[]{:S(2)}) %collective-permute-start) | collective-permute-done | bytes 4194336 | tf_op jit(solution)/shard_map/ppermute | solution.py:13
  98.9 7.9 %pad_maximum_fusion.4 = f32[1,2,512,2048]{3,2,1,0:T(8,128)} fusion(f32[1,2,256,2048]{3,2,1,0:T(8,128)} %collective-permute-done, f32[1,2,256,2048]{3,2,1,0:T(8,128)} %param.21), kind=kLoop, calls=%fused_computation.310 | loop fusion | flops 2097152 | bytes 16777216 | tf_op jit(solution)/shard_map/concatenate | solution.py:114
  106.8 16.3 %while.17 = (s32[]{:T(128)}, f32[1,2,512,2048]{3,2,1,0:T(8,128)}, s32[4,4]{1,0:T(4,128)S(1)}, f32[4,1,2,256,256]{4,3,2,1,0:T(8,128)}, s32[]{:T(128)}) while((s32[]{:T(128)}, f32[1,2,512,2048]{3,2,1,0:T(8,128)}, s32[4,4]{1,0:T(4,128)S(1)}, f32[4,1,2,256,256]{4,3,2,1,0:T(8,128)}, s32[]{:T(128)}) %tuple.122), condition=%wide.while_cond.1, body=%wide.while_body.1.sunk | while | flops 2 | bytes 1049725 | solution.py:117
  107.4 3.4 bitcast_dynamic-update-slice_fusion.2
  111.4 3.4 bitcast_dynamic-update-slice_fusion.2
  115.5 3.4 bitcast_dynamic-update-slice_fusion.2
  119.6 3.4 bitcast_dynamic-update-slice_fusion.2
  123.1 37.0 %conditional.5 = (f32[2,4,256,256]{3,2,1,0:T(8,128)}, f32[1,2,4,256,256]{4,3,2,1,0:T(8,128)S(1)}) conditional(s32[]{:T(128)} %convert_element_type.215, (f32[2,4,256,256]{2,3,1,0:T(8,128)S(1)}) %tuple.83, (f32[2,4,256,256]{2,3,1,0:T(8,128)S(1)}, f32[4,1,2,256,256]{4,3,2,1,0:T(8,128)}, f32[256,256]{1,0:T(8,128)S(1)}, f32[256,256]{1,0:T(8,128)S(1)}, ...), branch_computations={%region_0.1_spmd, %region_1.2_spmd} | conditional | flops 12892504064 | bytes 78118952 | solution.py:131
  125.7 3.5 copy.85
  160.1 3.7 copy.86
  170.4 13.9 %conditional.6 = (f32[2,4,256,256]{3,2,1,0:T(8,128)}, f32[1,2,4,256,256]{3,4,2,1,0:T(8,128)S(1)}) conditional(s32[]{:T(128)} %convert_element_type.216, (f32[2,4,256,256]{2,3,1,0:T(8,128)S(1)}, f32[1,2,4,256,256]{4,3,2,1,0:T(8,128)}) %tuple.138, (f32[2,4,256,256]{2,3,1,0:T(8,128)S(1)}, f32[4,1,2,256,256]{4,3,2,1,0:T(8,128)}, ...), branch_computations={%region_2.3_spmd, %region_3.4_spmd} | conditional | flops 12892504064 | bytes 67108880 | solution.py:131
  184.3 12.0 %conditional.7 = (f32[2,4,256,256]{3,2,1,0:T(8,128)}) conditional(s32[]{:T(128)} %convert_element_type.216, () %tuple.65, (f32[2,4,256,256]{3,2,1,0:T(8,128)}, f32[256,256]{1,0:T(8,128)S(1)}, f32[256,256]{1,0:T(8,128)S(1)}, f32[256,256]{1,0:T(8,128)S(1)}, f32[256,256]{1,0:T(8,128)S(1)}, /*index=5*/f32[256,256]{1,0:T(8,128)S(1)}, ...), branch_computations={%region_4.5_spmd, %region_5.6_spmd} | conditional | flops 12890669056 | bytes 75497552 | solution.py:142
  196.4 17.7 %conditional.8 = (f32[2,4,256,256]{3,2,1,0:T(8,128)}, f32[1,2,4,256,256]{4,3,2,1,0:T(8,128)}) conditional(s32[]{:T(128)} %convert_element_type.216, f32[2,4,256,256]{3,2,1,0:T(8,128)} %get-tuple-element.675, (f32[4,1,2,256,256]{4,3,2,1,0:T(8,128)}, f32[2,4,256,256]{3,2,1,0:T(8,128)}, f32[256,256]{1,0:T(8,128)S(1)}, f32[256,256]{1,0:T(8,128)S(1)}, ...), branch_computations={%region_6.7_spmd, %region_7.8_spmd} | conditional | flops 12894732288 | bytes 109052040 | solution.py:153
  218.2 77.8 %collective-permute-done.2 = f32[2,4,256,256]{2,3,1,0:T(8,128)} collective-permute-done((f32[2,4,256,256]{2,3,1,0:T(8,128)}, f32[2,4,256,256]{2,3,1,0:T(8,128)}, u32[]{:S(2)}, u32[]{:S(2)}) %collective-permute-start.2) | collective-permute-done | bytes 2097184 | tf_op jit(solution)/shard_map/ppermute | solution.py:19
  296.1 41.0 %conditional.9 = (f32[1,2,4,256,256]{4,3,1,2,0:T(8,128)}) conditional(s32[]{:T(128)} %convert_element_type.215, f32[1,2,4,256,256]{4,3,2,1,0:T(8,128)} %get-tuple-element.386, (f32[1,2,4,256,256]{3,4,2,1,0:T(8,128)S(1)}, pred[]{:T(512)}, f32[2,4,256,256]{3,2,1,0:T(8,128)}, f32[2,4,256,256]{2,3,1,0:T(8,128)}, f32[256,256]{1,0:T(8,128)S(1)}, ...), branch_computations={%region_8.9_spmd, %region_9.10_spmd} | conditional | flops 12893159424 | bytes 85983296 | solution.py:153
  330.7 4.4 add_bitcast_fusion.2
  337.0 4.3 broadcast_in_dim.7
  341.4 48.2 %while.16 = (s32[]{:T(128)}, f32[1,2,512,2048]{3,2,1,0:T(8,128)}, s32[4,2]{0,1:T(2,128)S(1)}, f32[1,2,4,256,256]{4,3,1,2,0:T(8,128)}, s32[]{:T(128)}, /*index=5*/s32[]{:T(128)}, s32[]{:T(128)}, s32[]{:T(128)}) while((s32[]{:T(128)}, f32[1,2,512,2048]{3,2,1,0:T(8,128)}, s32[4,2]{0,1:T(2,128)S(1)}, f32[1,2,4,256,256]{4,3,1,2,0:T(8,128)}, ...), condition=%wide.region_11.12_spmd, body=%wide.region_10.11_spmd.sunk | while | flops 131080 | bytes 2621653 | solution.py:166
  347.3 5.2 %dynamic_update_slice.8 = f32[1,2,512,2048]{3,2,1,0:T(8,128)} dynamic-update-slice(f32[1,2,512,2048]{3,2,1,0:T(8,128)} %get-tuple-element.660, f32[1,2,256,256]{3,2,1,0:T(8,128)S(1)} %bitcast_add_fusion.2, s32[]{:T(128)} %constant.122.clone.1..sunk, s32[]{:T(128)} %constant.122.clone.1..sunk, s32[]{:T(128)S(6)} %select_n.234, s32[]{:T(128)S(6)} %select_n.235) | dynamic-update-slice | bytes 1048580 | tf_op jit(solution)/shard_map/while/body/eval_jaxpr/dynamic_update_slice | solution.py:164
  358.6 6.1 %dynamic_update_slice.8 = f32[1,2,512,2048]{3,2,1,0:T(8,128)} dynamic-update-slice(f32[1,2,512,2048]{3,2,1,0:T(8,128)} %get-tuple-element.660, f32[1,2,256,256]{3,2,1,0:T(8,128)S(1)} %bitcast_add_fusion.2, s32[]{:T(128)} %constant.122.clone.1..sunk, s32[]{:T(128)} %constant.122.clone.1..sunk, s32[]{:T(128)S(6)} %select_n.234, s32[]{:T(128)S(6)} %select_n.235) | dynamic-update-slice | bytes 1048580 | tf_op jit(solution)/shard_map/while/body/eval_jaxpr/dynamic_update_slice | solution.py:164
  370.8 6.8 %dynamic_update_slice.8 = f32[1,2,512,2048]{3,2,1,0:T(8,128)} dynamic-update-slice(f32[1,2,512,2048]{3,2,1,0:T(8,128)} %get-tuple-element.660, f32[1,2,256,256]{3,2,1,0:T(8,128)S(1)} %bitcast_add_fusion.2, s32[]{:T(128)} %constant.122.clone.1..sunk, s32[]{:T(128)} %constant.122.clone.1..sunk, s32[]{:T(128)S(6)} %select_n.234, s32[]{:T(128)S(6)} %select_n.235) | dynamic-update-slice | bytes 1048580 | tf_op jit(solution)/shard_map/while/body/eval_jaxpr/dynamic_update_slice | solution.py:164
  383.6 6.0 %dynamic_update_slice.8 = f32[1,2,512,2048]{3,2,1,0:T(8,128)} dynamic-update-slice(f32[1,2,512,2048]{3,2,1,0:T(8,128)} %get-tuple-element.660, f32[1,2,256,256]{3,2,1,0:T(8,128)S(1)} %bitcast_add_fusion.2, s32[]{:T(128)} %constant.122.clone.1..sunk, s32[]{:T(128)} %constant.122.clone.1..sunk, s32[]{:T(128)S(6)} %select_n.234, s32[]{:T(128)S(6)} %select_n.235) | dynamic-update-slice | bytes 1048580 | tf_op jit(solution)/shard_map/while/body/eval_jaxpr/dynamic_update_slice | solution.py:164
  392.2 66.1 %collective-permute-done.3 = f32[1,2,256,2048]{3,2,1,0:T(8,128)S(1)} collective-permute-done((f32[1,2,256,2048]{3,2,1,0:T(8,128)S(1)}, f32[1,2,256,2048]{3,2,1,0:T(8,128)S(1)}, u32[]{:S(2)}, u32[]{:S(2)}) %collective-permute-start.3) | collective-permute-done | bytes 4194336 | tf_op jit(solution)/shard_map/ppermute | solution.py:13
  (101 shorter events, 111.1 us)
Async XLA Ops:
  0.0 98.9 %collective-permute-start = (f32[1,2,256,2048]{3,2,1,0:T(8,128)}, f32[1,2,256,2048]{3,2,1,0:T(8,128)}, u32[]{:S(2)}, u32[]{:S(2)}) collective-permute-start(f32[1,2,256,2048]{3,2,1,0:T(8,128)} %param.21), channel_id=1, source_target_pairs={{0,63},{1,0},{2,1},{3,2},{4,3},{5,4},{6,5},{7,6},{8,7},{9,8},{10,9... | collective-permute-start | bytes 12582920 | tf_op jit(solution)/shard_map/ppermute | solution.py:13
  11.0 0.8 copy-start.7
  157.4 2.3 copy-start.5
  160.1 3.7 copy-start.6
  163.8 5.4 %collective-permute-start.1 = (f32[2,4,256,256]{2,3,1,0:T(8,128)}, f32[2,4,256,256]{2,3,1,0:T(8,128)}, u32[]{:S(2)}, u32[]{:S(2)}) collective-permute-start(f32[2,4,256,256]{2,3,1,0:T(8,128)} %copy.86), channel_id=1, source_target_pairs={{0,64},{1,65},{2,66},{3,67},{4,68},{5,69},{6,70},{7,71},{8,72},{9,... | collective-permute-start | bytes 6291464 | tf_op jit(solution)/shard_map/ppermute | solution.py:19
  216.9 79.1 %collective-permute-start.2 = (f32[2,4,256,256]{2,3,1,0:T(8,128)}, f32[2,4,256,256]{2,3,1,0:T(8,128)}, u32[]{:S(2)}, u32[]{:S(2)}) collective-permute-start(f32[2,4,256,256]{2,3,1,0:T(8,128)} %copy.94), channel_id=1, source_target_pairs={{64,0},{65,1},{66,2},{67,3},{68,4},{69,5},{70,6},{71,7},{72,8},{73... | collective-permute-start | bytes 6291464 | tf_op jit(solution)/shard_map/ppermute | solution.py:19
  313.3 2.1 copy-start.9
  317.2 6.7 %copy-start.4 = (f32[4,256,256]{1,2,0:T(8,128)}, f32[4,256,256]{1,2,0:T(8,128)S(1)}, u32[]{:S(2)}) copy-start(f32[4,256,256]{1,2,0:T(8,128)S(1)} %fusion.180) | copy-start | bytes 3145732 | tf_op jit(solution)/shard_map/cond
  337.0 4.4 copy-start.12
  389.5 68.8 %copy-start.1 = (f32[1,2,512,2048]{3,2,1,0:T(8,128)S(1)}, f32[1,2,512,2048]{3,2,1,0:T(8,128)}, u32[]{:S(2)}) copy-start(f32[1,2,512,2048]{3,2,1,0:T(8,128)} %get-tuple-element.388) | copy-start | bytes 25165828
  392.2 66.2 %collective-permute-start.3 = (f32[1,2,256,2048]{3,2,1,0:T(8,128)S(1)}, f32[1,2,256,2048]{3,2,1,0:T(8,128)S(1)}, u32[]{:S(2)}, u32[]{:S(2)}) collective-permute-start(f32[1,2,256,2048]{3,2,1,0:T(8,128)S(1)} %slice.147), channel_id=1, source_target_pairs={{0,1},{1,2},{2,3},{3,4},{4,5},{5,6},{6,7},{7,8},{8,9},{9,10},{10,1... | collective-permute-start | bytes 12582920 | tf_op jit(solution)/shard_map/ppermute | solution.py:13
where the time goes:
time: 467 us; the launch traced here: 461 us
  waiting for transfers between devices  231 us (49%)
  local copies, waits for them, and re-layouts  82.4 us (18%)
  matrix products  57.9 us (12%)
  loops' own time  50.1 us (11%)
  other arithmetic  26.2 us (6%)
  starting transfers between devices  12.8 us (3%)
    ppermute x2, waiting for transfers between devices, from_behind(): lax.ppermute(value, axis, [(i, (i + by) % length) for i in range(length)])  151 us
    ppermute x2, waiting for transfers between devices, from_behind_2(): lax.ppermute(value, axis, [(source, source + steps) for source in range(i...  79.9 us
    dot_general x16, matrix products, right_product(): jnp.einsum('...jk,kl->...jl', values, matrix, precision=lax.Precision.HIG...  34.5 us
    dynamic_update_slice x4, local copies, waits for them, and re-layouts, add_window(): return lax.dynamic_update_slice(total, current + piece, corner)  24.1 us
    dot_general x16, matrix products, left_product(): jnp.einsum('jk,...kl->...jl', matrix, values, precision=lax.Precision.HIG...  23.3 us
    gather x12, local copies, waits for them, and re-layouts  16.3 us
    another operation x1, loops' own time, shards(): widened = lax.fori_loop(0, slots, add_window, widened)  15.5 us
    another operation x8, local copies, waits for them, and re-layouts  15 us
  transfers between devices with their start and end apart: 4, of which 4 were waited for; matrix products, arithmetic and copies ran while one was open for 1% of the time, Pallas kernels for 0%

commit v1 on v0

v1 whole, which is shorter than its diff:
```python
import functools

import jax
import jax.numpy as jnp
import ml_dtypes
import numpy as np
from jax import lax
from jax.experimental import pallas as pl
from jax.experimental.pallas import tpu as pltpu
from jax.sharding import PartitionSpec as P

N = 256
HALF = 128
STRENGTH = 8.0
MAX_JOBS = 3
BUDGET = 48
ROWS = 8 * BUDGET
PAD = 256
SPAN = 20


def split_bf16(a):
    hi = a.astype(np.float32).astype(ml_dtypes.bfloat16)
    lo = (a - hi.astype(np.float64)).astype(np.float32).astype(ml_dtypes.bfloat16)
    return hi, lo


def left_table(a):
    hi, lo = split_bf16(a)
    return np.concatenate([hi, hi, lo], axis=1)


def right_table(a):
    hi, lo = split_bf16(a)
    return np.concatenate([hi, hi, lo], axis=0)


def tables():
    index = np.arange(N)
    angle = 2.0 * np.pi * ((index[:, None] * index[None, :]) % N) / N
    dft = np.exp(-1j * angle) / 16.0
    centred = (index - N * (index >= HALF)) / N
    turn = np.exp(1j * np.pi * STRENGTH * centred**2)
    prop = np.conj(dft) @ (turn[:, None] * dft)
    c0, c1 = prop[:HALF, :HALF], prop[:HALF, HALF:]
    plus, minus = (c0 + c1) / 2, (c0 - c1) / 2

    def real_left(m):
        return np.block([[m.real, -m.imag], [m.imag, m.real]])

    lp, lm = real_left(plus), real_left(minus)
    lefts = np.stack([left_table(lp), left_table(lm), left_table(lp.T), left_table(lm.T)])
    rights = np.stack([right_table(lp.T), right_table(lm.T), right_table(lp), right_table(lm)])
    cos, sin = np.cos(angle) / 16.0, np.sin(angle) / 16.0
    dft_left = np.concatenate([left_table(cos), left_table(sin)], axis=0)
    dft_right = np.stack([right_table(cos), right_table(sin)])
    return lefts, rights, dft_left, dft_right


def make_plan(rows_of, cols_of, live, plan, base):
    up = [lax.div(rows_of[i] + 7, 8) for i in range(4)]
    down = [40 - lax.div(rows_of[i], 8) for i in range(4)]
    best = jnp.int32(1 << 20)
    pick = jnp.int32(0)
    for mask in range(16):
        right = [(mask >> i) & 1 for i in range(4)]
        top = max([i + 1 for i in range(4) if right[i]], default=0)
        n_right = sum(right)
        lefts = [jnp.where(live > i, up[i], 0) for i in range(4) if not right[i]]
        cost_left = sum(lefts, jnp.int32(0))
        cost_right = sum([down[i] for i in range(4) if right[i]], jnp.int32(0))
        n_left = live - n_right
        widest = jnp.maximum(cost_left, cost_right)
        most = jnp.maximum(n_left, n_right)
        bad = (live < top) | (widest > BUDGET) | (most > MAX_JOBS)
        key = most * 64 + widest + jnp.where(bad, jnp.int32(1 << 16), 0)
        pick = jnp.where(key < best, mask, pick)
        best = jnp.minimum(key, best)
    for side in range(2):
        at = base + side * SPAN
        count = jnp.int32(0)
        total = jnp.int32(0)
        for j in range(MAX_JOBS):
            for f in range(5):
                plan[at + 2 + 5 * j + f] = jnp.int32(0)
        for i in range(4):
            mine = (live > i) & ((lax.shift_right_logical(pick, i) & 1) == side)
            block = jnp.minimum(lax.div(cols_of[i], N), 6)
            spot = at + 2 + 5 * count

            @pl.when(mine)
            def _(spot=spot, i=i, block=block, total=total):
                plan[spot] = rows_of[i]
                plan[spot + 1] = block
                plan[spot + 2] = cols_of[i] - block * N
                plan[spot + 3] = total
                plan[spot + 4] = jnp.int32(i)

            size = up[i] if side == 0 else down[i] - 8
            total = total + jnp.where(mine, size, 0)
            count = count + jnp.where(mine, 1, 0)
        plan[at] = count
        plan[at + 1] = total


OWN_LEFT, OWN_RIGHT, PREV_LEFT, PREV_RIGHT = 0, SPAN, 2 * SPAN, 3 * SPAN


def lanes():
    return lax.broadcasted_iota(jnp.int32, (8, N), 1)


def pack_kernel(pos, cnt, prev_pos, prev_cnt, tile, measured, plan, a_ref, b_ref):
    depth = lax.axis_index("depth")
    make_plan([pos[i, 0] for i in range(4)], [pos[i, 1] for i in range(4)], cnt[0], plan, 0)
    make_plan(
        [prev_pos[i, 0] for i in range(4)],
        [prev_pos[i, 1] for i in range(4)],
        prev_cnt[0],
        plan,
        2 * SPAN,
    )

    def copy_rows(out, at, j, first, count):
        block = plan[at + 2 + 5 * j + 1]
        shift = plan[at + 2 + 5 * j + 2]
        start = plan[at + 2 + 5 * j + 3]
        low = pl.multiple_of(block * N, N)
        high = pl.multiple_of(block * N + N, N)
        keep = lanes() >= shift

        def step(g, carry):
            src = pl.multiple_of((first + g) * 8, 8)
            dst = pl.multiple_of((start + g) * 8, 8)
            for c in range(2):
                out[c, pl.ds(dst, 8), :] = jnp.where(
                    keep, tile[c, pl.ds(src, 8), pl.ds(low, N)], tile[c, pl.ds(src, 8), pl.ds(high, N)]
                )
            return carry

        lax.fori_loop(0, count, step, 0)

    def right_job(j, carry):
        first = lax.div(plan[OWN_RIGHT + 2 + 5 * j], 8)
        copy_rows(a_ref, OWN_RIGHT, j, first, 32 - first)
        slot = plan[OWN_RIGHT + 2 + 5 * j + 4]
        dst = pl.multiple_of((plan[OWN_RIGHT + 1] + 8 * j) * 8, 8)
        for c in range(2):
            src = pl.multiple_of(depth * HALF + 64 * c, 64)
            a_ref[c, pl.ds(dst, 64), :] = measured[slot, pl.ds(src, 64), :]
        return carry

    lax.fori_loop(0, plan[OWN_RIGHT], right_job, 0)

    def left_job(j, carry):
        count = lax.div(plan[PREV_LEFT + 2 + 5 * j] + 7, 8)
        copy_rows(b_ref, PREV_LEFT, j, 0, count)
        return carry

    lax.fori_loop(0, plan[PREV_LEFT], left_job, 0)


def halves(x):
    hi = x.astype(jnp.bfloat16)
    lo = (x - hi.astype(jnp.float32)).astype(jnp.bfloat16)
    return hi, lo


def dot(a, b):
    return jnp.dot(a, b, preferred_element_type=jnp.float32)


def wide(x):
    hi, lo = halves(x)
    return jnp.concatenate([hi, lo, hi], axis=1)


def tall(x):
    hi, lo = halves(x)
    return jnp.concatenate([hi, lo, hi], axis=0)


def propagate(re, im, lefts, rights, at):
    plus = jnp.concatenate([re[:, :HALF] + re[:, HALF:], im[:, :HALF] + im[:, HALF:]], axis=1)
    minus = jnp.concatenate([re[:, :HALF] - re[:, HALF:], im[:, :HALF] - im[:, HALF:]], axis=1)
    plus = dot(wide(plus), rights[at])
    minus = dot(wide(minus), rights[at + 1])
    first, second = plus + minus, plus - minus
    re = jnp.concatenate([first[:, :HALF], second[:, :HALF]], axis=1)
    im = jnp.concatenate([first[:, HALF:], second[:, HALF:]], axis=1)
    plus = jnp.concatenate([re[:HALF] + re[HALF:], im[:HALF] + im[HALF:]], axis=0)
    minus = jnp.concatenate([re[:HALF] - re[HALF:], im[:HALF] - im[HALF:]], axis=0)
    plus = dot(lefts[at], tall(plus))
    minus = dot(lefts[at + 1], tall(minus))
    first, second = plus + minus, plus - minus
    return (
        jnp.concatenate([first[:HALF], second[:HALF]], axis=0),
        jnp.concatenate([first[HALF:], second[HALF:]], axis=0),
    )


def transform(re, im, dft_left, dft_right, sign):
    both = wide(jnp.concatenate([re, im], axis=0))
    c = dot(both, dft_right[0])
    s = dot(both, dft_right[1]) * sign
    re, im = c[:N] - s[N:], c[N:] + s[:N]
    both = tall(jnp.concatenate([re, im], axis=1))
    c = dot(dft_left[:N], both)
    s = dot(dft_left[N:], both) * sign
    return c[:, :N] - s[:, N:], c[:, N:] + s[:, :N]


def compute_kernel(
    plan, tile, other, x_other, x_same, measured, probe, lefts, rights, dft_left, dft_right,
    g_other, g_same, mine, theirs,
    strips, received, amplitude, grads, sems,
):
    depth = lax.axis_index("depth")
    at = jnp.where(depth == 0, OWN_LEFT, PREV_RIGHT)
    copies = [
        pltpu.make_async_copy(x_same, received.at[depth, :, pl.ds(PAD, ROWS), :], sems.at[0]),
        pltpu.make_async_copy(x_other, received.at[1 - depth, :, pl.ds(PAD, ROWS), :], sems.at[1]),
    ]
    for copy in copies:
        copy.start()
    for copy in copies:
        copy.wait()
    row = lax.broadcasted_iota(jnp.int32, (N, N), 0)
    lane = lax.broadcasted_iota(jnp.int32, (N, N), 1)

    def job(j, carry):
        r = plan[at + 2 + 5 * j]
        block = plan[at + 2 + 5 * j + 1]
        shift = plan[at + 2 + 5 * j + 2]
        start = plan[at + 2 + 5 * j + 3]
        slot = plan[at + 2 + 5 * j + 4]
        column = pl.multiple_of(block * N, N)
        fetch = [
            pltpu.make_async_copy(
                tile.at[:, :, pl.ds(column, 2 * N)], strips.at[depth], sems.at[2]
            ),
            pltpu.make_async_copy(
                other.at[:, :, pl.ds(column, 2 * N)], strips.at[1 - depth], sems.at[3]
            ),
            pltpu.make_async_copy(measured.at[slot], amplitude, sems.at[4]),
        ]
        for copy in fetch:
            copy.start()
        for copy in fetch:
            copy.wait()

        @pl.when(depth == 1)
        def _():
            src = pl.multiple_of(PAD + (plan[PREV_RIGHT + 1] + 8 * j) * 8, 8)
            for s in range(2):
                for c in range(2):
                    amplitude[pl.ds(128 * s + 64 * c, 64), :] = received[s, c, pl.ds(src, 64), :]

        low = jnp.where(depth == 0, r, 0)
        high = jnp.where(depth == 0, N, r)
        here = (row >= low) & (row < high)
        keep = lane >= shift
        base = jnp.where(depth == 0, 0, lax.div(r, 8))
        src = pl.multiple_of(PAD + (start - base) * 8, 8)

        def window(s):
            return [
                jnp.where(
                    here,
                    jnp.where(keep, strips[s, c, :, :N], strips[s, c, :, N:]),
                    received[s, c, pl.ds(src, N), :],
                )
                for c in range(2)
            ]

        def rolled(c):
            turned = pltpu.roll(probe[c], r, 0)
            return pltpu.roll(turned, jnp.where(shift == N, 0, shift), 1)

        p_re, p_im = rolled(0), rolled(1)
        o_re, o_im = window(0)
        w_re, w_im = propagate(
            p_re * o_re - p_im * o_im, p_re * o_im + p_im * o_re, lefts, rights, 0
        )
        o_re, o_im = window(1)
        f_re, f_im = transform(
            w_re * o_re - w_im * o_im, w_re * o_im + w_im * o_re, dft_left, dft_right, -1.0
        )
        factor = 1.0 - amplitude[...] / jnp.sqrt(f_re * f_re + f_im * f_im + 1.0)
        a_re, a_im = transform(f_re * factor, f_im * factor, dft_left, dft_right, 1.0)
        grads[1, 0] = w_re * a_re + w_im * a_im
        grads[1, 1] = w_re * a_im - w_im * a_re
        a_re, a_im = propagate(
            o_re * a_re + o_im * a_im, o_re * a_im - o_im * a_re, lefts, rights, 2
        )
        grads[0, 0] = p_re * a_re + p_im * a_im
        grads[0, 1] = p_re * a_im - p_im * a_re
        mine[j] = grads[depth]
        theirs[j] = grads[1 - depth]
        count = jnp.where(depth == 0, lax.div(r + 7, 8), 32 - lax.div(r, 8))

        def step(g, carry):
            src = pl.multiple_of((base + g) * 8, 8)
            dst = pl.multiple_of((start + g) * 8, 8)
            for c in range(2):
                g_same[c, pl.ds(dst, 8), :] = grads[depth, c, pl.ds(src, 8), :]
                g_other[c, pl.ds(dst, 8), :] = grads[1 - depth, c, pl.ds(src, 8), :]
            return carry

        lax.fori_loop(0, count, step, 0)
        return carry

    lax.fori_loop(0, plan[at], job, 0)


def gather_kernel(plan, g_other, g_same, mine, theirs, out):
    depth = lax.axis_index("depth")

    def clear(i, carry):
        at = pl.multiple_of(i * 8, 8)
        for c in range(2):
            out[c, pl.ds(at, 8), :] = jnp.zeros((8, out.shape[2]), jnp.float32)
        return carry

    lax.fori_loop(0, N // 8, clear, 0)
    row = lax.broadcasted_iota(jnp.int32, (8, N), 0)

    def add(source, at, j, lower, packed):
        r = plan[at + 2 + 5 * j]
        block = plan[at + 2 + 5 * j + 1]
        shift = plan[at + 2 + 5 * j + 2]
        start = plan[at + 2 + 5 * j + 3]
        first = 0 if lower else lax.div(r, 8)
        last = lax.div(r + 7, 8) if lower else 32
        keep = lanes() >= shift
        low = pl.multiple_of(block * N, N)
        high = pl.multiple_of(block * N + N, N)

        def step(g, carry):
            dst = pl.multiple_of(g * 8, 8)
            inside = (row + dst < r) if lower else (row + dst >= r)
            for c in range(2):
                if packed:
                    src = pl.multiple_of((start + g - first) * 8, 8)
                    value = source[c, pl.ds(src, 8), :]
                else:
                    value = source[j, c, pl.ds(dst, 8), :]
                out[c, pl.ds(dst, 8), pl.ds(low, N)] += jnp.where(inside & keep, value, 0.0)
                out[c, pl.ds(dst, 8), pl.ds(high, N)] += jnp.where(
                    inside & jnp.logical_not(keep), value, 0.0
                )
            return carry

        lax.fori_loop(first, last, step, 0)

    def run(source, at, lower, packed):
        def step(j, carry):
            add(source, at, j, lower, packed)
            return carry

        lax.fori_loop(0, plan[at], step, 0)

    @pl.when(depth == 0)
    def _():
        run(mine, OWN_LEFT, False, False)
        run(theirs, PREV_RIGHT, True, False)
        run(g_other, OWN_RIGHT, False, True)
        run(g_same, PREV_LEFT, True, True)

    @pl.when(depth == 1)
    def _():
        run(theirs, OWN_LEFT, False, False)
        run(mine, PREV_RIGHT, True, False)
        run(g_same, OWN_RIGHT, False, True)
        run(g_other, PREV_LEFT, True, True)


SMEM = pl.BlockSpec(memory_space=pltpu.SMEM)
VMEM = pl.BlockSpec(memory_space=pltpu.VMEM)
ANY = pl.BlockSpec(memory_space=pl.ANY)


def shape(*dims):
    return jax.ShapeDtypeStruct(dims, jnp.float32)


def shards(n_lat, object_slices, probe, measured, positions, counts):
    columns = object_slices.shape[3]
    tile = object_slices.reshape(object_slices.shape[1:])
    ahead = [(i, (i + 1) % n_lat) for i in range(n_lat)]
    prev_positions = lax.ppermute(positions, "lat", ahead)
    prev_counts = lax.ppermute(counts, "lat", ahead)

    def device(core, lat):
        return core * n_lat + lat % n_lat

    to_other = [(device(0, t), device(1, t + 1)) for t in range(n_lat)]
    to_other += [(device(1, t), device(0, t - 1)) for t in range(n_lat)]
    to_same = [(device(0, t), device(0, t - 1)) for t in range(n_lat)]
    to_same += [(device(1, t), device(1, t + 1)) for t in range(n_lat)]
    back_other = [(device(0, t), device(1, t + 1)) for t in range(n_lat)]
    back_other += [(device(1, t), device(0, t - 1)) for t in range(n_lat)]
    back_same = [(device(0, t), device(0, t + 1)) for t in range(n_lat)]
    back_same += [(device(1, t), device(1, t - 1)) for t in range(n_lat)]
    axes = ("depth", "lat")

    other = lax.ppermute(tile, "depth", [(0, 1), (1, 0)])
    plan, ahead_rows, behind_rows = pl.pallas_call(
        pack_kernel,
        name="pack",
        out_shape=(
            jax.ShapeDtypeStruct((4 * SPAN,), jnp.int32),
            shape(2, ROWS, N),
            shape(2, ROWS, N),
        ),
        in_specs=[SMEM, SMEM, SMEM, SMEM, VMEM, VMEM],
        out_specs=(SMEM, VMEM, VMEM),
        compiler_params=pltpu.CompilerParams(vmem_limit_bytes=40 << 20),
    )(positions, counts, prev_positions, prev_counts, tile, measured)

    core = lax.axis_index("depth")
    send_other = jnp.where(core == 0, ahead_rows, behind_rows)
    send_same = jnp.where(core == 0, behind_rows, ahead_rows)
    x_other = lax.ppermute(send_other, axes, to_other)
    x_same = lax.ppermute(send_same, axes, to_same)

    lefts, rights, dft_left, dft_right = (jnp.asarray(t) for t in tables())
    g_other, g_same, mine, theirs = pl.pallas_call(
        compute_kernel,
        name="compute",
        out_shape=(
            shape(2, ROWS, N),
            shape(2, ROWS, N),
            shape(MAX_JOBS, 2, N, N),
            shape(MAX_JOBS, 2, N, N),
        ),
        in_specs=[SMEM, ANY, ANY, ANY, ANY, ANY, VMEM, VMEM, VMEM, VMEM, VMEM],
        out_specs=(VMEM, VMEM, VMEM, VMEM),
        scratch_shapes=[
            pltpu.VMEM((2, 2, N, 2 * N), jnp.float32),
            pltpu.VMEM((2, 2, ROWS + 2 * PAD, N), jnp.float32),
            pltpu.VMEM((N, N), jnp.float32),
            pltpu.VMEM((2, 2, N, N), jnp.float32),
            pltpu.SemaphoreType.DMA((5,)),
        ],
        compiler_params=pltpu.CompilerParams(vmem_limit_bytes=50 << 20),
    )(plan, tile, other, x_other, x_same, measured, probe, lefts, rights, dft_left, dft_right)

    r_other = lax.ppermute(g_other, axes, back_other)
    r_same = lax.ppermute(g_same, axes, back_same)
    theirs = lax.ppermute(theirs, "depth", [(0, 1), (1, 0)])
    out = pl.pallas_call(
        gather_kernel,
        name="gather",
        out_shape=shape(2, N, columns),
        in_specs=[SMEM, VMEM, VMEM, VMEM, VMEM],
        out_specs=VMEM,
        compiler_params=pltpu.CompilerParams(vmem_limit_bytes=40 << 20),
    )(plan, r_other, r_same, mine, theirs)
    return out.reshape(object_slices.shape)


def solution(mesh):
    return jax.shard_map(
        functools.partial(shards, mesh.shape["lat"]),
        mesh=mesh,
        in_specs=(
            P("depth", None, "lat", None),
            P(),
            P("lat", None, None),
            P("lat", None),
            P("lat"),
        ),
        out_specs=P("depth", None, "lat", None),
        check_vma=False,
    )
```

time: 467 us -> 93.6 us (0.20)
  the two profiles are of different devices: /device:TPU:0 before, /device:TPU:1 now
where the time goes in v1:
time: 93.6 us; the launch traced here: 93.3 us
  waiting for transfers between devices  44.1 us (47%)
  starting transfers between devices  25.5 us (27%)
  Pallas kernels  17.3 us (18%)
  local copies, waits for them, and re-layouts  5.59 us (6%)
    ppermute x1, waiting for transfers between devices, shards(): x_same = lax.ppermute(send_same, axes, to_same)  19.9 us
    ppermute x1, starting transfers between devices, shards(): r_other = lax.ppermute(g_other, axes, back_other)  17.2 us
    pallas_call x1, Pallas kernels, shards(): pl.pallas_call(compute_kernel, name='compute', out_shape=(shape(2, ROWS,...  11 us
    ppermute x1, waiting for transfers between devices, shards(): r_other = lax.ppermute(g_other, axes, back_other)  9.63 us
    ppermute x1, waiting for transfers between devices, shards(): r_same = lax.ppermute(g_same, axes, back_same)  7.69 us
    unnamed x9, local copies, waits for them, and re-layouts  5.59 us
    ppermute x1, waiting for transfers between devices, shards(): prev_counts = lax.ppermute(counts, 'lat', ahead)  5.58 us
    ppermute x1, starting transfers between devices, shards(): x_other = lax.ppermute(send_other, axes, to_other)  4.21 us
  transfers between devices with their start and end apart: 8, of which 6 were waited for; matrix products, arithmetic and copies ran while one was open for 1% of the time, Pallas kernels for 3%

profile of v1, /device:TPU:1, one launch (start us, length us, event | category | flops | bytes accessed | tf_op | source)
XLA Modules:
  0.0 93.3 jit_solution(467023632273574176)
XLA Ops:
  0.0 1.4 %collective-permute-start.2 = (f32[2,256,2048]{2,1,0:T(8,128)}, f32[2,256,2048]{2,1,0:T(8,128)}, u32[]{:S(2)}, u32[]{:S(2)}) collective-permute-start(f32[2,256,2048]{2,1,0:T(8,128)} %bitcast.2), channel_id=1, source_target_pairs={{0,64},{64,0},{1,65},{65,1},{2,66},{66,2},{3,67},{67,3},{4,68},{68... | collective-permute-start | bytes 12582920 | tf_op jit(solution)/shard_map/ppermute | solution.py:407
  1.4 1.3 %collective-permute-start.1 = (s32[1]{0:T(128)}, s32[1]{0:T(128)}, u32[]{:S(2)}, u32[]{:S(2)}) collective-permute-start(s32[1]{0:T(128)} %param.13), channel_id=1, source_target_pairs={{0,1},{1,2},{2,3},{3,4},{4,5},{5,6},{6,7},{7,8},{8,9},{9,10},{10,1... | collective-permute-start | bytes 20 | tf_op jit(solution)/shard_map/ppermute | solution.py:392
  2.7 0.8 copy.11.pos
  3.5 1.2 %collective-permute-start = (s32[4,2]{1,0:T(4,128)S(1)}, s32[4,2]{1,0:T(4,128)S(1)}, u32[]{:S(2)}, u32[]{:S(2)}) collective-permute-start(s32[4,2]{1,0:T(4,128)S(1)} %copy.11.pos), channel_id=1, source_target_pairs={{0,1},{1,2},{2,3},{3,4},{4,5},{5,6},{6,7},{7,8},{8,9},{9,10},{10,1... | collective-permute-start | bytes 104 | tf_op jit(solution)/shard_map/ppermute | solution.py:391
  5.3 5.6 %collective-permute-done.1.prev_cnt = s32[1]{0:T(128)} collective-permute-done((s32[1]{0:T(128)}, s32[1]{0:T(128)}, u32[]{:S(2)}, u32[]{:S(2)}) %collective-permute-start.1) | collective-permute-done | bytes 36 | tf_op jit(solution)/shard_map/ppermute | solution.py:392
  10.9 0.7 collective-permute-done.prev_pos
  11.7 2.2 %copy-done = f32[1,2,256,2048]{3,2,1,0:T(8,128)S(1)} copy-done((f32[1,2,256,2048]{3,2,1,0:T(8,128)S(1)}, f32[1,2,256,2048]{3,2,1,0:T(8,128)}, u32[]{:S(2)}) %copy-start) | copy-done | bytes 4194328
  13.8 1.2 %copy-done.1 = f32[4,256,256]{2,1,0:T(8,128)S(1)} copy-done((f32[4,256,256]{2,1,0:T(8,128)S(1)}, f32[4,256,256]{2,1,0:T(8,128)}, u32[]{:S(2)}) %copy-start.1) | copy-done | bytes 1048600
  15.1 2.5 %pack.1 = (s32[80]{0:T(128)S(1)}, f32[2,384,256]{2,1,0:T(8,128)S(1)}, f32[2,384,256]{2,1,0:T(8,128)S(1)}) custom-call(s32[4,2]{1,0:T(4,128)S(1)} %copy.11.pos, s32[1]{0:T(128)S(6)} %copy.12.cnt, s32[4,2]{1,0:T(4,128)S(1)} %collective-permute-done.prev_pos, s32[1]{0:T(128)} %collective-permute-done.1.prev_cnt, f32[2,256,2048]{2,1,0:T(8,128)S(1)} %bitcast.4, ...), custom_call_target="tpu_custom_call" | custom-call | tf_op jit(solution)/shard_map/pack/pallas_call | solution.py:408
  17.5 0.0 copy-start.3
  17.6 0.1 broadcast_select_fusion
  17.7 0.1 collective-permute-start.4
  17.8 4.2 %collective-permute-start.3 = (f32[2,384,256]{2,1,0:T(8,128)S(1)}, f32[2,384,256]{2,1,0:T(8,128)S(1)}, u32[]{:S(2)}, u32[]{:S(2)}) collective-permute-start(f32[2,384,256]{2,1,0:T(8,128)S(1)} %get-tuple-element.20), channel_id=1, source_target_pairs={{0,65},{1,66},{2,67},{3,68},{4,69},{5,70},{6,71},{7,72},{8,73},{9,... | collective-permute-start | bytes 2359304 | tf_op jit(solution)/shard_map/ppermute | solution.py:424
  22.0 19.9 %collective-permute-done.4.x_same = f32[2,384,256]{2,1,0:T(8,128)S(1)} collective-permute-done((f32[2,384,256]{2,1,0:T(8,128)S(1)}, f32[2,384,256]{2,1,0:T(8,128)S(1)}, u32[]{:S(2)}, u32[]{:S(2)}) %collective-permute-start.4) | collective-permute-done | bytes 786464 | tf_op jit(solution)/shard_map/ppermute | solution.py:425
  41.8 0.6 collective-permute-done.3.x_other
  42.4 0.0 collective-permute-done.2.other
  42.5 11.0 %compute.1 = (f32[2,384,256]{2,1,0:T(8,128)S(1)}, f32[2,384,256]{2,1,0:T(8,128)S(1)}, f32[3,2,256,256]{3,2,1,0:T(8,128)}, f32[3,2,256,256]{3,2,1,0:T(8,128)}) custom-call(s32[80]{0:T(128)S(1)} %get-tuple-element.12.plan, f32[2,256,2048]{2,1,0:T(8,128)} %bitcast.3, f32[2,256,2048]{2,1,0:T(8,128)} %collective-permute-done.2.other, ...), custom_call_target="tpu_custom_call" | custom-call | tf_op jit(solution)/shard_map/compute/pallas_call | solution.py:428
  53.5 0.1 collective-permute-start.7
  53.6 17.2 %collective-permute-start.5 = (f32[2,384,256]{2,1,0:T(8,128)S(1)}, f32[2,384,256]{2,1,0:T(8,128)S(1)}, u32[]{:S(2)}, u32[]{:S(2)}) collective-permute-start(f32[2,384,256]{2,1,0:T(8,128)S(1)} %get-tuple-element.15), channel_id=1, source_target_pairs={{0,65},{1,66},{2,67},{3,68},{4,69},{5,70},{6,71},{7,72},{8,73},{9,... | collective-permute-start | bytes 2359304 | tf_op jit(solution)/shard_map/ppermute | solution.py:449
  70.7 0.0 collective-permute-start.6
  70.8 9.6 %collective-permute-done.5.g_other = f32[2,384,256]{2,1,0:T(8,128)S(1)} collective-permute-done((f32[2,384,256]{2,1,0:T(8,128)S(1)}, f32[2,384,256]{2,1,0:T(8,128)S(1)}, u32[]{:S(2)}, u32[]{:S(2)}) %collective-permute-start.5) | collective-permute-done | bytes 786464 | tf_op jit(solution)/shard_map/ppermute | solution.py:449
  80.4 7.7 %collective-permute-done.6.g_same = f32[2,384,256]{2,1,0:T(8,128)S(1)} collective-permute-done((f32[2,384,256]{2,1,0:T(8,128)S(1)}, f32[2,384,256]{2,1,0:T(8,128)S(1)}, u32[]{:S(2)}, u32[]{:S(2)}) %collective-permute-start.6) | collective-permute-done | bytes 786464 | tf_op jit(solution)/shard_map/ppermute | solution.py:450
  88.1 1.4 %copy-done.2 = f32[3,2,256,256]{3,2,1,0:T(8,128)S(1)} copy-done((f32[3,2,256,256]{3,2,1,0:T(8,128)S(1)}, f32[3,2,256,256]{3,2,1,0:T(8,128)}, u32[]{:S(2)}) %copy-start.2) | copy-done | bytes 1572888
  89.5 3.8 %gather.1 = f32[2,256,2048]{2,1,0:T(8,128)} custom-call(s32[80]{0:T(128)S(1)} %get-tuple-element.12.plan, f32[2,384,256]{2,1,0:T(8,128)S(1)} %collective-permute-done.5.g_other, f32[2,384,256]{2,1,0:T(8,128)S(1)} %collective-permute-done.6.g_same, f32[3,2,256,256]{3,2,1,0:T(8,128)S(1)} %copy-done.2, f32[3,2,256,256]{3,2,1,0:T(8,128)S(1)} %collective-permute-done.7.theirs), custom_call_target="tpu_custom_call" | custom-call | tf_op jit(solution)/shard_map/gather/pallas_call | solution.py:452
  (5 shorter events, 0.0 us)
Async XLA Ops:
  0.0 42.5 %collective-permute-start.2 = (f32[2,256,2048]{2,1,0:T(8,128)}, f32[2,256,2048]{2,1,0:T(8,128)}, u32[]{:S(2)}, u32[]{:S(2)}) collective-permute-start(f32[2,256,2048]{2,1,0:T(8,128)} %bitcast.2), channel_id=1, source_target_pairs={{0,64},{64,0},{1,65},{65,1},{2,66},{66,2},{3,67},{67,3},{4,68},{68... | collective-permute-start | bytes 12582920 | tf_op jit(solution)/shard_map/ppermute | solution.py:407
  1.4 9.5 %collective-permute-start.1 = (s32[1]{0:T(128)}, s32[1]{0:T(128)}, u32[]{:S(2)}, u32[]{:S(2)}) collective-permute-start(s32[1]{0:T(128)} %param.13), channel_id=1, source_target_pairs={{0,1},{1,2},{2,3},{3,4},{4,5},{5,6},{6,7},{7,8},{8,9},{9,10},{10,1... | collective-permute-start | bytes 20 | tf_op jit(solution)/shard_map/ppermute | solution.py:392
  3.5 8.2 %collective-permute-start = (s32[4,2]{1,0:T(4,128)S(1)}, s32[4,2]{1,0:T(4,128)S(1)}, u32[]{:S(2)}, u32[]{:S(2)}) collective-permute-start(s32[4,2]{1,0:T(4,128)S(1)} %copy.11.pos), channel_id=1, source_target_pairs={{0,1},{1,2},{2,3},{3,4},{4,5},{5,6},{6,7},{7,8},{8,9},{9,10},{10,1... | collective-permute-start | bytes 104 | tf_op jit(solution)/shard_map/ppermute | solution.py:391
  11.7 2.2 %copy-start = (f32[1,2,256,2048]{3,2,1,0:T(8,128)S(1)}, f32[1,2,256,2048]{3,2,1,0:T(8,128)}, u32[]{:S(2)}) copy-start(f32[1,2,256,2048]{3,2,1,0:T(8,128)} %param.9) | copy-start | bytes 12582916
  13.8 1.2 %copy-start.1 = (f32[4,256,256]{2,1,0:T(8,128)S(1)}, f32[4,256,256]{2,1,0:T(8,128)}, u32[]{:S(2)}) copy-start(f32[4,256,256]{2,1,0:T(8,128)} %measured.3) | copy-start | bytes 3145732
  17.5 24.9 %copy-start.3 = (f32[2,256,256]{2,1,0:T(8,128)S(1)}, f32[2,256,256]{2,1,0:T(8,128)}, u32[]{:S(2)}) copy-start(f32[2,256,256]{2,1,0:T(8,128)} %probe.1) | copy-start | bytes 1572868
  17.7 24.1 %collective-permute-start.4 = (f32[2,384,256]{2,1,0:T(8,128)S(1)}, f32[2,384,256]{2,1,0:T(8,128)S(1)}, u32[]{:S(2)}, u32[]{:S(2)}) collective-permute-start(f32[2,384,256]{2,1,0:T(8,128)S(1)} %get-tuple-element.19), channel_id=1, source_target_pairs={{0,63},{1,0},{2,1},{3,2},{4,3},{5,4},{6,5},{7,6},{8,7},{9,8},{10,9... | collective-permute-start | bytes 2359304 | tf_op jit(solution)/shard_map/ppermute | solution.py:425
  17.8 24.7 %collective-permute-start.3 = (f32[2,384,256]{2,1,0:T(8,128)S(1)}, f32[2,384,256]{2,1,0:T(8,128)S(1)}, u32[]{:S(2)}, u32[]{:S(2)}) collective-permute-start(f32[2,384,256]{2,1,0:T(8,128)S(1)} %get-tuple-element.20), channel_id=1, source_target_pairs={{0,65},{1,66},{2,67},{3,68},{4,69},{5,70},{6,71},{7,72},{8,73},{9,... | collective-permute-start | bytes 2359304 | tf_op jit(solution)/shard_map/ppermute | solution.py:424
  53.5 34.6 %collective-permute-start.7 = (f32[3,2,256,256]{3,2,1,0:T(8,128)}, f32[3,2,256,256]{3,2,1,0:T(8,128)S(1)}, u32[]{:S(2)}, u32[]{:S(2)}) collective-permute-start(f32[3,2,256,256]{3,2,1,0:T(8,128)} %get-tuple-element.18), channel_id=1, source_target_pairs={{0,64},{64,0},{1,65},{65,1},{2,66},{66,2},{3,67},{67,3},{4,68},{68... | collective-permute-start | bytes 4718600 | tf_op jit(solution)/shard_map/ppermute | solution.py:451
  53.6 26.8 %collective-permute-start.5 = (f32[2,384,256]{2,1,0:T(8,128)S(1)}, f32[2,384,256]{2,1,0:T(8,128)S(1)}, u32[]{:S(2)}, u32[]{:S(2)}) collective-permute-start(f32[2,384,256]{2,1,0:T(8,128)S(1)} %get-tuple-element.15), channel_id=1, source_target_pairs={{0,65},{1,66},{2,67},{3,68},{4,69},{5,70},{6,71},{7,72},{8,73},{9,... | collective-permute-start | bytes 2359304 | tf_op jit(solution)/shard_map/ppermute | solution.py:449
  70.7 17.4 %collective-permute-start.6 = (f32[2,384,256]{2,1,0:T(8,128)S(1)}, f32[2,384,256]{2,1,0:T(8,128)S(1)}, u32[]{:S(2)}, u32[]{:S(2)}) collective-permute-start(f32[2,384,256]{2,1,0:T(8,128)S(1)} %get-tuple-element.16), channel_id=1, source_target_pairs={{0,1},{1,2},{2,3},{3,4},{4,5},{5,6},{6,7},{7,8},{8,9},{9,10},{10,1... | collective-permute-start | bytes 2359304 | tf_op jit(solution)/shard_map/ppermute | solution.py:450
  88.1 1.4 %copy-start.2 = (f32[3,2,256,256]{3,2,1,0:T(8,128)S(1)}, f32[3,2,256,256]{3,2,1,0:T(8,128)}, u32[]{:S(2)}) copy-start(f32[3,2,256,256]{3,2,1,0:T(8,128)} %get-tuple-element.17.mine) | copy-start | bytes 4718596

commit v2 on v1

v2 whole, which is shorter than its diff:
```python
import functools

import jax
import jax.numpy as jnp
import ml_dtypes
import numpy as np
from jax import lax
from jax.experimental import pallas as pl
from jax.experimental.pallas import tpu as pltpu
from jax.sharding import PartitionSpec as P

N = 256
HALF = 128
STRENGTH = 8.0
MAX_JOBS = 3
BUDGET = 48
ROWS = 8 * BUDGET
PAD = 256
SPAN = 20


def split_bf16(a):
    hi = a.astype(np.float32).astype(ml_dtypes.bfloat16)
    lo = (a - hi.astype(np.float64)).astype(np.float32).astype(ml_dtypes.bfloat16)
    return hi, lo


def tables():
    index = np.arange(N)
    angle = 2.0 * np.pi * ((index[:, None] * index[None, :]) % N) / N
    dft = np.exp(-1j * angle) / 16.0
    centred = (index - N * (index >= HALF)) / N
    turn = np.exp(1j * np.pi * STRENGTH * centred**2)
    prop = np.conj(dft) @ (turn[:, None] * dft)
    c0, c1 = prop[:HALF, :HALF], prop[:HALF, HALF:]

    def real_form(m):
        return np.block([[m.real, -m.imag], [m.imag, m.real]])

    forms = [real_form(m) for m in ((c0 + c1) / 2, (c0 - c1) / 2, dft[0::2, :HALF], dft[1::2, :HALF])]
    forms = forms + [m.T for m in forms]
    return np.stack([np.stack(split_bf16(m)) for m in forms])


OWN_LEFT, OWN_RIGHT, PREV_LEFT, PREV_RIGHT = 0, SPAN, 2 * SPAN, 3 * SPAN


def choose_sides(rows_of, cols_of, live):
    up = [lax.div(rows_of[i] + 7, 8) for i in range(4)]
    down = [32 - lax.div(rows_of[i], 8) for i in range(4)]
    best = jnp.int32(1 << 20)
    pick = jnp.int32(0)
    for mask in range(16):
        right = [(mask >> i) & 1 for i in range(4)]
        n_right = sum(right)
        if n_right > MAX_JOBS:
            continue
        top = max([i + 1 for i in range(4) if right[i]], default=0)
        lefts = [jnp.where(live > i, up[i], 0) for i in range(4) if not right[i]]
        cost_left = sum(lefts, jnp.int32(0))
        cost_right = sum([down[i] + 8 for i in range(4) if right[i]], jnp.int32(0))
        widest = jnp.maximum(cost_left, cost_right)
        most = jnp.maximum(live - n_right, n_right)
        bad = (live < top) | (widest > BUDGET) | (most > MAX_JOBS)
        key = most * 64 + widest + jnp.where(bad, jnp.int32(1 << 16), 0)
        pick = jnp.where(key < best, mask, pick)
        best = jnp.minimum(key, best)
    blocks = [jnp.minimum(lax.div(cols_of[i], N), 6) for i in range(4)]
    sides = []
    for side in range(2):
        mine = [(live > i) & ((lax.shift_right_logical(pick, i) & 1) == side) for i in range(4)]
        size = up if side == 0 else down
        count, total = jnp.int32(0), jnp.int32(0)
        words = [[jnp.int32(0)] * 5 for _ in range(MAX_JOBS)]
        for i in range(4):
            fields = [rows_of[i], blocks[i], cols_of[i] - blocks[i] * N, total, jnp.int32(i)]
            for j in range(MAX_JOBS):
                here = mine[i] & (count == j)
                words[j] = [jnp.where(here, f, w) for f, w in zip(fields, words[j])]
            count = count + jnp.where(mine[i], 1, 0)
            total = total + jnp.where(mine[i], size[i], 0)
        sides.append([count, total] + [w for job in words for w in job])
    return sides


def lanes():
    return lax.broadcasted_iota(jnp.int32, (8, N), 1)


def announce_kernel(n_lat, pos, cnt, prev_pos, prev_cnt, send, recv):
    depth = lax.axis_index("depth")
    lat = lax.axis_index("lat")
    after = lax.rem(lat + 1, n_lat)
    before = lax.rem(lat + n_lat - 1, n_lat)
    barrier = pltpu.get_barrier_semaphore()
    for other in (after, before):
        pl.semaphore_signal(
            barrier, inc=1, device_id=(depth, other), device_id_type=pl.DeviceIdType.MESH
        )
    pl.semaphore_wait(barrier, 2)
    copies = [
        remote(pos, prev_pos, send.at[0], recv.at[0], depth, after),
        remote(cnt, prev_cnt, send.at[1], recv.at[1], depth, after),
    ]
    for copy in copies:
        copy.start()
    for copy in copies:
        copy.wait()


def pack_kernel(
    pos, cnt, prev_pos, prev_cnt, tile_hbm, measured_hbm, plan, ahead, behind,
    tile, measured, sems,
):
    depth = lax.axis_index("depth")
    loads = [
        pltpu.make_async_copy(tile_hbm, tile, sems.at[0]),
        pltpu.make_async_copy(measured_hbm, measured, sems.at[1]),
    ]
    for load in loads:
        load.start()
    own = choose_sides([pos[i, 0] for i in range(4)], [pos[i, 1] for i in range(4)], cnt[0])
    prev = choose_sides(
        [prev_pos[i, 0] for i in range(4)], [prev_pos[i, 1] for i in range(4)], prev_cnt[0]
    )
    for k, side in enumerate(own + prev):
        for w, word in enumerate(side):
            plan[k * SPAN + w] = word
    for load in loads:
        load.wait()

    def copy_rows(out, at, j, first, count):
        start = plan[at + 2 + 5 * j + 3]
        low = pl.multiple_of(plan[at + 2 + 5 * j + 1] * N, N)
        high = pl.multiple_of(plan[at + 2 + 5 * j + 1] * N + N, N)
        keep = lanes() >= plan[at + 2 + 5 * j + 2]

        def step(g, carry):
            src = pl.multiple_of((first + g) * 8, 8)
            dst = pl.multiple_of((start + g) * 8, 8)
            for c in range(2):
                out[c, pl.ds(dst, 8), :] = jnp.where(
                    keep, tile[c, pl.ds(src, 8), pl.ds(low, N)], tile[c, pl.ds(src, 8), pl.ds(high, N)]
                )
            return carry

        lax.fori_loop(0, count, step, 0)

    def right_job(j, carry):
        first = lax.div(plan[OWN_RIGHT + 2 + 5 * j], 8)
        copy_rows(ahead, OWN_RIGHT, j, first, 32 - first)
        slot = plan[OWN_RIGHT + 2 + 5 * j + 4]
        dst = pl.multiple_of((plan[OWN_RIGHT + 1] + 8 * j) * 8, 8)
        for c in range(2):
            src = pl.multiple_of(depth * HALF + 64 * c, 64)
            ahead[c, pl.ds(dst, 64), :] = measured[slot, pl.ds(src, 64), :]
        return carry

    lax.fori_loop(0, plan[OWN_RIGHT], right_job, 0)

    def left_job(j, carry):
        copy_rows(behind, PREV_LEFT, j, 0, lax.div(plan[PREV_LEFT + 2 + 5 * j] + 7, 8))
        return carry

    lax.fori_loop(0, plan[PREV_LEFT], left_job, 0)


def exchange_kernel(
    n_lat, ahead, behind, tile, received, other,
    row_send, row_recv, tile_send, tile_recv,
):
    depth = lax.axis_index("depth")
    lat = lax.axis_index("lat")
    after = lax.rem(lat + 1, n_lat)
    before = lax.rem(lat + n_lat - 1, n_lat)
    greet(depth, lat, after, before)
    pl.semaphore_wait(pltpu.get_barrier_semaphore(), 4)
    sends = [
        remote(ahead, received.at[depth], row_send.at[0], row_recv.at[depth], 1, after),
        remote(behind, received.at[depth], row_send.at[1], row_recv.at[depth], 0, before),
    ]
    for copy in sends:
        copy.start()
    swap = remote(tile, other, tile_send, tile_recv, 1 - depth, lat)
    swap.start()
    for copy in sends:
        copy.wait_send()
    for s in range(2):
        remote(ahead, received.at[s], row_send.at[0], row_recv.at[s], 1, after).wait_recv()
    swap.wait()


def remote(src, dst, send, recv, depth, lat):
    return pltpu.make_async_remote_copy(
        src_ref=src,
        dst_ref=dst,
        send_sem=send,
        recv_sem=recv,
        device_id=(depth, lat),
        device_id_type=pl.DeviceIdType.MESH,
    )


def greet(depth, lat, after, before):
    barrier = pltpu.get_barrier_semaphore()
    partners = [
        (depth, after),
        (depth, before),
        (1 - depth, jnp.where(depth == 0, after, before)),
        (1 - depth, lat),
    ]
    for partner in partners:
        pl.semaphore_signal(
            barrier, inc=1, device_id=partner, device_id_type=pl.DeviceIdType.MESH
        )


def return_kernel(
    n_lat, rows_hbm, theirs_hbm, received, partner,
    row_send, row_recv, swap_send, swap_recv,
):
    depth = lax.axis_index("depth")
    lat = lax.axis_index("lat")
    after = lax.rem(lat + 1, n_lat)
    before = lax.rem(lat + n_lat - 1, n_lat)
    greet(depth, lat, after, before)
    pl.semaphore_wait(pltpu.get_barrier_semaphore(), 4)
    target = jnp.where(depth == 0, after, before)
    sends = [
        remote(
            rows_hbm.at[s], received.at[depth], row_send.at[s], row_recv.at[depth], s, target
        )
        for s in range(2)
    ]
    for copy in sends:
        copy.start()
    swap = remote(theirs_hbm, partner, swap_send, swap_recv, 1 - depth, lat)
    swap.start()
    for copy in sends:
        copy.wait_send()
    for c in range(2):
        remote(
            rows_hbm.at[0], received.at[c], row_send.at[0], row_recv.at[c], 0, target
        ).wait_recv()
    swap.wait()


P_PLUS, P_MINUS, F_EVEN, F_ODD = 0, 1, 2, 3
TURNED = 4


def halves(x):
    hi = x.astype(jnp.bfloat16)
    lo = (x - hi.astype(jnp.float32)).astype(jnp.bfloat16)
    return hi, lo


def dot(a, b):
    return jnp.dot(a, b, preferred_element_type=jnp.float32)


def times_right(x, table, at):
    hi, lo = halves(x)
    return dot(
        jnp.concatenate([hi, lo, hi], axis=1),
        jnp.concatenate([table[at, 0], table[at, 0], table[at, 1]], axis=0),
    )


def times_left(table, at, x):
    hi, lo = halves(x)
    return dot(
        jnp.concatenate([table[at, 0], table[at, 0], table[at, 1]], axis=1),
        jnp.concatenate([hi, lo, hi], axis=0),
    )


def fold_columns(re, im):
    plus = jnp.concatenate([re[:, :HALF] + re[:, HALF:], im[:, :HALF] + im[:, HALF:]], axis=1)
    minus = jnp.concatenate([re[:, :HALF] - re[:, HALF:], im[:, :HALF] - im[:, HALF:]], axis=1)
    return plus, minus


def pair_columns(re, im):
    return (
        jnp.concatenate([re[:, :HALF], im[:, :HALF]], axis=1),
        jnp.concatenate([re[:, HALF:], im[:, HALF:]], axis=1),
    )


def fold_rows(re, im):
    plus = jnp.concatenate([re[:HALF] + re[HALF:], im[:HALF] + im[HALF:]], axis=0)
    minus = jnp.concatenate([re[:HALF] - re[HALF:], im[:HALF] - im[HALF:]], axis=0)
    return plus, minus


def pair_rows(re, im):
    return (
        jnp.concatenate([re[:HALF], im[:HALF]], axis=0),
        jnp.concatenate([re[HALF:], im[HALF:]], axis=0),
    )


def propagate(re, im, table, adjoint):
    left, right = (TURNED, 0) if adjoint else (0, TURNED)
    plus, minus = fold_columns(re, im)
    plus = times_right(plus, table, right + P_PLUS)
    minus = times_right(minus, table, right + P_MINUS)
    re, im = pair_columns(plus + minus, plus - minus)
    plus, minus = fold_rows(re, im)
    plus = times_left(table, left + P_PLUS, plus)
    minus = times_left(table, left + P_MINUS, minus)
    return pair_rows(plus + minus, plus - minus)


def to_spectrum(re, im, table):
    plus, minus = fold_columns(re, im)
    re, im = pair_columns(
        times_right(plus, table, TURNED + F_EVEN), times_right(minus, table, TURNED + F_ODD)
    )
    plus, minus = fold_rows(re, im)
    return pair_rows(times_left(table, F_EVEN, plus), times_left(table, F_ODD, minus))


def from_spectrum(re, im, table):
    even, odd = pair_columns(re, im)
    plus = times_right(even, table, F_EVEN)
    minus = times_right(odd, table, F_ODD)
    re, im = pair_columns(plus + minus, plus - minus)
    even, odd = pair_rows(re, im)
    plus = times_left(table, TURNED + F_EVEN, even)
    minus = times_left(table, TURNED + F_ODD, odd)
    return pair_rows(plus + minus, plus - minus)


def compute_kernel(
    plan, tile, other, rows_in, measured, probe, table,
    rows_out, mine, theirs,
    strips, received, amplitude, spread, grads, sems, fetch_sems, out_sems,
):
    depth = lax.axis_index("depth")
    at = jnp.where(depth == 0, OWN_LEFT, PREV_RIGHT)
    jobs = plan[at]

    def fetches(j):
        column = pl.multiple_of(plan[at + 2 + 5 * j + 1] * N, N)
        slot = plan[at + 2 + 5 * j + 4]
        return [
            pltpu.make_async_copy(
                tile.at[:, :, pl.ds(column, 2 * N)], strips.at[j, depth], fetch_sems.at[j, 0]
            ),
            pltpu.make_async_copy(
                other.at[:, :, pl.ds(column, 2 * N)], strips.at[j, 1 - depth], fetch_sems.at[j, 1]
            ),
            pltpu.make_async_copy(measured.at[slot], amplitude.at[j], fetch_sems.at[j, 2]),
        ]

    def stores(j):
        return [
            pltpu.make_async_copy(grads.at[j, depth], mine.at[j], out_sems.at[j, 0]),
            pltpu.make_async_copy(grads.at[j, 1 - depth], theirs.at[j], out_sems.at[j, 1]),
        ]

    copies = [
        pltpu.make_async_copy(rows_in.at[s], received.at[s, :, pl.ds(PAD, ROWS), :], sems.at[s])
        for s in range(2)
    ]
    for copy in copies:
        copy.start()

    def begin(j, carry):
        for copy in fetches(j):
            copy.start()
        return carry

    lax.fori_loop(0, jobs, begin, 0)
    row = lax.broadcasted_iota(jnp.int32, (N, N), 0)
    lane = lax.broadcasted_iota(jnp.int32, (N, N), 1)
    order = jnp.where(lane < HALF, 2 * lane, 2 * lane - (N - 1))
    shuffle = jnp.where(row == order, 1.0, 0.0).astype(jnp.bfloat16)
    for copy in copies:
        copy.wait()

    def job(j, carry):
        r = plan[at + 2 + 5 * j]
        shift = plan[at + 2 + 5 * j + 2]
        start = plan[at + 2 + 5 * j + 3]
        for copy in fetches(j):
            copy.wait()

        @pl.when(depth == 1)
        def _():
            src = pl.multiple_of(PAD + (plan[PREV_RIGHT + 1] + 8 * j) * 8, 8)
            for s in range(2):
                for c in range(2):
                    amplitude[j, pl.ds(128 * s + 64 * c, 64), :] = received[s, c, pl.ds(src, 64), :]

        low = jnp.where(depth == 0, r, 0)
        high = jnp.where(depth == 0, N, r)
        here = (row >= low) & (row < high)
        keep = lane >= shift
        base = jnp.where(depth == 0, 0, lax.div(r, 8))
        src = pl.multiple_of(PAD + (start - base) * 8, 8)

        def window(s):
            return [
                jnp.where(
                    here,
                    jnp.where(keep, strips[j, s, c, :, :N], strips[j, s, c, :, N:]),
                    received[s, c, pl.ds(src, N), :],
                )
                for c in range(2)
            ]

        def rolled(c):
            turned = pltpu.roll(probe[c], r, 0)
            return pltpu.roll(turned, jnp.where(shift == N, 0, shift), 1)

        p_re, p_im = rolled(0), rolled(1)
        o_re, o_im = window(0)
        w_re, w_im = propagate(
            p_re * o_re - p_im * o_im, p_re * o_im + p_im * o_re, table, False
        )
        o_re, o_im = window(1)
        f_re, f_im = to_spectrum(w_re * o_re - w_im * o_im, w_re * o_im + w_im * o_re, table)
        hi, lo = halves(amplitude[j])
        apart = dot(
            jnp.concatenate([hi, lo], axis=1), jnp.concatenate([shuffle, shuffle], axis=0)
        )
        for k in range(2):
            spread[k] = apart[:, HALF * k : HALF * k + HALF]
        apart = jnp.concatenate(
            [
                jnp.concatenate([spread[k, pl.ds(p, HALF, stride=2), :] for k in range(2)], axis=1)
                for p in range(2)
            ],
            axis=0,
        )
        factor = 1.0 - apart / jnp.sqrt(f_re * f_re + f_im * f_im + 1.0)
        a_re, a_im = from_spectrum(f_re * factor, f_im * factor, table)
        grads[j, 1, 0] = w_re * a_re + w_im * a_im
        grads[j, 1, 1] = w_re * a_im - w_im * a_re
        a_re, a_im = propagate(
            o_re * a_re + o_im * a_im, o_re * a_im - o_im * a_re, table, True
        )
        grads[j, 0, 0] = p_re * a_re + p_im * a_im
        grads[j, 0, 1] = p_re * a_im - p_im * a_re
        for copy in stores(j):
            copy.start()
        count = jnp.where(depth == 0, lax.div(r + 7, 8), 32 - lax.div(r, 8))

        def step(g, carry):
            src = pl.multiple_of((base + g) * 8, 8)
            dst = pl.multiple_of((start + g) * 8, 8)
            for s in range(2):
                for c in range(2):
                    rows_out[s, c, pl.ds(dst, 8), :] = grads[j, s, c, pl.ds(src, 8), :]
            return carry

        lax.fori_loop(0, count, step, 0)
        return carry

    lax.fori_loop(0, jobs, job, 0)

    def finish(j, carry):
        for copy in stores(j):
            copy.wait()
        return carry

    lax.fori_loop(0, jobs, finish, 0)


def gather_kernel(
    plan, rows_in, partner, mine, out,
    tile, rows, windows, sems, out_sems,
):
    depth = lax.axis_index("depth")
    copies = [
        pltpu.make_async_copy(mine, windows.at[depth], sems.at[0]),
        pltpu.make_async_copy(partner, windows.at[1 - depth], sems.at[1]),
        pltpu.make_async_copy(rows_in, rows, sems.at[2]),
    ]
    for copy in copies:
        copy.start()

    def clear(i, carry):
        at = pl.multiple_of(i * 8, 8)
        for c in range(2):
            tile[c, pl.ds(at, 8), :] = jnp.zeros((8, tile.shape[2]), jnp.float32)
        return carry

    lax.fori_loop(0, N // 8, clear, 0)
    for copy in copies:
        copy.wait()
    row = lax.broadcasted_iota(jnp.int32, (8, N), 0)

    def add(at, j, c, lower, packed):
        r = plan[at + 2 + 5 * j]
        block = plan[at + 2 + 5 * j + 1]
        start = plan[at + 2 + 5 * j + 3]
        first = 0 if lower else lax.div(r, 8)
        last = lax.div(r + 7, 8) if lower else 32
        keep = lanes() >= plan[at + 2 + 5 * j + 2]
        low = pl.multiple_of(block * N, N)
        high = pl.multiple_of(block * N + N, N)

        def step(g, carry):
            dst = pl.multiple_of(g * 8, 8)
            inside = (row + dst < r) if lower else (row + dst >= r)
            if packed:
                src = pl.multiple_of((start + g - first) * 8, 8)
                value = rows[0 if lower else 1, c, pl.ds(src, 8), :]
            else:
                value = windows[1 if lower else 0, j, c, pl.ds(dst, 8), :]
            value = jnp.where(inside, value, 0.0)
            tile[c, pl.ds(dst, 8), pl.ds(low, N)] += jnp.where(keep, value, 0.0)
            tile[c, pl.ds(dst, 8), pl.ds(high, N)] += jnp.where(keep, 0.0, value)
            return carry

        lax.fori_loop(first, last, step, 0)

    for c in range(2):
        for at, lower, packed in (
            (OWN_LEFT, False, False),
            (PREV_RIGHT, True, False),
            (OWN_RIGHT, False, True),
            (PREV_LEFT, True, True),
        ):

            def step(j, carry, at=at, lower=lower, packed=packed, c=c):
                add(at, j, c, lower, packed)
                return carry

            lax.fori_loop(0, plan[at], step, 0)
        pltpu.make_async_copy(tile.at[c], out.at[c], out_sems.at[c]).start()
    for c in range(2):
        pltpu.make_async_copy(tile.at[c], out.at[c], out_sems.at[c]).wait()


SMEM = pl.BlockSpec(memory_space=pltpu.SMEM)
VMEM = pl.BlockSpec(memory_space=pltpu.VMEM)
ANY = pl.BlockSpec(memory_space=pl.ANY)


def shape(*dims):
    return jax.ShapeDtypeStruct(dims, jnp.float32)


def shards(n_lat, object_slices, probe, measured, positions, counts):
    columns = object_slices.shape[3]
    tile = object_slices.reshape(object_slices.shape[1:])
    dma = pltpu.SemaphoreType.DMA
    prev_positions, prev_counts = pl.pallas_call(
        functools.partial(announce_kernel, n_lat),
        name="announce",
        out_shape=(
            jax.ShapeDtypeStruct(positions.shape, jnp.int32),
            jax.ShapeDtypeStruct(counts.shape, jnp.int32),
        ),
        in_specs=[ANY, ANY],
        out_specs=(ANY, ANY),
        scratch_shapes=[dma((2,)), dma((2,))],
        compiler_params=pltpu.CompilerParams(collective_id=2, has_side_effects=True),
    )(positions, counts)
    plan, ahead, behind = pl.pallas_call(
        pack_kernel,
        name="pack",
        out_shape=(
            jax.ShapeDtypeStruct((4 * SPAN,), jnp.int32),
            shape(2, ROWS, N),
            shape(2, ROWS, N),
        ),
        in_specs=[SMEM, SMEM, SMEM, SMEM, ANY, ANY],
        out_specs=(SMEM, VMEM, VMEM),
        scratch_shapes=[
            pltpu.VMEM((2, N, columns), jnp.float32),
            pltpu.VMEM((4, N, N), jnp.float32),
            dma((2,)),
        ],
        compiler_params=pltpu.CompilerParams(vmem_limit_bytes=40 << 20),
    )(positions, counts, prev_positions, prev_counts, tile, measured)
    rows_in, other = pl.pallas_call(
        functools.partial(exchange_kernel, n_lat),
        name="exchange",
        out_shape=(shape(2, 2, ROWS, N), shape(2, N, columns)),
        in_specs=[ANY, ANY, ANY],
        out_specs=(ANY, ANY),
        scratch_shapes=[dma((2,)), dma((2,)), dma, dma],
        compiler_params=pltpu.CompilerParams(collective_id=0, has_side_effects=True),
    )(ahead, behind, tile)

    table = jnp.asarray(tables())
    rows_out, mine, theirs = pl.pallas_call(
        compute_kernel,
        name="compute",
        out_shape=(
            shape(2, 2, ROWS, N),
            shape(MAX_JOBS, 2, N, N),
            shape(MAX_JOBS, 2, N, N),
        ),
        in_specs=[SMEM, ANY, ANY, ANY, ANY, VMEM, VMEM],
        out_specs=(VMEM, ANY, ANY),
        scratch_shapes=[
            pltpu.VMEM((MAX_JOBS, 2, 2, N, 2 * N), jnp.float32),
            pltpu.VMEM((2, 2, ROWS + 2 * PAD, N), jnp.float32),
            pltpu.VMEM((MAX_JOBS, N, N), jnp.float32),
            pltpu.VMEM((2, N, HALF), jnp.float32),
            pltpu.VMEM((MAX_JOBS, 2, 2, N, N), jnp.float32),
            dma((2,)), dma((MAX_JOBS, 3)), dma((MAX_JOBS, 2)),
        ],
        compiler_params=pltpu.CompilerParams(vmem_limit_bytes=50 << 20),
    )(plan, tile, other, rows_in, measured, probe, table)

    rows_back, partner = pl.pallas_call(
        functools.partial(return_kernel, n_lat),
        name="giveback",
        out_shape=(shape(2, 2, ROWS, N), shape(MAX_JOBS, 2, N, N)),
        in_specs=[ANY, ANY],
        out_specs=(ANY, ANY),
        scratch_shapes=[dma((2,)), dma((2,)), dma, dma],
        compiler_params=pltpu.CompilerParams(collective_id=1, has_side_effects=True),
    )(rows_out, theirs)

    out = pl.pallas_call(
        gather_kernel,
        name="gather",
        out_shape=shape(2, N, columns),
        in_specs=[SMEM, ANY, ANY, ANY],
        out_specs=ANY,
        scratch_shapes=[
            pltpu.VMEM((2, N, columns), jnp.float32),
            pltpu.VMEM((2, 2, ROWS, N), jnp.float32),
            pltpu.VMEM((2, MAX_JOBS, 2, N, N), jnp.float32),
            dma((3,)), dma((2,)),
        ],
        compiler_params=pltpu.CompilerParams(vmem_limit_bytes=40 << 20),
    )(plan, rows_back, partner, mine)
    return out.reshape(object_slices.shape)


def solution(mesh):
    return jax.shard_map(
        functools.partial(shards, mesh.shape["lat"]),
        mesh=mesh,
        in_specs=(
            P("depth", None, "lat", None),
            P(),
            P("lat", None, None),
            P("lat", None),
            P("lat"),
        ),
        out_specs=P("depth", None, "lat", None),
        check_vma=False,
    )
```

time: 93.6 us -> 95 us (1.015)
  Pallas kernels: 17.3 us -> 82 us
  waiting for transfers between devices: 44.1 us -> 0 us
  starting transfers between devices: 25.5 us -> 0 us
  local copies, waits for them, and re-layouts: 5.59 us -> 11.8 us
    pallas_call x1 -> x4, Pallas kernels: 11 us -> 74.2 us  [the longest x1 25.7 us: shards(): pl.pallas_call(functools.partial(return_kernel, n_lat), name='giveback',...]
    ppermute x8 -> x0, waiting for transfers between devices: 44.1 us -> none  [the longest x1 19.9 us: shards(): x_same = lax.ppermute(send_same, axes, to_same)]
    ppermute x8 -> x0, starting transfers between devices: 25.5 us -> none  [the longest x1 17.2 us: shards(): r_other = lax.ppermute(g_other, axes, back_other)]
    unnamed x9 -> x25, local copies, waits for them, and re-layouts: 5.59 us -> 11.8 us
    pallas_call x1, Pallas kernels: 3.83 us -> 4.99 us  [shards(): pl.pallas_call(gather_kernel, name='gather', out_shape=shape(2, N, column...]
  transfers between devices with their start and end apart: 8 -> 0, of which waited for: 6 -> 0; matrix products, arithmetic and copies ran while one was open for 1% -> 0% of each run, Pallas kernels for 3% -> 0%
where the time goes in v2:
time: 95 us; the launch traced here: 94.6 us
  Pallas kernels  82 us (86%)
  local copies, waits for them, and re-layouts  11.8 us (12%)
    pallas_call x1, Pallas kernels, shards(): pl.pallas_call(functools.partial(return_kernel, n_lat), name='giveback',...  25.7 us
    pallas_call x1, Pallas kernels, shards(): pl.pallas_call(functools.partial(exchange_kernel, n_lat), name='exchange'...  25.1 us
    pallas_call x1, Pallas kernels, shards(): pl.pallas_call(compute_kernel, name='compute', out_shape=(shape(2, 2, ROW...  12.4 us
    unnamed x25, local copies, waits for them, and re-layouts  11.8 us
    pallas_call x1, Pallas kernels, shards(): pl.pallas_call(functools.partial(announce_kernel, n_lat), name='announce'...  11.1 us
    pallas_call x1, Pallas kernels, shards(): pl.pallas_call(gather_kernel, name='gather', out_shape=shape(2, N, column...  4.99 us
    pallas_call x1, Pallas kernels, shards(): pl.pallas_call(pack_kernel, name='pack', out_shape=(jax.ShapeDtypeStruct(...  2.79 us

profile of v2, /device:TPU:1, one launch (start us, length us, event | category | flops | bytes accessed | tf_op | source)
XLA Modules:
  0.0 94.6 jit_solution(4716594177756564929)
XLA Ops:
  0.7 1.3 %copy.8.pos = s32[4,2]{1,0:T(4,128)} copy(s32[4,2]{0,1:T(2,128)} %param.9) | data formatting | bytes 64 | tf_op args[3]
  2.0 11.1 %announce.1 = (s32[4,2]{1,0:T(4,128)}, s32[1]{0:T(128)}) custom-call(s32[4,2]{1,0:T(4,128)} %copy.8.pos, s32[1]{0:T(128)S(6)} %copy.9.cnt), custom_call_target="tpu_custom_call" | custom-call | tf_op jit(solution)/shard_map/announce/pallas_call | solution.py:553
  13.1 0.0 copy-start
  13.1 2.2 %copy-done = f32[1,2,256,2048]{3,2,1,0:T(8,128)S(1)} copy-done((f32[1,2,256,2048]{3,2,1,0:T(8,128)S(1)}, f32[1,2,256,2048]{3,2,1,0:T(8,128)}, u32[]{:S(2)}) %copy-start) | copy-done | bytes 4194328
  15.3 0.0 copy-start.1
  15.3 1.2 %copy-done.1 = f32[4,256,256]{2,1,0:T(8,128)S(1)} copy-done((f32[4,256,256]{2,1,0:T(8,128)S(1)}, f32[4,256,256]{2,1,0:T(8,128)}, u32[]{:S(2)}) %copy-start.1) | copy-done | bytes 1048600
  16.5 0.7 copy-done.10
  17.2 0.7 copy-done.11
  17.9 2.8 %pack.1 = (s32[80]{0:T(128)S(1)}, f32[2,384,256]{2,1,0:T(8,128)S(1)}, f32[2,384,256]{2,1,0:T(8,128)S(1)}) custom-call(s32[4,2]{1,0:T(4,128)S(1)} %copy-done.10, s32[1]{0:T(128)S(6)} %copy.9.cnt, s32[4,2]{1,0:T(4,128)S(1)} %copy-done.11, s32[1]{0:T(128)} %get-tuple-element.18.prev_cnt, f32[2,256,2048]{2,1,0:T(8,128)S(1)} %bitcast.4, f32[4,256,256]{2,1,0:T(8,128)S(1)} %copy-done.1), custom_call_target="tpu_custom_call" | custom-call | tf_op jit(solution)/shard_map/pack/pallas_call | solution.py:565
  20.7 0.0 copy-start.7
  20.7 0.9 copy-done.7
  21.6 0.9 copy-done.8
  22.4 25.1 %exchange.1 = (f32[2,2,384,256]{3,2,1,0:T(8,128)}, f32[2,256,2048]{2,1,0:T(8,128)}) custom-call(f32[2,384,256]{2,1,0:T(8,128)} %copy-done.7, f32[2,384,256]{2,1,0:T(8,128)} %copy-done.8, f32[2,256,2048]{2,1,0:T(8,128)} %bitcast.2), custom_call_target="tpu_custom_call" | custom-call | tf_op jit(solution)/shard_map/exchange/pallas_call | solution.py:582
  47.5 0.0 copy-done.2
  47.5 0.0 copy-done.9
  47.5 12.4 %compute.1 = (f32[2,2,384,256]{3,2,1,0:T(8,128)S(1)}, f32[3,2,256,256]{3,2,1,0:T(8,128)}, f32[3,2,256,256]{3,2,1,0:T(8,128)}) custom-call(s32[80]{0:T(128)S(1)} %get-tuple-element.19.plan, f32[2,256,2048]{2,1,0:T(8,128)} %bitcast.3, f32[2,256,2048]{2,1,0:T(8,128)} %get-tuple-element.22.other, f32[2,2,384,256]{3,2,1,0:T(8,128)} %get-tuple-element.23.rows_in, ...), custom_call_target="tpu_custom_call" | custom-call | tf_op jit(solution)/shard_map/compute/pallas_call | solution.py:593
  59.9 0.0 copy-start.6
  59.9 1.2 %copy-done.6 = f32[2,2,384,256]{3,2,1,0:T(8,128)} copy-done((f32[2,2,384,256]{3,2,1,0:T(8,128)}, f32[2,2,384,256]{3,2,1,0:T(8,128)S(1)}, u32[]{:S(2)}) %copy-start.6) | copy-done | bytes 1572888
  61.1 25.7 %giveback.1 = (f32[2,2,384,256]{3,2,1,0:T(8,128)}, f32[3,2,256,256]{3,2,1,0:T(8,128)}) custom-call(f32[2,2,384,256]{3,2,1,0:T(8,128)} %copy-done.6, f32[3,2,256,256]{3,2,1,0:T(8,128)} %get-tuple-element.25.theirs_hbm), custom_call_target="tpu_custom_call" | custom-call | tf_op jit(solution)/shard_map/giveback/pallas_call | solution.py:614
  86.8 0.0 copy-done.3
  86.8 0.0 copy-start.4
  86.8 1.4 %copy-done.4 = f32[2,2,384,256]{3,2,1,0:T(8,128)S(1)} copy-done((f32[2,2,384,256]{3,2,1,0:T(8,128)S(1)}, f32[2,2,384,256]{3,2,1,0:T(8,128)}, u32[]{:S(2)}) %copy-start.4) | copy-done | bytes 1572888
  88.2 1.4 %copy-done.5 = f32[3,2,256,256]{3,2,1,0:T(8,128)S(1)} copy-done((f32[3,2,256,256]{3,2,1,0:T(8,128)S(1)}, f32[3,2,256,256]{3,2,1,0:T(8,128)}, u32[]{:S(2)}) %copy-start.5) | copy-done | bytes 1572888
  89.6 5.0 %gather.1 = f32[2,256,2048]{2,1,0:T(8,128)} custom-call(s32[80]{0:T(128)S(1)} %get-tuple-element.19.plan, f32[2,2,384,256]{3,2,1,0:T(8,128)S(1)} %copy-done.4, f32[3,2,256,256]{3,2,1,0:T(8,128)S(1)} %copy-done.5, f32[3,2,256,256]{3,2,1,0:T(8,128)S(1)} %copy-done.3), custom_call_target="tpu_custom_call" | custom-call | tf_op jit(solution)/shard_map/gather/pallas_call | solution.py:624
  (7 shorter events, 0.0 us)
Async XLA Ops:
  13.1 2.2 %copy-start = (f32[1,2,256,2048]{3,2,1,0:T(8,128)S(1)}, f32[1,2,256,2048]{3,2,1,0:T(8,128)}, u32[]{:S(2)}) copy-start(f32[1,2,256,2048]{3,2,1,0:T(8,128)} %param.6) | copy-start | bytes 12582916
  15.3 1.2 %copy-start.1 = (f32[4,256,256]{2,1,0:T(8,128)S(1)}, f32[4,256,256]{2,1,0:T(8,128)}, u32[]{:S(2)}) copy-start(f32[4,256,256]{2,1,0:T(8,128)} %measured.1) | copy-start | bytes 3145732
  16.5 0.7 copy-start.10
  17.2 0.7 copy-start.11
  20.7 0.9 copy-start.7
  21.6 0.9 copy-start.8
  22.4 25.1 %copy-start.2 = (f32[4,256,256]{2,1,0:T(8,128)S(1)}, f32[4,256,256]{2,1,0:T(8,128)}, u32[]{:S(2)}) copy-start(f32[4,256,256]{2,1,0:T(8,128)} %measured.1) | copy-start | bytes 3145732
  22.4 25.1 %copy-start.9 = (f32[2,256,256]{2,1,0:T(8,128)S(1)}, f32[2,256,256]{2,1,0:T(8,128)}, u32[]{:S(2)}) copy-start(f32[2,256,256]{2,1,0:T(8,128)} %probe.1) | copy-start | bytes 1572868
  59.9 1.2 %copy-start.6 = (f32[2,2,384,256]{3,2,1,0:T(8,128)}, f32[2,2,384,256]{3,2,1,0:T(8,128)S(1)}, u32[]{:S(2)}) copy-start(f32[2,2,384,256]{3,2,1,0:T(8,128)S(1)} %get-tuple-element.24.rows_hbm) | copy-start | bytes 4718596
  61.1 25.7 %copy-start.3 = (f32[3,2,256,256]{3,2,1,0:T(8,128)S(1)}, f32[3,2,256,256]{3,2,1,0:T(8,128)}, u32[]{:S(2)}) copy-start(f32[3,2,256,256]{3,2,1,0:T(8,128)} %get-tuple-element.28.mine) | copy-start | bytes 4718596
  86.8 1.4 %copy-start.4 = (f32[2,2,384,256]{3,2,1,0:T(8,128)S(1)}, f32[2,2,384,256]{3,2,1,0:T(8,128)}, u32[]{:S(2)}) copy-start(f32[2,2,384,256]{3,2,1,0:T(8,128)} %get-tuple-element.26.rows_in) | copy-start | bytes 4718596
  88.2 1.4 %copy-start.5 = (f32[3,2,256,256]{3,2,1,0:T(8,128)S(1)}, f32[3,2,256,256]{3,2,1,0:T(8,128)}, u32[]{:S(2)}) copy-start(f32[3,2,256,256]{3,2,1,0:T(8,128)} %get-tuple-element.27.partner) | copy-start | bytes 4718596

commit v3 on v2

--- a/solution.py
+++ b/solution.py
@@ -87,7 +87,11 @@
     return lax.broadcasted_iota(jnp.int32, (8, N), 1)
 
 
-def announce_kernel(n_lat, pos, cnt, prev_pos, prev_cnt, send, recv):
+def announce_kernel(
+    n_lat, pos_hbm, cnt, tile_hbm, measured_hbm,
+    pos, prev_pos, prev_cnt, tile, measured,
+    send, recv, local,
+):
     depth = lax.axis_index("depth")
     lat = lax.axis_index("lat")
     after = lax.rem(lat + 1, n_lat)
@@ -97,37 +101,37 @@
         pl.semaphore_signal(
             barrier, inc=1, device_id=(depth, other), device_id_type=pl.DeviceIdType.MESH
         )
+    loads = [
+        pltpu.make_async_copy(pos_hbm, pos, local.at[0]),
+        pltpu.make_async_copy(tile_hbm, tile, local.at[1]),
+        pltpu.make_async_copy(measured_hbm, measured, local.at[2]),
+    ]
+    for load in loads:
+        load.start()
     pl.semaphore_wait(barrier, 2)
     copies = [
-        remote(pos, prev_pos, send.at[0], recv.at[0], depth, after),
+        remote(pos_hbm, prev_pos, send.at[0], recv.at[0], depth, after),
         remote(cnt, prev_cnt, send.at[1], recv.at[1], depth, after),
     ]
     for copy in copies:
         copy.start()
+    for load in loads:
+        load.wait()
     for copy in copies:
         copy.wait()
 
 
 def pack_kernel(
-    pos, cnt, prev_pos, prev_cnt, tile_hbm, measured_hbm, plan, ahead, behind,
-    tile, measured, sems,
+    pos, cnt, prev_pos, prev_cnt, tile, measured, plan, ahead, behind
 ):
     depth = lax.axis_index("depth")
-    loads = [
-        pltpu.make_async_copy(tile_hbm, tile, sems.at[0]),
-        pltpu.make_async_copy(measured_hbm, measured, sems.at[1]),
-    ]
-    for load in loads:
-        load.start()
-    own = choose_sides([pos[i, 0] for i in range(4)], [pos[i, 1] for i in range(4)], cnt[0])
+    own = choose_sides([pos[0, i] for i in range(4)], [pos[1, i] for i in range(4)], cnt[0])
     prev = choose_sides(
-        [prev_pos[i, 0] for i in range(4)], [prev_pos[i, 1] for i in range(4)], prev_cnt[0]
+        [prev_pos[0, i] for i in range(4)], [prev_pos[1, i] for i in range(4)], prev_cnt[0]
     )
     for k, side in enumerate(own + prev):
         for w, word in enumerate(side):
             plan[k * SPAN + w] = word
-    for load in loads:
-        load.wait()
 
     def copy_rows(out, at, j, first, count):
         start = plan[at + 2 + 5 * j + 3]
@@ -175,9 +179,13 @@
     before = lax.rem(lat + n_lat - 1, n_lat)
     greet(depth, lat, after, before)
     pl.semaphore_wait(pltpu.get_barrier_semaphore(), 4)
+
+    def slot(s):
+        return received.at[s, :, pl.ds(PAD, ROWS), :]
+
     sends = [
-        remote(ahead, received.at[depth], row_send.at[0], row_recv.at[depth], 1, after),
-        remote(behind, received.at[depth], row_send.at[1], row_recv.at[depth], 0, before),
+        remote(ahead, slot(depth), row_send.at[0], row_recv.at[depth], 1, after),
+        remote(behind, slot(depth), row_send.at[1], row_recv.at[depth], 0, before),
     ]
     for copy in sends:
         copy.start()
@@ -186,7 +194,7 @@
     for copy in sends:
         copy.wait_send()
     for s in range(2):
-        remote(ahead, received.at[s], row_send.at[0], row_recv.at[s], 1, after).wait_recv()
+        remote(ahead, slot(s), row_send.at[0], row_recv.at[s], 1, after).wait_recv()
     swap.wait()
 
 
@@ -216,7 +224,7 @@
 
 
 def return_kernel(
-    n_lat, rows_hbm, theirs_hbm, received, partner,
+    n_lat, rows, windows, received, partner,
     row_send, row_recv, swap_send, swap_recv,
 ):
     depth = lax.axis_index("depth")
@@ -227,20 +235,18 @@
     pl.semaphore_wait(pltpu.get_barrier_semaphore(), 4)
     target = jnp.where(depth == 0, after, before)
     sends = [
-        remote(
-            rows_hbm.at[s], received.at[depth], row_send.at[s], row_recv.at[depth], s, target
-        )
+        remote(rows.at[s], received.at[depth], row_send.at[s], row_recv.at[depth], s, target)
         for s in range(2)
     ]
     for copy in sends:
         copy.start()
-    swap = remote(theirs_hbm, partner, swap_send, swap_recv, 1 - depth, lat)
+    swap = remote(windows.at[1 - depth], partner, swap_send, swap_recv, 1 - depth, lat)
     swap.start()
     for copy in sends:
         copy.wait_send()
     for c in range(2):
         remote(
-            rows_hbm.at[0], received.at[c], row_send.at[0], row_recv.at[c], 0, target
+            rows.at[0], received.at[c], row_send.at[0], row_recv.at[c], 0, target
         ).wait_recv()
     swap.wait()
 
@@ -334,66 +340,35 @@
 
 
 def compute_kernel(
-    plan, tile, other, rows_in, measured, probe, table,
-    rows_out, mine, theirs,
-    strips, received, amplitude, spread, grads, sems, fetch_sems, out_sems,
+    plan, tile, other, received, measured, probe, table,
+    rows_out, grads,
+    amplitude, spread,
 ):
     depth = lax.axis_index("depth")
     at = jnp.where(depth == 0, OWN_LEFT, PREV_RIGHT)
     jobs = plan[at]
-
-    def fetches(j):
-        column = pl.multiple_of(plan[at + 2 + 5 * j + 1] * N, N)
-        slot = plan[at + 2 + 5 * j + 4]
-        return [
-            pltpu.make_async_copy(
-                tile.at[:, :, pl.ds(column, 2 * N)], strips.at[j, depth], fetch_sems.at[j, 0]
-            ),
-            pltpu.make_async_copy(
-                other.at[:, :, pl.ds(column, 2 * N)], strips.at[j, 1 - depth], fetch_sems.at[j, 1]
-            ),
-            pltpu.make_async_copy(measured.at[slot], amplitude.at[j], fetch_sems.at[j, 2]),
-        ]
-
-    def stores(j):
-        return [
-            pltpu.make_async_copy(grads.at[j, depth], mine.at[j], out_sems.at[j, 0]),
-            pltpu.make_async_copy(grads.at[j, 1 - depth], theirs.at[j], out_sems.at[j, 1]),
-        ]
-
-    copies = [
-        pltpu.make_async_copy(rows_in.at[s], received.at[s, :, pl.ds(PAD, ROWS), :], sems.at[s])
-        for s in range(2)
-    ]
-    for copy in copies:
-        copy.start()
-
-    def begin(j, carry):
-        for copy in fetches(j):
-            copy.start()
-        return carry
-
-    lax.fori_loop(0, jobs, begin, 0)
     row = lax.broadcasted_iota(jnp.int32, (N, N), 0)
     lane = lax.broadcasted_iota(jnp.int32, (N, N), 1)
     order = jnp.where(lane < HALF, 2 * lane, 2 * lane - (N - 1))
     shuffle = jnp.where(row == order, 1.0, 0.0).astype(jnp.bfloat16)
-    for copy in copies:
-        copy.wait()
 
     def job(j, carry):
         r = plan[at + 2 + 5 * j]
         shift = plan[at + 2 + 5 * j + 2]
         start = plan[at + 2 + 5 * j + 3]
-        for copy in fetches(j):
-            copy.wait()
+        column = pl.multiple_of(plan[at + 2 + 5 * j + 1] * N, N)
+        slot = plan[at + 2 + 5 * j + 4]
+
+        @pl.when(depth == 0)
+        def _():
+            amplitude[...] = measured[slot]
 
         @pl.when(depth == 1)
         def _():
             src = pl.multiple_of(PAD + (plan[PREV_RIGHT + 1] + 8 * j) * 8, 8)
             for s in range(2):
                 for c in range(2):
-                    amplitude[j, pl.ds(128 * s + 64 * c, 64), :] = received[s, c, pl.ds(src, 64), :]
+                    amplitude[pl.ds(128 * s + 64 * c, 64), :] = received[s, c, pl.ds(src, 64), :]
 
         low = jnp.where(depth == 0, r, 0)
         high = jnp.where(depth == 0, N, r)
@@ -403,10 +378,16 @@
         src = pl.multiple_of(PAD + (start - base) * 8, 8)
 
         def window(s):
+            near = depth == s
+            left, right = pl.ds(column, N), pl.ds(pl.multiple_of(column + N, N), N)
             return [
                 jnp.where(
                     here,
-                    jnp.where(keep, strips[j, s, c, :, :N], strips[j, s, c, :, N:]),
+                    jnp.where(
+                        keep,
+                        jnp.where(near, tile[c, :, left], other[c, :, left]),
+                        jnp.where(near, tile[c, :, right], other[c, :, right]),
+                    ),
                     received[s, c, pl.ds(src, N), :],
                 )
                 for c in range(2)
@@ -423,7 +404,7 @@
         )
         o_re, o_im = window(1)
         f_re, f_im = to_spectrum(w_re * o_re - w_im * o_im, w_re * o_im + w_im * o_re, table)
-        hi, lo = halves(amplitude[j])
+        hi, lo = halves(amplitude[...])
         apart = dot(
             jnp.concatenate([hi, lo], axis=1), jnp.concatenate([shuffle, shuffle], axis=0)
         )
@@ -438,15 +419,13 @@
         )
         factor = 1.0 - apart / jnp.sqrt(f_re * f_re + f_im * f_im + 1.0)
         a_re, a_im = from_spectrum(f_re * factor, f_im * factor, table)
-        grads[j, 1, 0] = w_re * a_re + w_im * a_im
-        grads[j, 1, 1] = w_re * a_im - w_im * a_re
+        grads[1, j, 0] = w_re * a_re + w_im * a_im
+        grads[1, j, 1] = w_re * a_im - w_im * a_re
         a_re, a_im = propagate(
             o_re * a_re + o_im * a_im, o_re * a_im - o_im * a_re, table, True
         )
-        grads[j, 0, 0] = p_re * a_re + p_im * a_im
-        grads[j, 0, 1] = p_re * a_im - p_im * a_re
-        for copy in stores(j):
-            copy.start()
+        grads[0, j, 0] = p_re * a_re + p_im * a_im
+        grads[0, j, 1] = p_re * a_im - p_im * a_re
         count = jnp.where(depth == 0, lax.div(r + 7, 8), 32 - lax.div(r, 8))
 
         def step(g, carry):
@@ -454,7 +433,7 @@
             dst = pl.multiple_of((start + g) * 8, 8)
             for s in range(2):
                 for c in range(2):
-                    rows_out[s, c, pl.ds(dst, 8), :] = grads[j, s, c, pl.ds(src, 8), :]
+                    rows_out[s, c, pl.ds(dst, 8), :] = grads[s, j, c, pl.ds(src, 8), :]
             return carry
 
         lax.fori_loop(0, count, step, 0)
@@ -462,26 +441,9 @@
 
     lax.fori_loop(0, jobs, job, 0)
 
-    def finish(j, carry):
-        for copy in stores(j):
-            copy.wait()
-        return carry
-
-    lax.fori_loop(0, jobs, finish, 0)
-
-
-def gather_kernel(
-    plan, rows_in, partner, mine, out,
-    tile, rows, windows, sems, out_sems,
-):
+
+def gather_kernel(plan, rows, partner, grads, out, tile, out_sems):
     depth = lax.axis_index("depth")
-    copies = [
-        pltpu.make_async_copy(mine, windows.at[depth], sems.at[0]),
-        pltpu.make_async_copy(partner, windows.at[1 - depth], sems.at[1]),
-        pltpu.make_async_copy(rows_in, rows, sems.at[2]),
-    ]
-    for copy in copies:
-        copy.start()
 
     def clear(i, carry):
         at = pl.multiple_of(i * 8, 8)
@@ -490,11 +452,9 @@
         return carry
 
     lax.fori_loop(0, N // 8, clear, 0)
-    for copy in copies:
-        copy.wait()
     row = lax.broadcasted_iota(jnp.int32, (8, N), 0)
 
-    def add(at, j, c, lower, packed):
+    def add(at, j, c, lower, packed, near):
         r = plan[at + 2 + 5 * j]
         block = plan[at + 2 + 5 * j + 1]
         start = plan[at + 2 + 5 * j + 3]
@@ -511,7 +471,7 @@
                 src = pl.multiple_of((start + g - first) * 8, 8)
                 value = rows[0 if lower else 1, c, pl.ds(src, 8), :]
             else:
-                value = windows[1 if lower else 0, j, c, pl.ds(dst, 8), :]
+                value = grads[depth, j, c, pl.ds(dst, 8), :] if near else partner[j, c, pl.ds(dst, 8), :]
             value = jnp.where(inside, value, 0.0)
             tile[c, pl.ds(dst, 8), pl.ds(low, N)] += jnp.where(keep, value, 0.0)
             tile[c, pl.ds(dst, 8), pl.ds(high, N)] += jnp.where(keep, 0.0, value)
@@ -519,19 +479,27 @@
 
         lax.fori_loop(first, last, step, 0)
 
+    def run(at, c, lower, packed, near):
+        def step(j, carry):
+            add(at, j, c, lower, packed, near)
+            return carry
+
+        lax.fori_loop(0, plan[at], step, 0)
+
     for c in range(2):
-        for at, lower, packed in (
-            (OWN_LEFT, False, False),
-            (PREV_RIGHT, True, False),
-            (OWN_RIGHT, False, True),
-            (PREV_LEFT, True, True),
-        ):
-
-            def step(j, carry, at=at, lower=lower, packed=packed, c=c):
-                add(at, j, c, lower, packed)
-                return carry
-
-            lax.fori_loop(0, plan[at], step, 0)
+
+        @pl.when(depth == 0)
+        def _(c=c):
+            run(OWN_LEFT, c, False, False, True)
+            run(PREV_RIGHT, c, True, False, False)
+
+        @pl.when(depth == 1)
+        def _(c=c):
+            run(OWN_LEFT, c, False, False, False)
+            run(PREV_RIGHT, c, True, False, True)
+
+        run(OWN_RIGHT, c, False, True, False)
+        run(PREV_LEFT, c, True, True, False)
         pltpu.make_async_copy(tile.at[c], out.at[c], out_sems.at[c]).start()
     for c in range(2):
         pltpu.make_async_copy(tile.at[c], out.at[c], out_sems.at[c]).wait()
@@ -539,7 +507,7 @@
 
 SMEM = pl.BlockSpec(memory_space=pltpu.SMEM)
 VMEM = pl.BlockSpec(memory_space=pltpu.VMEM)
-ANY = pl.BlockSpec(memory_space=pl.ANY)
+HBM = pl.BlockSpec(memory_space=pltpu.HBM)
 
 
 def shape(*dims):
@@ -550,18 +518,24 @@
     columns = object_slices.shape[3]
     tile = object_slices.reshape(object_slices.shape[1:])
     dma = pltpu.SemaphoreType.DMA
-    prev_positions, prev_counts = pl.pallas_call(
+    positions = positions.T
+    own_positions, prev_positions, prev_counts, tile, measured = pl.pallas_call(
         functools.partial(announce_kernel, n_lat),
         name="announce",
         out_shape=(
             jax.ShapeDtypeStruct(positions.shape, jnp.int32),
+            jax.ShapeDtypeStruct(positions.shape, jnp.int32),
             jax.ShapeDtypeStruct(counts.shape, jnp.int32),
+            shape(*tile.shape),
+            shape(*measured.shape),
         ),
-        in_specs=[ANY, ANY],
-        out_specs=(ANY, ANY),
-        scratch_shapes=[dma((2,)), dma((2,))],
-        compiler_params=pltpu.CompilerParams(collective_id=2, has_side_effects=True),
-    )(positions, counts)
+        in_specs=[HBM, HBM, HBM, HBM],
+        out_specs=(VMEM, VMEM, VMEM, VMEM, VMEM),
+        scratch_shapes=[dma((2,)), dma((2,)), dma((3,))],
+        compiler_params=pltpu.CompilerParams(
+            collective_id=2, has_side_effects=True, vmem_limit_bytes=8 << 20
+        ),
+    )(positions, counts, tile, measured)
     plan, ahead, behind = pl.pallas_call(
         pack_kernel,
         name="pack",
@@ -570,71 +544,57 @@
             shape(2, ROWS, N),
             shape(2, ROWS, N),
         ),
-        in_specs=[SMEM, SMEM, SMEM, SMEM, ANY, ANY],
+        in_specs=[SMEM, SMEM, SMEM, SMEM, VMEM, VMEM],
         out_specs=(SMEM, VMEM, VMEM),
-        scratch_shapes=[
-            pltpu.VMEM((2, N, columns), jnp.float32),
-            pltpu.VMEM((4, N, N), jnp.float32),
-            dma((2,)),
-        ],
-        compiler_params=pltpu.CompilerParams(vmem_limit_bytes=40 << 20),
-    )(positions, counts, prev_positions, prev_counts, tile, measured)
-    rows_in, other = pl.pallas_call(
+        compiler_params=pltpu.CompilerParams(vmem_limit_bytes=4 << 20),
+    )(own_positions, counts, prev_positions, prev_counts, tile, measured)
+    received, other = pl.pallas_call(
         functools.partial(exchange_kernel, n_lat),
         name="exchange",
-        out_shape=(shape(2, 2, ROWS, N), shape(2, N, columns)),
-        in_specs=[ANY, ANY, ANY],
-        out_specs=(ANY, ANY),
+        out_shape=(shape(2, 2, ROWS + 2 * PAD, N), shape(2, N, columns)),
+        in_specs=[VMEM, VMEM, VMEM],
+        out_specs=(VMEM, VMEM),
         scratch_shapes=[dma((2,)), dma((2,)), dma, dma],
-        compiler_params=pltpu.CompilerParams(collective_id=0, has_side_effects=True),
+        compiler_params=pltpu.CompilerParams(
+            collective_id=0, has_side_effects=True, vmem_limit_bytes=12 << 20
+        ),
     )(ahead, behind, tile)
 
     table = jnp.asarray(tables())
-    rows_out, mine, theirs = pl.pallas_call(
+    rows_out, grads = pl.pallas_call(
         compute_kernel,
         name="compute",
-        out_shape=(
-            shape(2, 2, ROWS, N),
-            shape(MAX_JOBS, 2, N, N),
-            shape(MAX_JOBS, 2, N, N),
-        ),
-        in_specs=[SMEM, ANY, ANY, ANY, ANY, VMEM, VMEM],
-        out_specs=(VMEM, ANY, ANY),
+        out_shape=(shape(2, 2, ROWS, N), shape(2, MAX_JOBS, 2, N, N)),
+        in_specs=[SMEM, VMEM, VMEM, VMEM, VMEM, VMEM, VMEM],
+        out_specs=(VMEM, VMEM),
         scratch_shapes=[
-            pltpu.VMEM((MAX_JOBS, 2, 2, N, 2 * N), jnp.float32),
-            pltpu.VMEM((2, 2, ROWS + 2 * PAD, N), jnp.float32),
-            pltpu.VMEM((MAX_JOBS, N, N), jnp.float32),
+            pltpu.VMEM((N, N), jnp.float32),
             pltpu.VMEM((2, N, HALF), jnp.float32),
-            pltpu.VMEM((MAX_JOBS, 2, 2, N, N), jnp.float32),
-            dma((2,)), dma((MAX_JOBS, 3)), dma((MAX_JOBS, 2)),
         ],
-        compiler_params=pltpu.CompilerParams(vmem_limit_bytes=50 << 20),
-    )(plan, tile, other, rows_in, measured, probe, table)
+        compiler_params=pltpu.CompilerParams(vmem_limit_bytes=30 << 20),
+    )(plan, tile, other, received, measured, probe, table)
 
     rows_back, partner = pl.pallas_call(
         functools.partial(return_kernel, n_lat),
         name="giveback",
         out_shape=(shape(2, 2, ROWS, N), shape(MAX_JOBS, 2, N, N)),
-        in_specs=[ANY, ANY],
-        out_specs=(ANY, ANY),
+        in_specs=[VMEM, VMEM],
+        out_specs=(VMEM, VMEM),
         scratch_shapes=[dma((2,)), dma((2,)), dma, dma],
-        compiler_params=pltpu.CompilerParams(collective_id=1, has_side_effects=True),
-    )(rows_out, theirs)
+        compiler_params=pltpu.CompilerParams(
+            collective_id=1, has_side_effects=True, vmem_limit_bytes=12 << 20
+        ),
+    )(rows_out, grads)
 
     out = pl.pallas_call(
         gather_kernel,
         name="gather",
         out_shape=shape(2, N, columns),
-        in_specs=[SMEM, ANY, ANY, ANY],
-        out_specs=ANY,
-        scratch_shapes=[
-            pltpu.VMEM((2, N, columns), jnp.float32),
-            pltpu.VMEM((2, 2, ROWS, N), jnp.float32),
-            pltpu.VMEM((2, MAX_JOBS, 2, N, N), jnp.float32),
-            dma((3,)), dma((2,)),
-        ],
-        compiler_params=pltpu.CompilerParams(vmem_limit_bytes=40 << 20),
-    )(plan, rows_back, partner, mine)
+        in_specs=[SMEM, VMEM, VMEM, VMEM],
+        out_specs=HBM,
+        scratch_shapes=[pltpu.VMEM((2, N, columns), jnp.float32), dma((2,))],
+        compiler_params=pltpu.CompilerParams(vmem_limit_bytes=20 << 20),
+    )(plan, rows_back, partner, grads)
     return out.reshape(object_slices.shape)
 
 

time: 95 us -> 79 us (0.83)
  Pallas kernels: 82 us -> 73.9 us
  local copies, waits for them, and re-layouts: 11.8 us -> 4.1 us
    pallas_call x1, Pallas kernels: 12.4 us -> 4.57 us  [shards(): pl.pallas_call(compute_kernel, name='compute', out_shape=(shape(2, 2, ROW...]
    unnamed x25 -> x10, local copies, waits for them, and re-layouts: 11.8 us -> 4.1 us
where the time goes in v3:
time: 79 us; the launch traced here: 78.8 us
  Pallas kernels  73.9 us (94%)
  local copies, waits for them, and re-layouts  4.1 us (5%)
    pallas_call x1, Pallas kernels, shards(): pl.pallas_call(functools.partial(return_kernel, n_lat), name='giveback',...  26.4 us
    pallas_call x1, Pallas kernels, shards(): pl.pallas_call(functools.partial(exchange_kernel, n_lat), name='exchange'...  24.8 us
    pallas_call x1, Pallas kernels, shards(): pl.pallas_call(functools.partial(announce_kernel, n_lat), name='announce'...  11.4 us
    pallas_call x1, Pallas kernels, shards(): pl.pallas_call(compute_kernel, name='compute', out_shape=(shape(2, 2, ROW...  4.57 us
    pallas_call x1, Pallas kernels, shards(): pl.pallas_call(gather_kernel, name='gather', out_shape=shape(2, N, column...  4.23 us
    unnamed x10, local copies, waits for them, and re-layouts  4.1 us
    pallas_call x1, Pallas kernels, shards(): pl.pallas_call(pack_kernel, name='pack', out_shape=(jax.ShapeDtypeStruct(...  2.44 us

profile of v3, /device:TPU:1, one launch (start us, length us, event | category | flops | bytes accessed | tf_op | source)
XLA Modules:
  0.0 78.8 jit_solution(14861243141020177104)
XLA Ops:
  0.7 0.0 copy-start
  0.7 2.2 %copy-done = f32[1,2,256,2048]{3,2,1,0:T(8,128)S(1)} copy-done((f32[1,2,256,2048]{3,2,1,0:T(8,128)S(1)}, f32[1,2,256,2048]{3,2,1,0:T(8,128)}, u32[]{:S(2)}) %copy-start) | copy-done | bytes 4194328
  2.8 0.0 copy-start.2
  2.8 1.2 %copy-done.2 = f32[4,256,256]{2,1,0:T(8,128)S(1)} copy-done((f32[4,256,256]{2,1,0:T(8,128)S(1)}, f32[4,256,256]{2,1,0:T(8,128)}, u32[]{:S(2)}) %copy-start.2) | copy-done | bytes 1048600
  4.1 0.0 copy-start.4
  4.1 0.7 copy-done.4
  4.7 11.4 %announce.1 = (s32[2,4]{1,0:T(2,128)S(1)}, s32[2,4]{1,0:T(2,128)S(1)}, s32[1]{0:T(128)}, f32[2,256,2048]{2,1,0:T(8,128)S(1)}, f32[4,256,256]{2,1,0:T(8,128)S(1)}) custom-call(s32[2,4]{1,0:T(2,128)S(1)} %bitcast.4, s32[1]{0:T(128)S(6)} %copy.7.cnt, f32[2,256,2048]{2,1,0:T(8,128)S(1)} %bitcast.3, f32[4,256,256]{2,1,0:T(8,128)S(1)} %copy-done.2), custom_call_target="tpu_custom_call" | custom-call | tf_op jit(solution)/shard_map/announce/pallas_call | solution.py:522
  16.2 2.4 %pack.1 = (s32[80]{0:T(128)S(1)}, f32[2,384,256]{2,1,0:T(8,128)S(1)}, f32[2,384,256]{2,1,0:T(8,128)S(1)}) custom-call(s32[2,4]{1,0:T(2,128)S(1)} %get-tuple-element.19.pos, s32[1]{0:T(128)S(6)} %copy.7.cnt, s32[2,4]{1,0:T(2,128)S(1)} %get-tuple-element.20.prev_pos, s32[1]{0:T(128)} %get-tuple-element.21.prev_cnt, ...), custom_call_target="tpu_custom_call" | custom-call | tf_op jit(solution)/shard_map/pack/pallas_call | solution.py:539
  18.6 0.0 copy-start.1
  18.6 0.0 copy-start.3
  18.7 24.8 %exchange.1 = (f32[2,2,896,256]{3,2,1,0:T(8,128)S(1)}, f32[2,256,2048]{2,1,0:T(8,128)S(1)}) custom-call(f32[2,384,256]{2,1,0:T(8,128)S(1)} %get-tuple-element.25.ahead, f32[2,384,256]{2,1,0:T(8,128)S(1)} %get-tuple-element.26.behind, f32[2,256,2048]{2,1,0:T(8,128)S(1)} %get-tuple-element.22.tile), custom_call_target="tpu_custom_call" | custom-call | tf_op jit(solution)/shard_map/exchange/pallas_call | solution.py:551
  43.5 0.0 copy-done.1
  43.5 0.0 copy-done.3
  43.5 4.6 %compute.1 = (f32[2,2,384,256]{3,2,1,0:T(8,128)S(1)}, f32[2,3,2,256,256]{4,3,2,1,0:T(8,128)S(1)}) custom-call(s32[80]{0:T(128)S(1)} %get-tuple-element.24.plan, f32[2,256,2048]{2,1,0:T(8,128)S(1)} %get-tuple-element.22.tile, f32[2,256,2048]{2,1,0:T(8,128)S(1)} %get-tuple-element.27.other, f32[2,2,896,256]{3,2,1,0:T(8,128)S(1)} %get-tuple-element.28.received, ...), custom_call_target="tpu_custom_call" | custom-call | tf_op jit(solution)/shard_map/compute/pallas_call | solution.py:564
  48.1 26.4 %giveback.1 = (f32[2,2,384,256]{3,2,1,0:T(8,128)S(1)}, f32[3,2,256,256]{3,2,1,0:T(8,128)S(1)}) custom-call(f32[2,2,384,256]{3,2,1,0:T(8,128)S(1)} %get-tuple-element.29.rows, f32[2,3,2,256,256]{4,3,2,1,0:T(8,128)S(1)} %get-tuple-element.30.windows.grads), custom_call_target="tpu_custom_call" | custom-call | tf_op jit(solution)/shard_map/giveback/pallas_call | solution.py:577
  74.5 4.2 %gather.1 = f32[2,256,2048]{2,1,0:T(8,128)} custom-call(s32[80]{0:T(128)S(1)} %get-tuple-element.24.plan, f32[2,2,384,256]{3,2,1,0:T(8,128)S(1)} %get-tuple-element.31.rows, f32[3,2,256,256]{3,2,1,0:T(8,128)S(1)} %get-tuple-element.32.partner, f32[2,3,2,256,256]{4,3,2,1,0:T(8,128)S(1)} %get-tuple-element.30.windows.grads), custom_call_target="tpu_custom_call" | custom-call | tf_op jit(solution)/shard_map/gather/pallas_call | solution.py:589
Async XLA Ops:
  0.7 2.2 %copy-start = (f32[1,2,256,2048]{3,2,1,0:T(8,128)S(1)}, f32[1,2,256,2048]{3,2,1,0:T(8,128)}, u32[]{:S(2)}) copy-start(f32[1,2,256,2048]{3,2,1,0:T(8,128)} %param.6) | copy-start | bytes 12582916
  2.8 1.2 %copy-start.2 = (f32[4,256,256]{2,1,0:T(8,128)S(1)}, f32[4,256,256]{2,1,0:T(8,128)}, u32[]{:S(2)}) copy-start(f32[4,256,256]{2,1,0:T(8,128)} %measured_hbm.1) | copy-start | bytes 3145732
  4.1 0.7 copy-start.4
  18.6 24.9 %copy-start.1 = (bf16[8,2,256,256]{3,2,1,0:T(8,128)(2,1)S(1)}, bf16[8,2,256,256]{3,2,1,0:T(8,128)(2,1)}, u32[]{:S(2)}) copy-start(bf16[8,2,256,256]{3,2,1,0:T(8,128)(2,1)} %constant.2.clone.table) | copy-start | bytes 6291460
  18.6 24.9 %copy-start.3 = (f32[2,256,256]{2,1,0:T(8,128)S(1)}, f32[2,256,256]{2,1,0:T(8,128)}, u32[]{:S(2)}) copy-start(f32[2,256,256]{2,1,0:T(8,128)} %probe.1) | copy-start | bytes 1572868

commit v4 on v3

--- a/solution.py
+++ b/solution.py
@@ -87,11 +87,7 @@
     return lax.broadcasted_iota(jnp.int32, (8, N), 1)
 
 
-def announce_kernel(
-    n_lat, pos_hbm, cnt, tile_hbm, measured_hbm,
-    pos, prev_pos, prev_cnt, tile, measured,
-    send, recv, local,
-):
+def announce_kernel(n_lat, pos, cnt, prev_pos, prev_cnt, send, recv):
     depth = lax.axis_index("depth")
     lat = lax.axis_index("lat")
     after = lax.rem(lat + 1, n_lat)
@@ -101,30 +97,32 @@
         pl.semaphore_signal(
             barrier, inc=1, device_id=(depth, other), device_id_type=pl.DeviceIdType.MESH
         )
-    loads = [
-        pltpu.make_async_copy(pos_hbm, pos, local.at[0]),
-        pltpu.make_async_copy(tile_hbm, tile, local.at[1]),
-        pltpu.make_async_copy(measured_hbm, measured, local.at[2]),
-    ]
-    for load in loads:
-        load.start()
     pl.semaphore_wait(barrier, 2)
     copies = [
-        remote(pos_hbm, prev_pos, send.at[0], recv.at[0], depth, after),
+        remote(pos, prev_pos, send.at[0], recv.at[0], depth, after),
         remote(cnt, prev_cnt, send.at[1], recv.at[1], depth, after),
     ]
     for copy in copies:
         copy.start()
-    for load in loads:
-        load.wait()
     for copy in copies:
         copy.wait()
 
 
 def pack_kernel(
-    pos, cnt, prev_pos, prev_cnt, tile, measured, plan, ahead, behind
+    pos_hbm, cnt, prev_pos_hbm, prev_cnt, tile_hbm, measured_hbm, plan, ahead, behind,
+    tile, measured, pos, prev_pos, sems,
 ):
     depth = lax.axis_index("depth")
+    loads = [
+        pltpu.make_async_copy(pos_hbm, pos, sems.at[0]),
+        pltpu.make_async_copy(prev_pos_hbm, prev_pos, sems.at[1]),
+        pltpu.make_async_copy(tile_hbm, tile, sems.at[2]),
+        pltpu.make_async_copy(measured_hbm, measured, sems.at[3]),
+    ]
+    for load in loads:
+        load.start()
+    for load in loads[:2]:
+        load.wait()
     own = choose_sides([pos[0, i] for i in range(4)], [pos[1, i] for i in range(4)], cnt[0])
     prev = choose_sides(
         [prev_pos[0, i] for i in range(4)], [prev_pos[1, i] for i in range(4)], prev_cnt[0]
@@ -132,6 +130,8 @@
     for k, side in enumerate(own + prev):
         for w, word in enumerate(side):
             plan[k * SPAN + w] = word
+    for load in loads[2:]:
+        load.wait()
 
     def copy_rows(out, at, j, first, count):
         start = plan[at + 2 + 5 * j + 3]
@@ -307,36 +307,49 @@
     )
 
 
-def propagate(re, im, table, adjoint):
+def product(u, v):
+    return u[0] * v[0] - u[1] * v[1], u[0] * v[1] + u[1] * v[0]
+
+
+def conj_product(u, v):
+    return u[0] * v[0] + u[1] * v[1], u[0] * v[1] - u[1] * v[0]
+
+
+def both_right(pairs, table, first, second):
+    return [(times_right(p, table, first), times_right(m, table, second)) for p, m in pairs]
+
+
+def both_left(pairs, table, first, second):
+    return [(times_left(table, first, p), times_left(table, second, m)) for p, m in pairs]
+
+
+def unfold(pairs):
+    return [(p + m, p - m) for p, m in pairs]
+
+
+def propagate(fields, table, adjoint):
     left, right = (TURNED, 0) if adjoint else (0, TURNED)
-    plus, minus = fold_columns(re, im)
-    plus = times_right(plus, table, right + P_PLUS)
-    minus = times_right(minus, table, right + P_MINUS)
-    re, im = pair_columns(plus + minus, plus - minus)
-    plus, minus = fold_rows(re, im)
-    plus = times_left(table, left + P_PLUS, plus)
-    minus = times_left(table, left + P_MINUS, minus)
-    return pair_rows(plus + minus, plus - minus)
-
-
-def to_spectrum(re, im, table):
-    plus, minus = fold_columns(re, im)
-    re, im = pair_columns(
-        times_right(plus, table, TURNED + F_EVEN), times_right(minus, table, TURNED + F_ODD)
-    )
-    plus, minus = fold_rows(re, im)
-    return pair_rows(times_left(table, F_EVEN, plus), times_left(table, F_ODD, minus))
-
-
-def from_spectrum(re, im, table):
-    even, odd = pair_columns(re, im)
-    plus = times_right(even, table, F_EVEN)
-    minus = times_right(odd, table, F_ODD)
-    re, im = pair_columns(plus + minus, plus - minus)
-    even, odd = pair_rows(re, im)
-    plus = times_left(table, TURNED + F_EVEN, even)
-    minus = times_left(table, TURNED + F_ODD, odd)
-    return pair_rows(plus + minus, plus - minus)
+    pairs = [fold_columns(*f) for f in fields]
+    pairs = unfold(both_right(pairs, table, right + P_PLUS, right + P_MINUS))
+    pairs = [fold_rows(*pair_columns(*p)) for p in pairs]
+    pairs = unfold(both_left(pairs, table, left + P_PLUS, left + P_MINUS))
+    return [pair_rows(*p) for p in pairs]
+
+
+def to_spectrum(fields, table):
+    pairs = [fold_columns(*f) for f in fields]
+    pairs = both_right(pairs, table, TURNED + F_EVEN, TURNED + F_ODD)
+    pairs = [fold_rows(*pair_columns(*p)) for p in pairs]
+    pairs = both_left(pairs, table, F_EVEN, F_ODD)
+    return [pair_rows(*p) for p in pairs]
+
+
+def from_spectrum(fields, table):
+    pairs = [pair_columns(*f) for f in fields]
+    pairs = unfold(both_right(pairs, table, F_EVEN, F_ODD))
+    pairs = [pair_rows(*pair_columns(*p)) for p in pairs]
+    pairs = unfold(both_left(pairs, table, TURNED + F_EVEN, TURNED + F_ODD))
+    return [pair_rows(*p) for p in pairs]
 
 
 def compute_kernel(
@@ -352,34 +365,37 @@
     order = jnp.where(lane < HALF, 2 * lane, 2 * lane - (N - 1))
     shuffle = jnp.where(row == order, 1.0, 0.0).astype(jnp.bfloat16)
 
-    def job(j, carry):
-        r = plan[at + 2 + 5 * j]
-        shift = plan[at + 2 + 5 * j + 2]
-        start = plan[at + 2 + 5 * j + 3]
-        column = pl.multiple_of(plan[at + 2 + 5 * j + 1] * N, N)
-        slot = plan[at + 2 + 5 * j + 4]
-
-        @pl.when(depth == 0)
-        def _():
-            amplitude[...] = measured[slot]
-
-        @pl.when(depth == 1)
-        def _():
-            src = pl.multiple_of(PAD + (plan[PREV_RIGHT + 1] + 8 * j) * 8, 8)
-            for s in range(2):
-                for c in range(2):
-                    amplitude[pl.ds(128 * s + 64 * c, 64), :] = received[s, c, pl.ds(src, 64), :]
-
-        low = jnp.where(depth == 0, r, 0)
-        high = jnp.where(depth == 0, N, r)
-        here = (row >= low) & (row < high)
-        keep = lane >= shift
-        base = jnp.where(depth == 0, 0, lax.div(r, 8))
-        src = pl.multiple_of(PAD + (start - base) * 8, 8)
-
-        def window(s):
+    def work(numbers):
+        each = range(len(numbers))
+        words = [[plan[at + 2 + 5 * j + w] for w in range(5)] for j in numbers]
+
+        for k in each:
+            _, _, _, _, slot = words[k]
+
+            @pl.when(depth == 0)
+            def _(k=k, slot=slot):
+                amplitude[k] = measured[slot]
+
+            @pl.when(depth == 1)
+            def _(k=k):
+                src = pl.multiple_of(PAD + (plan[PREV_RIGHT + 1] + 8 * numbers[k]) * 8, 8)
+                for s in range(2):
+                    for c in range(2):
+                        amplitude[k, pl.ds(128 * s + 64 * c, 64), :] = received[
+                            s, c, pl.ds(src, 64), :
+                        ]
+
+        def base_of(k):
+            return jnp.where(depth == 0, 0, lax.div(words[k][0], 8))
+
+        def window(k, s):
+            r, block, shift, start, _ = words[k]
+            here = (row >= jnp.where(depth == 0, r, 0)) & (row < jnp.where(depth == 0, N, r))
+            keep = lane >= shift
+            src = pl.multiple_of(PAD + (start - base_of(k)) * 8, 8)
+            column = pl.multiple_of(block * N, N)
+            left, right = pl.ds(column, N), pl.ds(pl.multiple_of(column + N, N), N)
             near = depth == s
-            left, right = pl.ds(column, N), pl.ds(pl.multiple_of(column + N, N), N)
             return [
                 jnp.where(
                     here,
@@ -393,53 +409,70 @@
                 for c in range(2)
             ]
 
-        def rolled(c):
-            turned = pltpu.roll(probe[c], r, 0)
-            return pltpu.roll(turned, jnp.where(shift == N, 0, shift), 1)
-
-        p_re, p_im = rolled(0), rolled(1)
-        o_re, o_im = window(0)
-        w_re, w_im = propagate(
-            p_re * o_re - p_im * o_im, p_re * o_im + p_im * o_re, table, False
-        )
-        o_re, o_im = window(1)
-        f_re, f_im = to_spectrum(w_re * o_re - w_im * o_im, w_re * o_im + w_im * o_re, table)
-        hi, lo = halves(amplitude[...])
-        apart = dot(
-            jnp.concatenate([hi, lo], axis=1), jnp.concatenate([shuffle, shuffle], axis=0)
-        )
-        for k in range(2):
-            spread[k] = apart[:, HALF * k : HALF * k + HALF]
-        apart = jnp.concatenate(
-            [
-                jnp.concatenate([spread[k, pl.ds(p, HALF, stride=2), :] for k in range(2)], axis=1)
-                for p in range(2)
-            ],
-            axis=0,
-        )
-        factor = 1.0 - apart / jnp.sqrt(f_re * f_re + f_im * f_im + 1.0)
-        a_re, a_im = from_spectrum(f_re * factor, f_im * factor, table)
-        grads[1, j, 0] = w_re * a_re + w_im * a_im
-        grads[1, j, 1] = w_re * a_im - w_im * a_re
-        a_re, a_im = propagate(
-            o_re * a_re + o_im * a_im, o_re * a_im - o_im * a_re, table, True
-        )
-        grads[0, j, 0] = p_re * a_re + p_im * a_im
-        grads[0, j, 1] = p_re * a_im - p_im * a_re
-        count = jnp.where(depth == 0, lax.div(r + 7, 8), 32 - lax.div(r, 8))
-
-        def step(g, carry):
-            src = pl.multiple_of((base + g) * 8, 8)
-            dst = pl.multiple_of((start + g) * 8, 8)
-            for s in range(2):
-                for c in range(2):
-                    rows_out[s, c, pl.ds(dst, 8), :] = grads[s, j, c, pl.ds(src, 8), :]
-            return carry
-
-        lax.fori_loop(0, count, step, 0)
-        return carry
-
-    lax.fori_loop(0, jobs, job, 0)
+        def rolled(k):
+            r, _, shift, _, _ = words[k]
+            return [
+                pltpu.roll(pltpu.roll(probe[c], r, 0), jnp.where(shift == N, 0, shift), 1)
+                for c in range(2)
+            ]
+
+        probes = [rolled(k) for k in each]
+        waves = [product(p, window(k, 0)) for k, p in enumerate(probes)]
+        waves = propagate(waves, table, False)
+        slices = [window(k, 1) for k in each]
+        spectra = to_spectrum([product(w, o) for w, o in zip(waves, slices)], table)
+        backs = []
+        for k in each:
+            hi, lo = halves(amplitude[k])
+            apart = dot(
+                jnp.concatenate([hi, lo], axis=1), jnp.concatenate([shuffle, shuffle], axis=0)
+            )
+            for h in range(2):
+                spread[k, h] = apart[:, HALF * h : HALF * h + HALF]
+        for k in each:
+            apart = jnp.concatenate(
+                [
+                    jnp.concatenate(
+                        [spread[k, h, pl.ds(p, HALF, stride=2), :] for h in range(2)], axis=1
+                    )
+                    for p in range(2)
+                ],
+                axis=0,
+            )
+            re, im = spectra[k]
+            factor = 1.0 - apart * lax.rsqrt(re * re + im * im + 1.0)
+            backs.append((re * factor, im * factor))
+        backs = from_spectrum(backs, table)
+        for k in each:
+            grads[1, numbers[k], 0], grads[1, numbers[k], 1] = conj_product(waves[k], backs[k])
+        backs = [conj_product(o, b) for o, b in zip(slices, backs)]
+        backs = propagate(backs, table, True)
+        for k in each:
+            grads[0, numbers[k], 0], grads[0, numbers[k], 1] = conj_product(probes[k], backs[k])
+        for k in each:
+            r, start = words[k][0], words[k][3]
+            base = base_of(k)
+            count = jnp.where(depth == 0, lax.div(r + 7, 8), 32 - lax.div(r, 8))
+
+            def step(g, carry, k=k, base=base, start=start):
+                src = pl.multiple_of((base + g) * 8, 8)
+                dst = pl.multiple_of((start + g) * 8, 8)
+                for s in range(2):
+                    for c in range(2):
+                        rows_out[s, c, pl.ds(dst, 8), :] = grads[
+                            s, numbers[k], c, pl.ds(src, 8), :
+                        ]
+                return carry
+
+            lax.fori_loop(0, count, step, 0)
+
+    @pl.when(jobs >= 2)
+    def _():
+        work([0, 1])
+
+    @pl.when(lax.rem(jobs, 2) == 1)
+    def _():
+        work([jobs - 1])
 
 
 def gather_kernel(plan, rows, partner, grads, out, tile, out_sems):
@@ -519,23 +552,18 @@
     tile = object_slices.reshape(object_slices.shape[1:])
     dma = pltpu.SemaphoreType.DMA
     positions = positions.T
-    own_positions, prev_positions, prev_counts, tile, measured = pl.pallas_call(
+    prev_positions, prev_counts = pl.pallas_call(
         functools.partial(announce_kernel, n_lat),
         name="announce",
         out_shape=(
             jax.ShapeDtypeStruct(positions.shape, jnp.int32),
-            jax.ShapeDtypeStruct(positions.shape, jnp.int32),
             jax.ShapeDtypeStruct(counts.shape, jnp.int32),
-            shape(*tile.shape),
-            shape(*measured.shape),
         ),
-        in_specs=[HBM, HBM, HBM, HBM],
-        out_specs=(VMEM, VMEM, VMEM, VMEM, VMEM),
-        scratch_shapes=[dma((2,)), dma((2,)), dma((3,))],
-        compiler_params=pltpu.CompilerParams(
-            collective_id=2, has_side_effects=True, vmem_limit_bytes=8 << 20
-        ),
-    )(positions, counts, tile, measured)
+        in_specs=[HBM, HBM],
+        out_specs=(HBM, HBM),
+        scratch_shapes=[dma((2,)), dma((2,))],
+        compiler_params=pltpu.CompilerParams(collective_id=2, has_side_effects=True),
+    )(positions, counts)
     plan, ahead, behind = pl.pallas_call(
         pack_kernel,
         name="pack",
@@ -544,15 +572,22 @@
             shape(2, ROWS, N),
             shape(2, ROWS, N),
         ),
-        in_specs=[SMEM, SMEM, SMEM, SMEM, VMEM, VMEM],
+        in_specs=[HBM, SMEM, HBM, SMEM, HBM, HBM],
         out_specs=(SMEM, VMEM, VMEM),
-        compiler_params=pltpu.CompilerParams(vmem_limit_bytes=4 << 20),
-    )(own_positions, counts, prev_positions, prev_counts, tile, measured)
+        scratch_shapes=[
+            pltpu.VMEM((2, N, columns), jnp.float32),
+            pltpu.VMEM((4, N, N), jnp.float32),
+            pltpu.SMEM((2, 4), jnp.int32),
+            pltpu.SMEM((2, 4), jnp.int32),
+            dma((4,)),
+        ],
+        compiler_params=pltpu.CompilerParams(vmem_limit_bytes=51 << 20),
+    )(positions, counts, prev_positions, prev_counts, tile, measured)
     received, other = pl.pallas_call(
         functools.partial(exchange_kernel, n_lat),
         name="exchange",
         out_shape=(shape(2, 2, ROWS + 2 * PAD, N), shape(2, N, columns)),
-        in_specs=[VMEM, VMEM, VMEM],
+        in_specs=[VMEM, VMEM, HBM],
         out_specs=(VMEM, VMEM),
         scratch_shapes=[dma((2,)), dma((2,)), dma, dma],
         compiler_params=pltpu.CompilerParams(
@@ -568,8 +603,8 @@
         in_specs=[SMEM, VMEM, VMEM, VMEM, VMEM, VMEM, VMEM],
         out_specs=(VMEM, VMEM),
         scratch_shapes=[
-            pltpu.VMEM((N, N), jnp.float32),
-            pltpu.VMEM((2, N, HALF), jnp.float32),
+            pltpu.VMEM((2, N, N), jnp.float32),
+            pltpu.VMEM((2, 2, N, HALF), jnp.float32),
         ],
         compiler_params=pltpu.CompilerParams(vmem_limit_bytes=30 << 20),
     )(plan, tile, other, received, measured, probe, table)

time: 79 us -> 77.8 us (0.985)
  local copies, waits for them, and re-layouts: 4.1 us -> 2.89 us
    pallas_call x1, Pallas kernels: 2.44 us -> 3.73 us  [shards(): pl.pallas_call(pack_kernel, name='pack', out_shape=(jax.ShapeDtypeStruct(...]
    unnamed x10 -> x12, local copies, waits for them, and re-layouts: 4.1 us -> 2.89 us
    pallas_call x1, Pallas kernels: 26.4 us -> 25.5 us  [shards(): pl.pallas_call(functools.partial(return_kernel, n_lat), name='giveback',...]
where the time goes in v4:
time: 77.8 us; the launch traced here: 77.6 us
  Pallas kernels  74 us (95%)
  local copies, waits for them, and re-layouts  2.89 us (4%)
    pallas_call x1, Pallas kernels, shards(): pl.pallas_call(functools.partial(return_kernel, n_lat), name='giveback',...  25.5 us
    pallas_call x1, Pallas kernels, shards(): pl.pallas_call(functools.partial(exchange_kernel, n_lat), name='exchange'...  24.8 us
    pallas_call x1, Pallas kernels, shards(): pl.pallas_call(functools.partial(announce_kernel, n_lat), name='announce'...  11.2 us
    pallas_call x1, Pallas kernels, shards(): pl.pallas_call(compute_kernel, name='compute', out_shape=(shape(2, 2, ROW...  4.55 us
    pallas_call x1, Pallas kernels, shards(): pl.pallas_call(gather_kernel, name='gather', out_shape=shape(2, N, column...  4.14 us
    pallas_call x1, Pallas kernels, shards(): pl.pallas_call(pack_kernel, name='pack', out_shape=(jax.ShapeDtypeStruct(...  3.73 us
    unnamed x12, local copies, waits for them, and re-layouts  2.89 us

profile of v4, /device:TPU:1, one launch (start us, length us, event | category | flops | bytes accessed | tf_op | source)
XLA Modules:
  0.0 77.6 jit_solution(12126762290683495507)
XLA Ops:
  0.7 11.2 %announce.1 = (s32[2,4]{1,0:T(2,128)}, s32[1]{0:T(128)}) custom-call(s32[2,4]{1,0:T(2,128)} %bitcast.6, s32[1]{0:T(128)S(6)} %copy.7.cnt), custom_call_target="tpu_custom_call" | custom-call | tf_op jit(solution)/shard_map/announce/pallas_call | solution.py:555
  11.9 0.0 copy-start
  11.9 0.0 copy-start.1
  11.9 1.4 %copy-done.1 = f32[4,256,256]{2,1,0:T(8,128)S(1)} copy-done((f32[4,256,256]{2,1,0:T(8,128)S(1)}, f32[4,256,256]{2,1,0:T(8,128)}, u32[]{:S(2)}) %copy-start.1) | copy-done | bytes 1048600
  13.3 0.0 copy-start.4
  13.3 0.9 %copy-done.4 = s32[4,2]{0,1:T(2,128)S(1)} copy-done((s32[4,2]{0,1:T(2,128)S(1)}, s32[4,2]{0,1:T(2,128)}, u32[]{:S(2)}) %copy-start.4) | copy-done | bytes 56
  14.2 0.0 copy-start.5
  14.2 0.6 copy-done.5
  14.8 3.7 %pack.1 = (s32[80]{0:T(128)S(1)}, f32[2,384,256]{2,1,0:T(8,128)S(1)}, f32[2,384,256]{2,1,0:T(8,128)S(1)}) custom-call(s32[2,4]{1,0:T(2,128)S(1)} %bitcast.7, s32[1]{0:T(128)S(6)} %copy.7.cnt, s32[2,4]{1,0:T(2,128)S(1)} %copy-done.5, s32[1]{0:T(128)} %get-tuple-element.17.prev_cnt, f32[2,256,2048]{2,1,0:T(8,128)} %bitcast.3, f32[4,256,256]{2,1,0:T(8,128)S(1)} %copy-done.1), custom_call_target="tpu_custom_call" | custom-call | tf_op jit(solution)/shard_map/pack/pallas_call | solution.py:567
  18.5 0.0 copy-start.2
  18.5 0.0 copy-start.3
  18.6 0.0 copy-done
  18.6 24.8 %exchange.1 = (f32[2,2,896,256]{3,2,1,0:T(8,128)S(1)}, f32[2,256,2048]{2,1,0:T(8,128)S(1)}) custom-call(f32[2,384,256]{2,1,0:T(8,128)S(1)} %get-tuple-element.19.ahead, f32[2,384,256]{2,1,0:T(8,128)S(1)} %get-tuple-element.20.behind, f32[2,256,2048]{2,1,0:T(8,128)S(1)} %bitcast.4), custom_call_target="tpu_custom_call" | custom-call | tf_op jit(solution)/shard_map/exchange/pallas_call | solution.py:586
  43.4 0.0 copy-done.2
  43.4 0.0 copy-done.3
  43.4 4.6 %compute.1 = (f32[2,2,384,256]{3,2,1,0:T(8,128)S(1)}, f32[2,3,2,256,256]{4,3,2,1,0:T(8,128)S(1)}) custom-call(s32[80]{0:T(128)S(1)} %get-tuple-element.18.plan, f32[2,256,2048]{2,1,0:T(8,128)S(1)} %bitcast.5, f32[2,256,2048]{2,1,0:T(8,128)S(1)} %get-tuple-element.21.other, f32[2,2,896,256]{3,2,1,0:T(8,128)S(1)} %get-tuple-element.22.received, ...), custom_call_target="tpu_custom_call" | custom-call | tf_op jit(solution)/shard_map/compute/pallas_call | solution.py:599
  48.0 25.5 %giveback.1 = (f32[2,2,384,256]{3,2,1,0:T(8,128)S(1)}, f32[3,2,256,256]{3,2,1,0:T(8,128)S(1)}) custom-call(f32[2,2,384,256]{3,2,1,0:T(8,128)S(1)} %get-tuple-element.23.rows, f32[2,3,2,256,256]{4,3,2,1,0:T(8,128)S(1)} %get-tuple-element.24.windows.grads), custom_call_target="tpu_custom_call" | custom-call | tf_op jit(solution)/shard_map/giveback/pallas_call | solution.py:612
  73.5 4.1 %gather.1 = f32[2,256,2048]{2,1,0:T(8,128)} custom-call(s32[80]{0:T(128)S(1)} %get-tuple-element.18.plan, f32[2,2,384,256]{3,2,1,0:T(8,128)S(1)} %get-tuple-element.25.rows, f32[3,2,256,256]{3,2,1,0:T(8,128)S(1)} %get-tuple-element.26.partner, f32[2,3,2,256,256]{4,3,2,1,0:T(8,128)S(1)} %get-tuple-element.24.windows.grads), custom_call_target="tpu_custom_call" | custom-call | tf_op jit(solution)/shard_map/gather/pallas_call | solution.py:624
Async XLA Ops:
  11.9 6.7 %copy-start = (f32[1,2,256,2048]{3,2,1,0:T(8,128)S(1)}, f32[1,2,256,2048]{3,2,1,0:T(8,128)}, u32[]{:S(2)}) copy-start(f32[1,2,256,2048]{3,2,1,0:T(8,128)} %param.6) | copy-start | bytes 12582916
  11.9 1.4 %copy-start.1 = (f32[4,256,256]{2,1,0:T(8,128)S(1)}, f32[4,256,256]{2,1,0:T(8,128)}, u32[]{:S(2)}) copy-start(f32[4,256,256]{2,1,0:T(8,128)} %measured.1) | copy-start | bytes 3145732
  13.3 0.9 %copy-start.4 = (s32[4,2]{0,1:T(2,128)S(1)}, s32[4,2]{0,1:T(2,128)}, u32[]{:S(2)}) copy-start(s32[4,2]{0,1:T(2,128)} %param.9) | copy-start | bytes 100
  14.2 0.6 copy-start.5
  18.5 24.9 %copy-start.2 = (bf16[8,2,256,256]{3,2,1,0:T(8,128)(2,1)S(1)}, bf16[8,2,256,256]{3,2,1,0:T(8,128)(2,1)}, u32[]{:S(2)}) copy-start(bf16[8,2,256,256]{3,2,1,0:T(8,128)(2,1)} %constant.2.clone.table) | copy-start | bytes 6291460
  18.5 24.9 %copy-start.3 = (f32[2,256,256]{2,1,0:T(8,128)S(1)}, f32[2,256,256]{2,1,0:T(8,128)}, u32[]{:S(2)}) copy-start(f32[2,256,256]{2,1,0:T(8,128)} %probe.1) | copy-start | bytes 1572868

commit v5 on v4

--- a/solution.py
+++ b/solution.py
@@ -16,6 +16,10 @@
 BUDGET = 48
 ROWS = 8 * BUDGET
 PAD = 256
+CHUNK = 32
+EASY = 30
+RETURN_BUDGETS = tuple(range(30, 49, 3))
+RETURN_BUDGETS = (32, 36, 40, 44, 48)
 SPAN = 20
 
 
@@ -60,9 +64,10 @@
         cost_left = sum(lefts, jnp.int32(0))
         cost_right = sum([down[i] + 8 for i in range(4) if right[i]], jnp.int32(0))
         widest = jnp.maximum(cost_left, cost_right)
+        back = jnp.maximum(cost_left, cost_right - 8 * n_right)
         most = jnp.maximum(live - n_right, n_right)
         bad = (live < top) | (widest > BUDGET) | (most > MAX_JOBS)
-        key = most * 64 + widest + jnp.where(bad, jnp.int32(1 << 16), 0)
+        key = jnp.maximum(back, EASY) * 8 + most + jnp.where(bad, jnp.int32(1 << 16), 0)
         pick = jnp.where(key < best, mask, pick)
         best = jnp.minimum(key, best)
     blocks = [jnp.minimum(lax.div(cols_of[i], N), 6) for i in range(4)]
@@ -109,7 +114,7 @@
 
 
 def pack_kernel(
-    pos_hbm, cnt, prev_pos_hbm, prev_cnt, tile_hbm, measured_hbm, plan, ahead, behind,
+    pos_hbm, cnt, prev_pos_hbm, prev_cnt, tile_hbm, measured_hbm, plan, packed, need,
     tile, measured, pos, prev_pos, sems,
 ):
     depth = lax.axis_index("depth")
@@ -130,71 +135,113 @@
     for k, side in enumerate(own + prev):
         for w, word in enumerate(side):
             plan[k * SPAN + w] = word
+    need[...] = jnp.full(need.shape, jnp.maximum(own[0][1], own[1][1]), jnp.int32)
     for load in loads[2:]:
         load.wait()
 
-    def copy_rows(out, at, j, first, count):
+    def copy_rows(way, at, j, first, count):
         start = plan[at + 2 + 5 * j + 3]
         low = pl.multiple_of(plan[at + 2 + 5 * j + 1] * N, N)
         high = pl.multiple_of(plan[at + 2 + 5 * j + 1] * N + N, N)
         keep = lanes() >= plan[at + 2 + 5 * j + 2]
 
         def step(g, carry):
-            src = pl.multiple_of((first + g) * 8, 8)
-            dst = pl.multiple_of((start + g) * 8, 8)
-            for c in range(2):
-                out[c, pl.ds(dst, 8), :] = jnp.where(
-                    keep, tile[c, pl.ds(src, 8), pl.ds(low, N)], tile[c, pl.ds(src, 8), pl.ds(high, N)]
-                )
+            for k in range(4):
+                at_row = jnp.minimum(4 * g + k, count - 1)
+                src = pl.multiple_of((first + at_row) * 8, 8)
+                dst = pl.multiple_of((start + at_row) * 8, 8)
+                for c in range(2):
+                    packed[way, c, pl.ds(dst, 8), :] = jnp.where(
+                        keep,
+                        tile[c, pl.ds(src, 8), pl.ds(low, N)],
+                        tile[c, pl.ds(src, 8), pl.ds(high, N)],
+                    )
             return carry
 
-        lax.fori_loop(0, count, step, 0)
+        lax.fori_loop(0, lax.div(count + 3, 4), step, 0)
 
     def right_job(j, carry):
         first = lax.div(plan[OWN_RIGHT + 2 + 5 * j], 8)
-        copy_rows(ahead, OWN_RIGHT, j, first, 32 - first)
+        copy_rows(0, OWN_RIGHT, j, first, 32 - first)
         slot = plan[OWN_RIGHT + 2 + 5 * j + 4]
         dst = pl.multiple_of((plan[OWN_RIGHT + 1] + 8 * j) * 8, 8)
         for c in range(2):
             src = pl.multiple_of(depth * HALF + 64 * c, 64)
-            ahead[c, pl.ds(dst, 64), :] = measured[slot, pl.ds(src, 64), :]
+            packed[0, c, pl.ds(dst, 64), :] = measured[slot, pl.ds(src, 64), :]
         return carry
 
     lax.fori_loop(0, plan[OWN_RIGHT], right_job, 0)
 
     def left_job(j, carry):
-        copy_rows(behind, PREV_LEFT, j, 0, lax.div(plan[PREV_LEFT + 2 + 5 * j] + 7, 8))
+        copy_rows(1, PREV_LEFT, j, 0, lax.div(plan[PREV_LEFT + 2 + 5 * j] + 7, 8))
         return carry
 
     lax.fori_loop(0, plan[PREV_LEFT], left_job, 0)
 
 
 def exchange_kernel(
-    n_lat, ahead, behind, tile, received, other,
-    row_send, row_recv, tile_send, tile_recv,
+    n_lat, packed, tile, need, received, other, bucket,
+    mine, theirs, row_send, row_recv, tile_send, tile_recv, need_send, need_recv,
 ):
     depth = lax.axis_index("depth")
     lat = lax.axis_index("lat")
     after = lax.rem(lat + 1, n_lat)
     before = lax.rem(lat + n_lat - 1, n_lat)
     greet(depth, lat, after, before)
-    pl.semaphore_wait(pltpu.get_barrier_semaphore(), 4)
+    barrier = pltpu.get_barrier_semaphore()
+    rings = []
+    for unit in (1, 4, 16):
+        digit = lax.rem(lax.div(lat, unit), 4)
+        rings.append([lat + (lax.rem(digit + k, 4) - digit) * unit for k in range(1, 4)])
+    for ring in rings:
+        for mate in ring:
+            pl.semaphore_signal(
+                barrier, inc=1, device_id=(depth, mate), device_id_type=pl.DeviceIdType.MESH
+            )
+    pl.semaphore_wait(barrier, 13)
 
     def slot(s):
         return received.at[s, :, pl.ds(PAD, ROWS), :]
 
+    def tell(turn):
+        copies = [
+            remote(
+                mine.at[turn], theirs.at[turn, k], need_send.at[turn, k], need_recv.at[turn, k],
+                depth, mate,
+            )
+            for k, mate in enumerate(rings[turn])
+        ]
+        for copy in copies:
+            copy.start()
+        return copies
+
+    mine[0] = need[...]
+    told = tell(0)
     sends = [
-        remote(ahead, slot(depth), row_send.at[0], row_recv.at[depth], 1, after),
-        remote(behind, slot(depth), row_send.at[1], row_recv.at[depth], 0, before),
+        remote(packed.at[0], slot(depth), row_send.at[0], row_recv.at[depth], 1, after),
+        remote(packed.at[1], slot(depth), row_send.at[1], row_recv.at[depth], 0, before),
     ]
     for copy in sends:
         copy.start()
     swap = remote(tile, other, tile_send, tile_recv, 1 - depth, lat)
     swap.start()
+    for turn in range(3):
+        for copy in told:
+            copy.wait()
+        top = mine[turn]
+        for k in range(3):
+            top = jnp.maximum(top, theirs[turn, k])
+        if turn < 2:
+            mine[turn + 1] = top
+            told = tell(turn + 1)
+    place = jnp.zeros_like(top)
+    for budget in RETURN_BUDGETS[:-1]:
+        place = place + jnp.where(top > budget, 1, 0)
+    bucket[...] = place
     for copy in sends:
         copy.wait_send()
     for s in range(2):
-        remote(ahead, slot(s), row_send.at[0], row_recv.at[s], 1, after).wait_recv()
+        remote(packed.at[0], slot(s), row_send.at[0], row_recv.at[s], 1, after).wait_recv()
     swap.wait()
 
 
@@ -224,7 +271,7 @@
 
 
 def return_kernel(
-    n_lat, rows, windows, received, partner,
+    n_lat, count, rows, windows, received, partner,
     row_send, row_recv, swap_send, swap_recv,
 ):
     depth = lax.axis_index("depth")
@@ -234,8 +281,15 @@
     greet(depth, lat, after, before)
     pl.semaphore_wait(pltpu.get_barrier_semaphore(), 4)
     target = jnp.where(depth == 0, after, before)
+
+    def part(c):
+        return received.at[c, :, pl.ds(CHUNK, count), :]
+
+    def sent(s):
+        return rows.at[s, :, pl.ds(0, count), :]
+
     sends = [
-        remote(rows.at[s], received.at[depth], row_send.at[s], row_recv.at[depth], s, target)
+        remote(sent(s), part(depth), row_send.at[s], row_recv.at[depth], s, target)
         for s in range(2)
     ]
     for copy in sends:
@@ -246,7 +300,7 @@
         copy.wait_send()
     for c in range(2):
         remote(
-            rows.at[0], received.at[c], row_send.at[0], row_recv.at[c], 0, target
+            sent(0), part(c), row_send.at[0], row_recv.at[c], 0, target
         ).wait_recv()
     swap.wait()
 
@@ -353,13 +407,14 @@
 
 
 def compute_kernel(
-    plan, tile, other, received, measured, probe, table,
-    rows_out, grads,
+    plan, bucket, tile, other, received, measured, probe, table,
+    rows_out, grads, choice,
     amplitude, spread,
 ):
     depth = lax.axis_index("depth")
     at = jnp.where(depth == 0, OWN_LEFT, PREV_RIGHT)
     jobs = plan[at]
+    choice[0] = bucket[0, 0]
     row = lax.broadcasted_iota(jnp.int32, (N, N), 0)
     lane = lax.broadcasted_iota(jnp.int32, (N, N), 1)
     order = jnp.where(lane < HALF, 2 * lane, 2 * lane - (N - 1))
@@ -454,17 +509,19 @@
             base = base_of(k)
             count = jnp.where(depth == 0, lax.div(r + 7, 8), 32 - lax.div(r, 8))
 
-            def step(g, carry, k=k, base=base, start=start):
-                src = pl.multiple_of((base + g) * 8, 8)
-                dst = pl.multiple_of((start + g) * 8, 8)
-                for s in range(2):
-                    for c in range(2):
-                        rows_out[s, c, pl.ds(dst, 8), :] = grads[
-                            s, numbers[k], c, pl.ds(src, 8), :
-                        ]
+            def step(g, carry, k=k, base=base, start=start, count=count):
+                for q in range(2):
+                    at_row = jnp.minimum(2 * g + q, count - 1)
+                    src = pl.multiple_of((base + at_row) * 8, 8)
+                    dst = pl.multiple_of((start + at_row) * 8, 8)
+                    for s in range(2):
+                        for c in range(2):
+                            rows_out[s, c, pl.ds(dst, 8), :] = grads[
+                                s, numbers[k], c, pl.ds(src, 8), :
+                            ]
                 return carry
 
-            lax.fori_loop(0, count, step, 0)
+            lax.fori_loop(0, lax.div(count + 1, 2), step, 0)
 
     @pl.when(jobs >= 2)
     def _():
@@ -475,8 +532,16 @@
         work([jobs - 1])
 
 
-def gather_kernel(plan, rows, partner, grads, out, tile, out_sems):
+def gather_kernel(
+    plan, rows_hbm, partner_hbm, grads, out, tile, rows, partner, in_sems, out_sems
+):
     depth = lax.axis_index("depth")
+    loads = [
+        pltpu.make_async_copy(rows_hbm, rows, in_sems.at[0]),
+        pltpu.make_async_copy(partner_hbm, partner, in_sems.at[1]),
+    ]
+    for load in loads:
+        load.start()
 
     def clear(i, carry):
         at = pl.multiple_of(i * 8, 8)
@@ -485,29 +550,35 @@
         return carry
 
     lax.fori_loop(0, N // 8, clear, 0)
-    row = lax.broadcasted_iota(jnp.int32, (8, N), 0)
+    for load in loads:
+        load.wait()
+    row = lax.broadcasted_iota(jnp.int32, (CHUNK, N), 0)
+    lane = lax.broadcasted_iota(jnp.int32, (CHUNK, N), 1)
 
     def add(at, j, c, lower, packed, near):
         r = plan[at + 2 + 5 * j]
         block = plan[at + 2 + 5 * j + 1]
         start = plan[at + 2 + 5 * j + 3]
-        first = 0 if lower else lax.div(r, 8)
-        last = lax.div(r + 7, 8) if lower else 32
-        keep = lanes() >= plan[at + 2 + 5 * j + 2]
+        first = 0 if lower else lax.div(r, CHUNK)
+        last = lax.div(r + CHUNK - 1, CHUNK) if lower else N // CHUNK
+        skip = 0 if lower else lax.div(r, 8)
+        keep = lane >= plan[at + 2 + 5 * j + 2]
         low = pl.multiple_of(block * N, N)
         high = pl.multiple_of(block * N + N, N)
 
         def step(g, carry):
-            dst = pl.multiple_of(g * 8, 8)
+            dst = pl.multiple_of(g * CHUNK, CHUNK)
             inside = (row + dst < r) if lower else (row + dst >= r)
             if packed:
-                src = pl.multiple_of((start + g - first) * 8, 8)
-                value = rows[0 if lower else 1, c, pl.ds(src, 8), :]
+                src = pl.multiple_of(CHUNK + (start - skip) * 8 + g * CHUNK, 8)
+                value = rows[0 if lower else 1, c, pl.ds(src, CHUNK), :]
+            elif near:
+                value = grads[depth, j, c, pl.ds(dst, CHUNK), :]
             else:
-                value = grads[depth, j, c, pl.ds(dst, 8), :] if near else partner[j, c, pl.ds(dst, 8), :]
+                value = partner[j, c, pl.ds(dst, CHUNK), :]
             value = jnp.where(inside, value, 0.0)
-            tile[c, pl.ds(dst, 8), pl.ds(low, N)] += jnp.where(keep, value, 0.0)
-            tile[c, pl.ds(dst, 8), pl.ds(high, N)] += jnp.where(keep, 0.0, value)
+            tile[c, pl.ds(dst, CHUNK), pl.ds(low, N)] += jnp.where(keep, value, 0.0)
+            tile[c, pl.ds(dst, CHUNK), pl.ds(high, N)] += jnp.where(keep, 0.0, value)
             return carry
 
         lax.fori_loop(first, last, step, 0)
@@ -564,13 +635,13 @@
         scratch_shapes=[dma((2,)), dma((2,))],
         compiler_params=pltpu.CompilerParams(collective_id=2, has_side_effects=True),
     )(positions, counts)
-    plan, ahead, behind = pl.pallas_call(
+    plan, packed, need = pl.pallas_call(
         pack_kernel,
         name="pack",
         out_shape=(
             jax.ShapeDtypeStruct((4 * SPAN,), jnp.int32),
-            shape(2, ROWS, N),
-            shape(2, ROWS, N),
+            shape(2, 2, ROWS, N),
+            jax.ShapeDtypeStruct((8, 128), jnp.int32),
         ),
         in_specs=[HBM, SMEM, HBM, SMEM, HBM, HBM],
         out_specs=(SMEM, VMEM, VMEM),
@@ -583,51 +654,75 @@
         ],
         compiler_params=pltpu.CompilerParams(vmem_limit_bytes=51 << 20),
     )(positions, counts, prev_positions, prev_counts, tile, measured)
-    received, other = pl.pallas_call(
+    received, other, bucket = pl.pallas_call(
         functools.partial(exchange_kernel, n_lat),
         name="exchange",
-        out_shape=(shape(2, 2, ROWS + 2 * PAD, N), shape(2, N, columns)),
-        in_specs=[VMEM, VMEM, HBM],
-        out_specs=(VMEM, VMEM),
-        scratch_shapes=[dma((2,)), dma((2,)), dma, dma],
+        out_shape=(
+            shape(2, 2, ROWS + 2 * PAD, N),
+            shape(2, N, columns),
+            jax.ShapeDtypeStruct((8, 128), jnp.int32),
+        ),
+        in_specs=[VMEM, HBM, VMEM],
+        out_specs=(VMEM, VMEM, VMEM),
+        scratch_shapes=[
+            pltpu.VMEM((3, 8, 128), jnp.int32),
+            pltpu.VMEM((3, 3, 8, 128), jnp.int32),
+            dma((2,)), dma((2,)), dma, dma, dma((3, 3)), dma((3, 3)),
+        ],
         compiler_params=pltpu.CompilerParams(
             collective_id=0, has_side_effects=True, vmem_limit_bytes=12 << 20
         ),
-    )(ahead, behind, tile)
+    )(packed, tile, need)
 
     table = jnp.asarray(tables())
-    rows_out, grads = pl.pallas_call(
+    rows_out, grads, choice = pl.pallas_call(
         compute_kernel,
         name="compute",
-        out_shape=(shape(2, 2, ROWS, N), shape(2, MAX_JOBS, 2, N, N)),
-        in_specs=[SMEM, VMEM, VMEM, VMEM, VMEM, VMEM, VMEM],
-        out_specs=(VMEM, VMEM),
+        out_shape=(
+            shape(2, 2, ROWS, N),
+            shape(2, MAX_JOBS, 2, N, N),
+            jax.ShapeDtypeStruct((1,), jnp.int32),
+        ),
+        in_specs=[SMEM, SMEM, VMEM, VMEM, VMEM, VMEM, VMEM, VMEM],
+        out_specs=(VMEM, VMEM, SMEM),
         scratch_shapes=[
             pltpu.VMEM((2, N, N), jnp.float32),
             pltpu.VMEM((2, 2, N, HALF), jnp.float32),
         ],
         compiler_params=pltpu.CompilerParams(vmem_limit_bytes=30 << 20),
-    )(plan, tile, other, received, measured, probe, table)
-
-    rows_back, partner = pl.pallas_call(
-        functools.partial(return_kernel, n_lat),
-        name="giveback",
-        out_shape=(shape(2, 2, ROWS, N), shape(MAX_JOBS, 2, N, N)),
-        in_specs=[VMEM, VMEM],
-        out_specs=(VMEM, VMEM),
-        scratch_shapes=[dma((2,)), dma((2,)), dma, dma],
-        compiler_params=pltpu.CompilerParams(
-            collective_id=1, has_side_effects=True, vmem_limit_bytes=12 << 20
-        ),
-    )(rows_out, grads)
+    )(plan, bucket, tile, other, received, measured, probe, table)
+
+    def give_back(budget):
+        return pl.pallas_call(
+            functools.partial(return_kernel, n_lat, 8 * budget),
+            name="giveback%d" % budget,
+            out_shape=(shape(2, 2, ROWS + 2 * CHUNK, N), shape(MAX_JOBS, 2, N, N)),
+            in_specs=[VMEM, VMEM],
+            out_specs=(VMEM, VMEM),
+            scratch_shapes=[dma((2,)), dma((2,)), dma, dma],
+            compiler_params=pltpu.CompilerParams(
+                collective_id=3 + RETURN_BUDGETS.index(budget),
+                has_side_effects=True,
+                vmem_limit_bytes=12 << 20,
+            ),
+        )
+
+    rows_back, partner = lax.switch(
+        choice[0], [give_back(b) for b in RETURN_BUDGETS], rows_out, grads
+    )
 
     out = pl.pallas_call(
         gather_kernel,
         name="gather",
         out_shape=shape(2, N, columns),
-        in_specs=[SMEM, VMEM, VMEM, VMEM],
+        in_specs=[SMEM, HBM, HBM, VMEM],
         out_specs=HBM,
-        scratch_shapes=[pltpu.VMEM((2, N, columns), jnp.float32), dma((2,))],
+        scratch_shapes=[
+            pltpu.VMEM((2, N, columns), jnp.float32),
+            pltpu.VMEM((2, 2, ROWS + 2 * CHUNK, N), jnp.float32),
+            pltpu.VMEM((MAX_JOBS, 2, N, N), jnp.float32),
+            dma((2,)), dma((2,)),
+        ],
         compiler_params=pltpu.CompilerParams(vmem_limit_bytes=20 << 20),
     )(plan, rows_back, partner, grads)
     return out.reshape(object_slices.shape)

time: 77.8 us -> 77.8 us (level)
    pallas_call x1, Pallas kernels: 25.5 us -> 23.3 us  [shards(): lax.switch(choice[0], [give_back(b) for b in RETURN_BUDGETS], rows_out, g...]
where the time goes in v5:
time: 77.8 us; the launch traced here: 77.6 us
  Pallas kernels  73.7 us (95%)
  local copies, waits for them, and re-layouts  2.53 us (3%)
  between operations  1.39 us (2%)
    pallas_call x1, Pallas kernels, shards(): pl.pallas_call(functools.partial(exchange_kernel, n_lat), name='exchange'...  25.3 us
    pallas_call x1, Pallas kernels, shards(): lax.switch(choice[0], [give_back(b) for b in RETURN_BUDGETS], rows_out, g...  23.3 us
    pallas_call x1, Pallas kernels, shards(): pl.pallas_call(functools.partial(announce_kernel, n_lat), name='announce'...  11.1 us
    pallas_call x1, Pallas kernels, shards(): pl.pallas_call(compute_kernel, name='compute', out_shape=(shape(2, 2, ROW...  5.18 us
    pallas_call x1, Pallas kernels, shards(): pl.pallas_call(gather_kernel, name='gather', out_shape=shape(2, N, column...  4.84 us
    pallas_call x1, Pallas kernels, shards(): pl.pallas_call(pack_kernel, name='pack', out_shape=(jax.ShapeDtypeStruct(...  3.94 us
    unnamed x12, local copies, waits for them, and re-layouts  2.53 us

profile of v5, /device:TPU:1, one launch (start us, length us, event | category | flops | bytes accessed | tf_op | source)
XLA Modules:
  0.0 77.6 jit_solution(14259974126994315278)
XLA Ops:
  0.7 11.1 %announce.1 = (s32[2,4]{1,0:T(2,128)}, s32[1]{0:T(128)}) custom-call(s32[2,4]{1,0:T(2,128)} %bitcast.7, s32[1]{0:T(128)S(6)} %copy.17.cnt), custom_call_target="tpu_custom_call" | custom-call | tf_op jit(solution)/shard_map/announce/pallas_call | solution.py:626
  11.7 0.0 copy-start.1
  11.8 1.2 %copy-done.1 = f32[4,256,256]{2,1,0:T(8,128)S(1)} copy-done((f32[4,256,256]{2,1,0:T(8,128)S(1)}, f32[4,256,256]{2,1,0:T(8,128)}, u32[]{:S(2)}) %copy-start.1) | copy-done | bytes 1048600
  13.0 0.0 copy-start.4
  13.0 0.7 copy-done.4
  13.7 0.0 copy-start.5
  13.7 0.6 copy-done.5
  14.3 0.0 copy-start
  14.3 3.9 %pack.1 = (s32[80]{0:T(128)S(1)}, f32[2,2,384,256]{3,2,1,0:T(8,128)S(1)}, s32[8,128]{1,0:T(8,128)S(1)}) custom-call(s32[2,4]{1,0:T(2,128)S(1)} %bitcast.8, s32[1]{0:T(128)S(6)} %copy.17.cnt, s32[2,4]{1,0:T(2,128)S(1)} %copy-done.5, s32[1]{0:T(128)} %get-tuple-element.49.prev_cnt, f32[2,256,2048]{2,1,0:T(8,128)} %bitcast.4, f32[4,256,256]{2,1,0:T(8,128)S(1)} %copy-done.1), custom_call_target="tpu_custom_call" | custom-call | tf_op jit(solution)/shard_map/pack/pallas_call | solution.py:638
  18.2 0.0 copy-done
  18.2 0.0 copy-start.2
  18.2 0.0 copy-start.3
  18.3 25.3 %exchange.1 = (f32[2,2,896,256]{3,2,1,0:T(8,128)S(1)}, f32[2,256,2048]{2,1,0:T(8,128)S(1)}, s32[8,128]{1,0:T(8,128)S(1)}) custom-call(f32[2,2,384,256]{3,2,1,0:T(8,128)S(1)} %get-tuple-element.51.packed, f32[2,256,2048]{2,1,0:T(8,128)S(1)} %bitcast.5, s32[8,128]{1,0:T(8,128)S(1)} %get-tuple-element.52.need), custom_call_target="tpu_custom_call" | custom-call | tf_op jit(solution)/shard_map/exchange/pallas_call | solution.py:657
  43.5 0.0 copy-done.2
  43.6 0.0 copy-done.3
  43.6 5.2 %compute.1 = (f32[2,2,384,256]{3,2,1,0:T(8,128)S(1)}, f32[2,3,2,256,256]{4,3,2,1,0:T(8,128)S(1)}, s32[1]{0:T(128)}) custom-call(s32[80]{0:T(128)S(1)} %get-tuple-element.50.plan, s32[8,128]{1,0:T(8,128)S(1)} %get-tuple-element.53.bucket, f32[2,256,2048]{2,1,0:T(8,128)S(1)} %bitcast.6, f32[2,256,2048]{2,1,0:T(8,128)S(1)} %get-tuple-element.54.other, ...), custom_call_target="tpu_custom_call" | custom-call | tf_op jit(solution)/shard_map/compute/pallas_call | solution.py:678
  49.4 23.4 %conditional.1 = ((f32[2,2,448,256]{3,2,1,0:T(8,128)}, f32[3,2,256,256]{3,2,1,0:T(8,128)})) conditional(s32[]{:T(128)} %bitcast.2, (f32[2,2,384,256]{3,2,1,0:T(8,128)S(1)}, f32[2,3,2,256,256]{4,3,2,1,0:T(8,128)S(1)}) %tuple.20, (f32[2,2,384,256]{3,2,1,0:T(8,128)S(1)}, f32[2,3,2,256,256]{4,3,2,1,0:T(8,128)S(1)}) %tuple.20, ...), branch_computations={%region_0.0_spmd, %region_1.0_spmd, %region_2.0_spmd, %region_3.0_... | conditional | bytes 8 | solution.py:710
  49.4 23.3 %giveback36.1 = (f32[2,2,448,256]{3,2,1,0:T(8,128)}, f32[3,2,256,256]{3,2,1,0:T(8,128)}) custom-call(f32[2,2,384,256]{3,2,1,0:T(8,128)S(1)} %get-tuple-element.27.rows, f32[2,3,2,256,256]{4,3,2,1,0:T(8,128)S(1)} %get-tuple-element.28.windows), custom_call_target="tpu_custom_call" | custom-call | tf_op jit(solution)/shard_map/cond/branch_1_fun/giveback36/pallas_call | solution.py:710
  72.8 4.8 %gather.1 = f32[2,256,2048]{2,1,0:T(8,128)} custom-call(s32[80]{0:T(128)S(1)} %get-tuple-element.50.plan, f32[2,2,448,256]{3,2,1,0:T(8,128)} %get-tuple-element.59.rows_hbm, f32[3,2,256,256]{3,2,1,0:T(8,128)} %get-tuple-element.60.partner_hbm, f32[2,3,2,256,256]{4,3,2,1,0:T(8,128)S(1)} %get-tuple-element.58.grads), custom_call_target="tpu_custom_call" | custom-call | tf_op jit(solution)/shard_map/gather/pallas_call | solution.py:714
Async XLA Ops:
  11.7 1.2 %copy-start.1 = (f32[4,256,256]{2,1,0:T(8,128)S(1)}, f32[4,256,256]{2,1,0:T(8,128)}, u32[]{:S(2)}) copy-start(f32[4,256,256]{2,1,0:T(8,128)} %measured.1) | copy-start | bytes 3145732
  13.0 0.7 copy-start.4
  13.7 0.6 copy-start.5
  14.3 4.0 %copy-start = (f32[1,2,256,2048]{3,2,1,0:T(8,128)S(1)}, f32[1,2,256,2048]{3,2,1,0:T(8,128)}, u32[]{:S(2)}) copy-start(f32[1,2,256,2048]{3,2,1,0:T(8,128)} %param.11) | copy-start | bytes 12582916
  18.2 25.3 %copy-start.2 = (bf16[8,2,256,256]{3,2,1,0:T(8,128)(2,1)S(1)}, bf16[8,2,256,256]{3,2,1,0:T(8,128)(2,1)}, u32[]{:S(2)}) copy-start(bf16[8,2,256,256]{3,2,1,0:T(8,128)(2,1)} %constant.8.clone.table) | copy-start | bytes 6291460
  18.2 25.3 %copy-start.3 = (f32[2,256,256]{2,1,0:T(8,128)S(1)}, f32[2,256,256]{2,1,0:T(8,128)}, u32[]{:S(2)}) copy-start(f32[2,256,256]{2,1,0:T(8,128)} %probe.1) | copy-start | bytes 1572868

commit v6 on v4

--- a/solution.py
+++ b/solution.py
@@ -87,7 +87,11 @@
     return lax.broadcasted_iota(jnp.int32, (8, N), 1)
 
 
-def announce_kernel(n_lat, pos, cnt, prev_pos, prev_cnt, send, recv):
+def announce_kernel(
+    n_lat, pos_hbm, cnt, tile_hbm, measured_hbm,
+    pos, prev_pos, prev_cnt, tile, apart,
+    measured, spread, send, recv, local,
+):
     depth = lax.axis_index("depth")
     lat = lax.axis_index("lat")
     after = lax.rem(lat + 1, n_lat)
@@ -97,32 +101,47 @@
         pl.semaphore_signal(
             barrier, inc=1, device_id=(depth, other), device_id_type=pl.DeviceIdType.MESH
         )
+    loads = [
+        pltpu.make_async_copy(measured_hbm, measured, local.at[0]),
+        pltpu.make_async_copy(tile_hbm, tile, local.at[1]),
+        pltpu.make_async_copy(pos_hbm, pos, local.at[2]),
+    ]
+    for load in loads:
+        load.start()
     pl.semaphore_wait(barrier, 2)
     copies = [
-        remote(pos, prev_pos, send.at[0], recv.at[0], depth, after),
+        remote(pos_hbm, prev_pos, send.at[0], recv.at[0], depth, after),
         remote(cnt, prev_cnt, send.at[1], recv.at[1], depth, after),
     ]
     for copy in copies:
         copy.start()
+    row = lax.broadcasted_iota(jnp.int32, (N, N), 0)
+    lane = lax.broadcasted_iota(jnp.int32, (N, N), 1)
+    order = jnp.where(lane < HALF, 2 * lane, 2 * lane - (N - 1))
+    shuffle = jnp.where(row == order, 1.0, 0.0).astype(jnp.bfloat16)
+    loads[0].wait()
+    for slot in range(4):
+        hi, lo = halves(measured[slot])
+        columns = dot(
+            jnp.concatenate([hi, lo], axis=1), jnp.concatenate([shuffle, shuffle], axis=0)
+        )
+        for h in range(2):
+            spread[h] = columns[:, HALF * h : HALF * h + HALF]
+        for p in range(2):
+            for h in range(2):
+                apart[slot, HALF * p : HALF * p + HALF, HALF * h : HALF * h + HALF] = spread[
+                    h, pl.ds(p, HALF, stride=2), :
+                ]
+    for load in loads[1:]:
+        load.wait()
     for copy in copies:
         copy.wait()
 
 
 def pack_kernel(
-    pos_hbm, cnt, prev_pos_hbm, prev_cnt, tile_hbm, measured_hbm, plan, ahead, behind,
-    tile, measured, pos, prev_pos, sems,
+    pos, cnt, prev_pos, prev_cnt, tile, measured, plan, ahead, behind
 ):
     depth = lax.axis_index("depth")
-    loads = [
-        pltpu.make_async_copy(pos_hbm, pos, sems.at[0]),
-        pltpu.make_async_copy(prev_pos_hbm, prev_pos, sems.at[1]),
-        pltpu.make_async_copy(tile_hbm, tile, sems.at[2]),
-        pltpu.make_async_copy(measured_hbm, measured, sems.at[3]),
-    ]
-    for load in loads:
-        load.start()
-    for load in loads[:2]:
-        load.wait()
     own = choose_sides([pos[0, i] for i in range(4)], [pos[1, i] for i in range(4)], cnt[0])
     prev = choose_sides(
         [prev_pos[0, i] for i in range(4)], [prev_pos[1, i] for i in range(4)], prev_cnt[0]
@@ -130,8 +149,6 @@
     for k, side in enumerate(own + prev):
         for w, word in enumerate(side):
             plan[k * SPAN + w] = word
-    for load in loads[2:]:
-        load.wait()
 
     def copy_rows(out, at, j, first, count):
         start = plan[at + 2 + 5 * j + 3]
@@ -140,15 +157,19 @@
         keep = lanes() >= plan[at + 2 + 5 * j + 2]
 
         def step(g, carry):
-            src = pl.multiple_of((first + g) * 8, 8)
-            dst = pl.multiple_of((start + g) * 8, 8)
-            for c in range(2):
-                out[c, pl.ds(dst, 8), :] = jnp.where(
-                    keep, tile[c, pl.ds(src, 8), pl.ds(low, N)], tile[c, pl.ds(src, 8), pl.ds(high, N)]
-                )
+            for k in range(4):
+                granule = jnp.minimum(4 * g + k, count - 1)
+                src = pl.multiple_of((first + granule) * 8, 8)
+                dst = pl.multiple_of((start + granule) * 8, 8)
+                for c in range(2):
+                    out[c, pl.ds(dst, 8), :] = jnp.where(
+                        keep,
+                        tile[c, pl.ds(src, 8), pl.ds(low, N)],
+                        tile[c, pl.ds(src, 8), pl.ds(high, N)],
+                    )
             return carry
 
-        lax.fori_loop(0, count, step, 0)
+        lax.fori_loop(0, lax.div(count + 3, 4), step, 0)
 
     def right_job(j, carry):
         first = lax.div(plan[OWN_RIGHT + 2 + 5 * j], 8)
@@ -355,15 +376,13 @@
 def compute_kernel(
     plan, tile, other, received, measured, probe, table,
     rows_out, grads,
-    amplitude, spread,
+    amplitude,
 ):
     depth = lax.axis_index("depth")
     at = jnp.where(depth == 0, OWN_LEFT, PREV_RIGHT)
     jobs = plan[at]
     row = lax.broadcasted_iota(jnp.int32, (N, N), 0)
     lane = lax.broadcasted_iota(jnp.int32, (N, N), 1)
-    order = jnp.where(lane < HALF, 2 * lane, 2 * lane - (N - 1))
-    shuffle = jnp.where(row == order, 1.0, 0.0).astype(jnp.bfloat16)
 
     def work(numbers):
         each = range(len(numbers))
@@ -423,24 +442,8 @@
         spectra = to_spectrum([product(w, o) for w, o in zip(waves, slices)], table)
         backs = []
         for k in each:
-            hi, lo = halves(amplitude[k])
-            apart = dot(
-                jnp.concatenate([hi, lo], axis=1), jnp.concatenate([shuffle, shuffle], axis=0)
-            )
-            for h in range(2):
-                spread[k, h] = apart[:, HALF * h : HALF * h + HALF]
-        for k in each:
-            apart = jnp.concatenate(
-                [
-                    jnp.concatenate(
-                        [spread[k, h, pl.ds(p, HALF, stride=2), :] for h in range(2)], axis=1
-                    )
-                    for p in range(2)
-                ],
-                axis=0,
-            )
             re, im = spectra[k]
-            factor = 1.0 - apart * lax.rsqrt(re * re + im * im + 1.0)
+            factor = 1.0 - amplitude[k] * lax.rsqrt(re * re + im * im + 1.0)
             backs.append((re * factor, im * factor))
         backs = from_spectrum(backs, table)
         for k in each:
@@ -552,18 +555,27 @@
     tile = object_slices.reshape(object_slices.shape[1:])
     dma = pltpu.SemaphoreType.DMA
     positions = positions.T
-    prev_positions, prev_counts = pl.pallas_call(
+    positions, prev_positions, prev_counts, tile, measured = pl.pallas_call(
         functools.partial(announce_kernel, n_lat),
         name="announce",
         out_shape=(
             jax.ShapeDtypeStruct(positions.shape, jnp.int32),
+            jax.ShapeDtypeStruct(positions.shape, jnp.int32),
             jax.ShapeDtypeStruct(counts.shape, jnp.int32),
+            shape(*tile.shape),
+            shape(*measured.shape),
         ),
-        in_specs=[HBM, HBM],
-        out_specs=(HBM, HBM),
-        scratch_shapes=[dma((2,)), dma((2,))],
-        compiler_params=pltpu.CompilerParams(collective_id=2, has_side_effects=True),
-    )(positions, counts)
+        in_specs=[HBM, HBM, HBM, HBM],
+        out_specs=(VMEM, VMEM, VMEM, VMEM, VMEM),
+        scratch_shapes=[
+            pltpu.VMEM((4, N, N), jnp.float32),
+            pltpu.VMEM((2, N, HALF), jnp.float32),
+            dma((2,)), dma((2,)), dma((3,)),
+        ],
+        compiler_params=pltpu.CompilerParams(
+            collective_id=2, has_side_effects=True, vmem_limit_bytes=46 << 20
+        ),
+    )(positions, counts, tile, measured)
     plan, ahead, behind = pl.pallas_call(
         pack_kernel,
         name="pack",
@@ -572,22 +584,15 @@
             shape(2, ROWS, N),
             shape(2, ROWS, N),
         ),
-        in_specs=[HBM, SMEM, HBM, SMEM, HBM, HBM],
+        in_specs=[SMEM, SMEM, SMEM, SMEM, VMEM, VMEM],
         out_specs=(SMEM, VMEM, VMEM),
-        scratch_shapes=[
-            pltpu.VMEM((2, N, columns), jnp.float32),
-            pltpu.VMEM((4, N, N), jnp.float32),
-            pltpu.SMEM((2, 4), jnp.int32),
-            pltpu.SMEM((2, 4), jnp.int32),
-            dma((4,)),
-        ],
-        compiler_params=pltpu.CompilerParams(vmem_limit_bytes=51 << 20),
+        compiler_params=pltpu.CompilerParams(vmem_limit_bytes=4 << 20),
     )(positions, counts, prev_positions, prev_counts, tile, measured)
     received, other = pl.pallas_call(
         functools.partial(exchange_kernel, n_lat),
         name="exchange",
         out_shape=(shape(2, 2, ROWS + 2 * PAD, N), shape(2, N, columns)),
-        in_specs=[VMEM, VMEM, HBM],
+        in_specs=[VMEM, VMEM, VMEM],
         out_specs=(VMEM, VMEM),
         scratch_shapes=[dma((2,)), dma((2,)), dma, dma],
         compiler_params=pltpu.CompilerParams(
@@ -602,10 +607,7 @@
         out_shape=(shape(2, 2, ROWS, N), shape(2, MAX_JOBS, 2, N, N)),
         in_specs=[SMEM, VMEM, VMEM, VMEM, VMEM, VMEM, VMEM],
         out_specs=(VMEM, VMEM),
-        scratch_shapes=[
-            pltpu.VMEM((2, N, N), jnp.float32),
-            pltpu.VMEM((2, 2, N, HALF), jnp.float32),
-        ],
+        scratch_shapes=[pltpu.VMEM((2, N, N), jnp.float32)],
         compiler_params=pltpu.CompilerParams(vmem_limit_bytes=30 << 20),
     )(plan, tile, other, received, measured, probe, table)
 

time: 77.8 us -> 77.3 us (level)
  local copies, waits for them, and re-layouts: 2.89 us -> 1.91 us
    pallas_call x1, Pallas kernels: 3.73 us -> 2.48 us  [shards(): pl.pallas_call(pack_kernel, name='pack', out_shape=(jax.ShapeDtypeStruct(...]
    pallas_call x1, Pallas kernels: 4.55 us -> 5.77 us  [shards(): pl.pallas_call(compute_kernel, name='compute', out_shape=(shape(2, 2, ROW...]
    unnamed x12 -> x8, local copies, waits for them, and re-layouts: 2.89 us -> 1.91 us
where the time goes in v6:
time: 77.3 us; the launch traced here: 77.1 us
  Pallas kernels  74.4 us (96%)
  local copies, waits for them, and re-layouts  1.91 us (2%)
    pallas_call x1, Pallas kernels, shards(): pl.pallas_call(functools.partial(return_kernel, n_lat), name='giveback',...  25.5 us
    pallas_call x1, Pallas kernels, shards(): pl.pallas_call(functools.partial(exchange_kernel, n_lat), name='exchange'...  24.8 us
    pallas_call x1, Pallas kernels, shards(): pl.pallas_call(functools.partial(announce_kernel, n_lat), name='announce'...  11.4 us
    pallas_call x1, Pallas kernels, shards(): pl.pallas_call(compute_kernel, name='compute', out_shape=(shape(2, 2, ROW...  5.77 us
    pallas_call x1, Pallas kernels, shards(): pl.pallas_call(gather_kernel, name='gather', out_shape=shape(2, N, column...  4.44 us
    pallas_call x1, Pallas kernels, shards(): pl.pallas_call(pack_kernel, name='pack', out_shape=(jax.ShapeDtypeStruct(...  2.48 us
    unnamed x8, local copies, waits for them, and re-layouts  1.91 us

profile of v6, /device:TPU:1, one launch (start us, length us, event | category | flops | bytes accessed | tf_op | source)
XLA Modules:
  0.0 77.1 jit_solution(16153163343350439020)
XLA Ops:
  0.7 0.0 copy-start.1
  0.7 1.2 %copy-done.1 = f32[4,256,256]{2,1,0:T(8,128)S(1)} copy-done((f32[4,256,256]{2,1,0:T(8,128)S(1)}, f32[4,256,256]{2,1,0:T(8,128)}, u32[]{:S(2)}) %copy-start.1) | copy-done | bytes 1048600
  1.9 0.0 copy-start.3
  1.9 0.7 copy-done.3
  2.6 11.4 %announce.1 = (s32[2,4]{1,0:T(2,128)S(1)}, s32[2,4]{1,0:T(2,128)S(1)}, s32[1]{0:T(128)}, f32[2,256,2048]{2,1,0:T(8,128)S(1)}, f32[4,256,256]{2,1,0:T(8,128)S(1)}) custom-call(s32[2,4]{1,0:T(2,128)S(1)} %bitcast.3, s32[1]{0:T(128)S(6)} %copy.7.cnt, f32[2,256,2048]{2,1,0:T(8,128)} %bitcast.4, f32[4,256,256]{2,1,0:T(8,128)S(1)} %copy-done.1), custom_call_target="tpu_custom_call" | custom-call | tf_op jit(solution)/shard_map/announce/pallas_call | solution.py:558
  14.0 2.5 %pack.1 = (s32[80]{0:T(128)S(1)}, f32[2,384,256]{2,1,0:T(8,128)S(1)}, f32[2,384,256]{2,1,0:T(8,128)S(1)}) custom-call(s32[2,4]{1,0:T(2,128)S(1)} %get-tuple-element.19.pos, s32[1]{0:T(128)S(6)} %copy.7.cnt, s32[2,4]{1,0:T(2,128)S(1)} %get-tuple-element.20.prev_pos, s32[1]{0:T(128)} %get-tuple-element.21.prev_cnt, ...), custom_call_target="tpu_custom_call" | custom-call | tf_op jit(solution)/shard_map/pack/pallas_call | solution.py:579
  16.5 0.0 copy-start
  16.5 0.0 copy-start.2
  16.5 24.8 %exchange.1 = (f32[2,2,896,256]{3,2,1,0:T(8,128)S(1)}, f32[2,256,2048]{2,1,0:T(8,128)S(1)}) custom-call(f32[2,384,256]{2,1,0:T(8,128)S(1)} %get-tuple-element.25.ahead, f32[2,384,256]{2,1,0:T(8,128)S(1)} %get-tuple-element.26.behind, f32[2,256,2048]{2,1,0:T(8,128)S(1)} %get-tuple-element.22.tile), custom_call_target="tpu_custom_call" | custom-call | tf_op jit(solution)/shard_map/exchange/pallas_call | solution.py:591
  41.4 0.0 copy-done
  41.4 0.0 copy-done.2
  41.4 5.8 %compute.1 = (f32[2,2,384,256]{3,2,1,0:T(8,128)S(1)}, f32[2,3,2,256,256]{4,3,2,1,0:T(8,128)S(1)}) custom-call(s32[80]{0:T(128)S(1)} %get-tuple-element.24.plan, f32[2,256,2048]{2,1,0:T(8,128)S(1)} %get-tuple-element.22.tile, f32[2,256,2048]{2,1,0:T(8,128)S(1)} %get-tuple-element.27.other, f32[2,2,896,256]{3,2,1,0:T(8,128)S(1)} %get-tuple-element.28.received, ...), custom_call_target="tpu_custom_call" | custom-call | tf_op jit(solution)/shard_map/compute/pallas_call | solution.py:604
  47.2 25.5 %giveback.1 = (f32[2,2,384,256]{3,2,1,0:T(8,128)S(1)}, f32[3,2,256,256]{3,2,1,0:T(8,128)S(1)}) custom-call(f32[2,2,384,256]{3,2,1,0:T(8,128)S(1)} %get-tuple-element.29.rows, f32[2,3,2,256,256]{4,3,2,1,0:T(8,128)S(1)} %get-tuple-element.30.windows.grads), custom_call_target="tpu_custom_call" | custom-call | tf_op jit(solution)/shard_map/giveback/pallas_call | solution.py:614
  72.6 4.4 %gather.1 = f32[2,256,2048]{2,1,0:T(8,128)} custom-call(s32[80]{0:T(128)S(1)} %get-tuple-element.24.plan, f32[2,2,384,256]{3,2,1,0:T(8,128)S(1)} %get-tuple-element.31.rows, f32[3,2,256,256]{3,2,1,0:T(8,128)S(1)} %get-tuple-element.32.partner, f32[2,3,2,256,256]{4,3,2,1,0:T(8,128)S(1)} %get-tuple-element.30.windows.grads), custom_call_target="tpu_custom_call" | custom-call | tf_op jit(solution)/shard_map/gather/pallas_call | solution.py:626
Async XLA Ops:
  0.7 1.2 %copy-start.1 = (f32[4,256,256]{2,1,0:T(8,128)S(1)}, f32[4,256,256]{2,1,0:T(8,128)}, u32[]{:S(2)}) copy-start(f32[4,256,256]{2,1,0:T(8,128)} %measured_hbm.1) | copy-start | bytes 3145732
  1.9 0.7 copy-start.3
  16.5 24.9 %copy-start = (bf16[8,2,256,256]{3,2,1,0:T(8,128)(2,1)S(1)}, bf16[8,2,256,256]{3,2,1,0:T(8,128)(2,1)}, u32[]{:S(2)}) copy-start(bf16[8,2,256,256]{3,2,1,0:T(8,128)(2,1)} %constant.2.clone.table) | copy-start | bytes 6291460
  16.5 24.9 %copy-start.2 = (f32[2,256,256]{2,1,0:T(8,128)S(1)}, f32[2,256,256]{2,1,0:T(8,128)}, u32[]{:S(2)}) copy-start(f32[2,256,256]{2,1,0:T(8,128)} %probe.1) | copy-start | bytes 1572868

commit v7 on v6

--- a/solution.py
+++ b/solution.py
@@ -16,6 +16,7 @@
 BUDGET = 48
 ROWS = 8 * BUDGET
 PAD = 256
+CHUNK = 32
 SPAN = 20
 
 
@@ -245,8 +246,8 @@
 
 
 def return_kernel(
-    n_lat, rows, windows, received, partner,
-    row_send, row_recv, swap_send, swap_recv,
+    n_lat, plan, rows, windows, received, tile,
+    partner, row_send, row_recv, swap_send, swap_recv,
 ):
     depth = lax.axis_index("depth")
     lat = lax.axis_index("lat")
@@ -255,21 +256,57 @@
     greet(depth, lat, after, before)
     pl.semaphore_wait(pltpu.get_barrier_semaphore(), 4)
     target = jnp.where(depth == 0, after, before)
+
+    def part(c):
+        return received.at[c, :, pl.ds(CHUNK, ROWS), :]
+
     sends = [
-        remote(rows.at[s], received.at[depth], row_send.at[s], row_recv.at[depth], s, target)
+        remote(rows.at[s], part(depth), row_send.at[s], row_recv.at[depth], s, target)
         for s in range(2)
     ]
     for copy in sends:
         copy.start()
     swap = remote(windows.at[1 - depth], partner, swap_send, swap_recv, 1 - depth, lat)
     swap.start()
+    sum_windows(plan, depth, lambda j, c, at: windows[depth, j, c, at, :], tile, True)
+    swap.wait()
+    sum_windows(plan, 1 - depth, lambda j, c, at: partner[j, c, at, :], tile, False)
     for copy in sends:
         copy.wait_send()
     for c in range(2):
-        remote(
-            rows.at[0], received.at[c], row_send.at[0], row_recv.at[c], 0, target
-        ).wait_recv()
-    swap.wait()
+        remote(rows.at[0], part(c), row_send.at[0], row_recv.at[c], 0, target).wait_recv()
+
+
+def sum_windows(plan, core, read, tile, first):
+    at = jnp.where(core == 0, OWN_LEFT, PREV_RIGHT)
+    row = lax.broadcasted_iota(jnp.int32, (8, N), 0)
+    lane = lanes()
+    jobs = []
+    for j in range(MAX_JOBS):
+        r = plan[at + 2 + 5 * j]
+        low = jnp.where(core == 0, r, 0)
+        high = jnp.where(plan[at] > j, jnp.where(core == 0, N, r), 0)
+        jobs.append((low, high, plan[at + 2 + 5 * j + 1] * N + plan[at + 2 + 5 * j + 2]))
+
+    def step(g, carry):
+        dst = pl.ds(pl.multiple_of(g * 8, 8), 8)
+        here = row + g * 8
+        for c in range(2):
+            values = [
+                jnp.where((here >= low) & (here < high), read(j, c, dst), 0.0)
+                for j, (low, high, _) in enumerate(jobs)
+            ]
+            for q in range(tile.shape[2] // N):
+                total = None if first else tile[c, dst, q * N : q * N + N]
+                for value, (_, _, column) in zip(values, jobs):
+                    offset = lane + (q * N - column)
+                    inside = (offset >= 0) & (offset < N)
+                    value = jnp.where(inside, value, 0.0)
+                    total = value if total is None else total + value
+                tile[c, dst, q * N : q * N + N] = total
+        return carry
+
+    lax.fori_loop(0, N // 8, step, 0)
 
 
 P_PLUS, P_MINUS, F_EVEN, F_ODD = 0, 1, 2, 3
@@ -478,64 +515,39 @@
         work([jobs - 1])
 
 
-def gather_kernel(plan, rows, partner, grads, out, tile, out_sems):
-    depth = lax.axis_index("depth")
-
-    def clear(i, carry):
-        at = pl.multiple_of(i * 8, 8)
-        for c in range(2):
-            tile[c, pl.ds(at, 8), :] = jnp.zeros((8, tile.shape[2]), jnp.float32)
-        return carry
-
-    lax.fori_loop(0, N // 8, clear, 0)
-    row = lax.broadcasted_iota(jnp.int32, (8, N), 0)
-
-    def add(at, j, c, lower, packed, near):
+def gather_kernel(plan, rows, tile_in, out, tile, out_sems):
+    row = lax.broadcasted_iota(jnp.int32, (CHUNK, N), 0)
+    lane = lax.broadcasted_iota(jnp.int32, (CHUNK, N), 1)
+
+    def add(at, j, c, lower):
         r = plan[at + 2 + 5 * j]
-        block = plan[at + 2 + 5 * j + 1]
         start = plan[at + 2 + 5 * j + 3]
-        first = 0 if lower else lax.div(r, 8)
-        last = lax.div(r + 7, 8) if lower else 32
-        keep = lanes() >= plan[at + 2 + 5 * j + 2]
-        low = pl.multiple_of(block * N, N)
-        high = pl.multiple_of(block * N + N, N)
+        first = 0 if lower else lax.div(r, CHUNK)
+        last = lax.div(r + CHUNK - 1, CHUNK) if lower else N // CHUNK
+        skip = 0 if lower else lax.div(r, 8)
+        keep = lane >= plan[at + 2 + 5 * j + 2]
+        low = pl.multiple_of(plan[at + 2 + 5 * j + 1] * N, N)
+        high = pl.multiple_of(plan[at + 2 + 5 * j + 1] * N + N, N)
 
         def step(g, carry):
-            dst = pl.multiple_of(g * 8, 8)
+            dst = pl.multiple_of(g * CHUNK, CHUNK)
             inside = (row + dst < r) if lower else (row + dst >= r)
-            if packed:
-                src = pl.multiple_of((start + g - first) * 8, 8)
-                value = rows[0 if lower else 1, c, pl.ds(src, 8), :]
-            else:
-                value = grads[depth, j, c, pl.ds(dst, 8), :] if near else partner[j, c, pl.ds(dst, 8), :]
-            value = jnp.where(inside, value, 0.0)
-            tile[c, pl.ds(dst, 8), pl.ds(low, N)] += jnp.where(keep, value, 0.0)
-            tile[c, pl.ds(dst, 8), pl.ds(high, N)] += jnp.where(keep, 0.0, value)
+            src = pl.multiple_of(CHUNK + (start - skip) * 8 + g * CHUNK, 8)
+            value = jnp.where(inside, rows[0 if lower else 1, c, pl.ds(src, CHUNK), :], 0.0)
+            tile[c, pl.ds(dst, CHUNK), pl.ds(low, N)] += jnp.where(keep, value, 0.0)
+            tile[c, pl.ds(dst, CHUNK), pl.ds(high, N)] += jnp.where(keep, 0.0, value)
             return carry
 
         lax.fori_loop(first, last, step, 0)
 
-    def run(at, c, lower, packed, near):
-        def step(j, carry):
-            add(at, j, c, lower, packed, near)
-            return carry
-
-        lax.fori_loop(0, plan[at], step, 0)
-
     for c in range(2):
-
-        @pl.when(depth == 0)
-        def _(c=c):
-            run(OWN_LEFT, c, False, False, True)
-            run(PREV_RIGHT, c, True, False, False)
-
-        @pl.when(depth == 1)
-        def _(c=c):
-            run(OWN_LEFT, c, False, False, False)
-            run(PREV_RIGHT, c, True, False, True)
-
-        run(OWN_RIGHT, c, False, True, False)
-        run(PREV_LEFT, c, True, True, False)
+        for at, lower in ((OWN_RIGHT, False), (PREV_LEFT, True)):
+
+            def step(j, carry, at=at, lower=lower, c=c):
+                add(at, j, c, lower)
+                return carry
+
+            lax.fori_loop(0, plan[at], step, 0)
         pltpu.make_async_copy(tile.at[c], out.at[c], out_sems.at[c]).start()
     for c in range(2):
         pltpu.make_async_copy(tile.at[c], out.at[c], out_sems.at[c]).wait()
@@ -611,27 +623,31 @@
         compiler_params=pltpu.CompilerParams(vmem_limit_bytes=30 << 20),
     )(plan, tile, other, received, measured, probe, table)
 
-    rows_back, partner = pl.pallas_call(
+    rows_back, tile = pl.pallas_call(
         functools.partial(return_kernel, n_lat),
         name="giveback",
-        out_shape=(shape(2, 2, ROWS, N), shape(MAX_JOBS, 2, N, N)),
-        in_specs=[VMEM, VMEM],
+        out_shape=(shape(2, 2, ROWS + 2 * CHUNK, N), shape(2, N, columns)),
+        in_specs=[SMEM, VMEM, VMEM],
         out_specs=(VMEM, VMEM),
-        scratch_shapes=[dma((2,)), dma((2,)), dma, dma],
+        scratch_shapes=[
+            pltpu.VMEM((MAX_JOBS, 2, N, N), jnp.float32),
+            dma((2,)), dma((2,)), dma, dma,
+        ],
         compiler_params=pltpu.CompilerParams(
             collective_id=1, has_side_effects=True, vmem_limit_bytes=12 << 20
         ),
-    )(rows_out, grads)
-
-    out = pl.pallas_call(
+    )(plan, rows_out, grads)
+
+    out, _ = pl.pallas_call(
         gather_kernel,
         name="gather",
-        out_shape=shape(2, N, columns),
-        in_specs=[SMEM, VMEM, VMEM, VMEM],
-        out_specs=HBM,
-        scratch_shapes=[pltpu.VMEM((2, N, columns), jnp.float32), dma((2,))],
-        compiler_params=pltpu.CompilerParams(vmem_limit_bytes=20 << 20),
-    )(plan, rows_back, partner, grads)
+        out_shape=(shape(2, N, columns), shape(2, N, columns)),
+        in_specs=[SMEM, VMEM, VMEM],
+        out_specs=(HBM, VMEM),
+        scratch_shapes=[dma((2,))],
+        input_output_aliases={2: 1},
+        compiler_params=pltpu.CompilerParams(vmem_limit_bytes=12 << 20),
+    )(plan, rows_back, tile)
     return out.reshape(object_slices.shape)
 
 

time: 77.3 us -> 76.2 us (0.986)
  Pallas kernels: 74.4 us -> 73.3 us
    pallas_call x1, Pallas kernels: 4.44 us -> 2.68 us  [shards(): pl.pallas_call(gather_kernel, name='gather', out_shape=(shape(2, N, colum...]
where the time goes in v7:
time: 76.2 us; the launch traced here: 76 us
  Pallas kernels  73.3 us (96%)
  local copies, waits for them, and re-layouts  1.91 us (3%)
    pallas_call x1, Pallas kernels, shards(): pl.pallas_call(functools.partial(return_kernel, n_lat), name='giveback',...  26 us
    pallas_call x1, Pallas kernels, shards(): pl.pallas_call(functools.partial(exchange_kernel, n_lat), name='exchange'...  24.8 us
    pallas_call x1, Pallas kernels, shards(): pl.pallas_call(functools.partial(announce_kernel, n_lat), name='announce'...  11.4 us
    pallas_call x1, Pallas kernels, shards(): pl.pallas_call(compute_kernel, name='compute', out_shape=(shape(2, 2, ROW...  5.95 us
    pallas_call x1, Pallas kernels, shards(): pl.pallas_call(gather_kernel, name='gather', out_shape=(shape(2, N, colum...  2.68 us
    pallas_call x1, Pallas kernels, shards(): pl.pallas_call(pack_kernel, name='pack', out_shape=(jax.ShapeDtypeStruct(...  2.43 us
    unnamed x8, local copies, waits for them, and re-layouts  1.91 us

profile of v7, /device:TPU:1, one launch (start us, length us, event | category | flops | bytes accessed | tf_op | source)
XLA Modules:
  0.0 76.0 jit_solution(10792702604247380496)
XLA Ops:
  0.7 0.0 copy-start.1
  0.7 1.2 %copy-done.1 = f32[4,256,256]{2,1,0:T(8,128)S(1)} copy-done((f32[4,256,256]{2,1,0:T(8,128)S(1)}, f32[4,256,256]{2,1,0:T(8,128)}, u32[]{:S(2)}) %copy-start.1) | copy-done | bytes 1048600
  1.9 0.0 copy-start.3
  1.9 0.7 copy-done.3
  2.6 11.4 %announce.1 = (s32[2,4]{1,0:T(2,128)S(1)}, s32[2,4]{1,0:T(2,128)S(1)}, s32[1]{0:T(128)}, f32[2,256,2048]{2,1,0:T(8,128)S(1)}, f32[4,256,256]{2,1,0:T(8,128)S(1)}) custom-call(s32[2,4]{1,0:T(2,128)S(1)} %bitcast.3, s32[1]{0:T(128)S(6)} %copy.9.cnt, f32[2,256,2048]{2,1,0:T(8,128)} %bitcast.4, f32[4,256,256]{2,1,0:T(8,128)S(1)} %copy-done.1), custom_call_target="tpu_custom_call" | custom-call | tf_op jit(solution)/shard_map/announce/pallas_call | solution.py:570
  14.0 2.4 %pack.1 = (s32[80]{0:T(128)S(1)}, f32[2,384,256]{2,1,0:T(8,128)S(1)}, f32[2,384,256]{2,1,0:T(8,128)S(1)}) custom-call(s32[2,4]{1,0:T(2,128)S(1)} %get-tuple-element.20.pos, s32[1]{0:T(128)S(6)} %copy.9.cnt, s32[2,4]{1,0:T(2,128)S(1)} %get-tuple-element.21.prev_pos, s32[1]{0:T(128)} %get-tuple-element.22.prev_cnt, ...), custom_call_target="tpu_custom_call" | custom-call | tf_op jit(solution)/shard_map/pack/pallas_call | solution.py:591
  16.4 0.0 copy-start
  16.4 0.0 copy-start.2
  16.5 24.8 %exchange.1 = (f32[2,2,896,256]{3,2,1,0:T(8,128)S(1)}, f32[2,256,2048]{2,1,0:T(8,128)S(1)}) custom-call(f32[2,384,256]{2,1,0:T(8,128)S(1)} %get-tuple-element.26.ahead, f32[2,384,256]{2,1,0:T(8,128)S(1)} %get-tuple-element.27.behind, f32[2,256,2048]{2,1,0:T(8,128)S(1)} %get-tuple-element.23.tile), custom_call_target="tpu_custom_call" | custom-call | tf_op jit(solution)/shard_map/exchange/pallas_call | solution.py:603
  41.3 0.0 copy-done
  41.3 0.0 copy-done.2
  41.3 6.0 %compute.1 = (f32[2,2,384,256]{3,2,1,0:T(8,128)S(1)}, f32[2,3,2,256,256]{4,3,2,1,0:T(8,128)S(1)}) custom-call(s32[80]{0:T(128)S(1)} %get-tuple-element.25.plan, f32[2,256,2048]{2,1,0:T(8,128)S(1)} %get-tuple-element.23.tile, f32[2,256,2048]{2,1,0:T(8,128)S(1)} %get-tuple-element.28.other, f32[2,2,896,256]{3,2,1,0:T(8,128)S(1)} %get-tuple-element.29.received, ...), custom_call_target="tpu_custom_call" | custom-call | tf_op jit(solution)/shard_map/compute/pallas_call | solution.py:616
  47.3 26.0 %giveback.1 = (f32[2,2,448,256]{3,2,1,0:T(8,128)S(1)}, f32[2,256,2048]{2,1,0:T(8,128)S(1)}) custom-call(s32[80]{0:T(128)S(1)} %get-tuple-element.25.plan, f32[2,2,384,256]{3,2,1,0:T(8,128)S(1)} %get-tuple-element.30.rows, f32[2,3,2,256,256]{4,3,2,1,0:T(8,128)S(1)} %get-tuple-element.31.windows), custom_call_target="tpu_custom_call" | custom-call | tf_op jit(solution)/shard_map/giveback/pallas_call | solution.py:626
  73.3 2.7 %gather.1 = (f32[2,256,2048]{2,1,0:T(8,128)}, f32[2,256,2048]{2,1,0:T(8,128)S(1)}) custom-call(s32[80]{0:T(128)S(1)} %get-tuple-element.25.plan, f32[2,2,448,256]{3,2,1,0:T(8,128)S(1)} %get-tuple-element.32.rows, f32[2,256,2048]{2,1,0:T(8,128)S(1)} %get-tuple-element.33.tile_in), custom_call_target="tpu_custom_call", output_to_operand_aliasing={{1}: (2, {})} | custom-call | tf_op jit(solution)/shard_map/gather/pallas_call | solution.py:641
Async XLA Ops:
  0.7 1.2 %copy-start.1 = (f32[4,256,256]{2,1,0:T(8,128)S(1)}, f32[4,256,256]{2,1,0:T(8,128)}, u32[]{:S(2)}) copy-start(f32[4,256,256]{2,1,0:T(8,128)} %measured_hbm.1) | copy-start | bytes 3145732
  1.9 0.7 copy-start.3
  16.4 24.9 %copy-start = (bf16[8,2,256,256]{3,2,1,0:T(8,128)(2,1)S(1)}, bf16[8,2,256,256]{3,2,1,0:T(8,128)(2,1)}, u32[]{:S(2)}) copy-start(bf16[8,2,256,256]{3,2,1,0:T(8,128)(2,1)} %constant.2.clone.table) | copy-start | bytes 6291460
  16.4 24.9 %copy-start.2 = (f32[2,256,256]{2,1,0:T(8,128)S(1)}, f32[2,256,256]{2,1,0:T(8,128)}, u32[]{:S(2)}) copy-start(f32[2,256,256]{2,1,0:T(8,128)} %probe.1) | copy-start | bytes 1572868

commit v8 on v7

--- a/solution.py
+++ b/solution.py
@@ -192,8 +192,8 @@
 
 
 def exchange_kernel(
-    n_lat, ahead, behind, tile, received, other,
-    row_send, row_recv, tile_send, tile_recv,
+    n_lat, plan, ahead, behind, tile, probe, received, windows, probes,
+    other, row_send, row_recv, tile_send, tile_recv,
 ):
     depth = lax.axis_index("depth")
     lat = lax.axis_index("lat")
@@ -213,11 +213,41 @@
         copy.start()
     swap = remote(tile, other, tile_send, tile_recv, 1 - depth, lat)
     swap.start()
+    at = jnp.where(depth == 0, OWN_LEFT, PREV_RIGHT)
+    for j in range(MAX_JOBS):
+        shift = plan[at + 2 + 5 * j + 2]
+        shift = jnp.where(shift == N, 0, shift)
+        for c in range(2):
+            probes[j, c] = pltpu.roll(pltpu.roll(probe[c], plan[at + 2 + 5 * j], 0), shift, 1)
+    pick_columns(plan, at, tile, windows, depth)
+    swap.wait()
+    pick_columns(plan, at, other, windows, 1 - depth)
     for copy in sends:
         copy.wait_send()
     for s in range(2):
         remote(ahead, slot(s), row_send.at[0], row_recv.at[s], 1, after).wait_recv()
-    swap.wait()
+
+
+def pick_columns(plan, at, source, windows, s):
+    lane = lanes()
+    columns = [
+        plan[at + 2 + 5 * j + 1] * N + plan[at + 2 + 5 * j + 2] for j in range(MAX_JOBS)
+    ]
+
+    def step(g, carry):
+        rows = pl.ds(pl.multiple_of(g * 8, 8), 8)
+        for c in range(2):
+            picked = [jnp.zeros((8, N), jnp.float32)] * MAX_JOBS
+            for q in range(source.shape[2] // N):
+                value = source[c, rows, q * N : q * N + N]
+                for j, column in enumerate(columns):
+                    offset = lane + (q * N - column)
+                    picked[j] = jnp.where((offset >= 0) & (offset < N), value, picked[j])
+            for j in range(MAX_JOBS):
+                windows[s, j, c, rows, :] = picked[j]
+        return carry
+
+    lax.fori_loop(0, N // 8, step, 0)
 
 
 def remote(src, dst, send, recv, depth, lat):
@@ -411,7 +441,7 @@
 
 
 def compute_kernel(
-    plan, tile, other, received, measured, probe, table,
+    plan, windows, probes, received, measured, table,
     rows_out, grads,
     amplitude,
 ):
@@ -419,7 +449,6 @@
     at = jnp.where(depth == 0, OWN_LEFT, PREV_RIGHT)
     jobs = plan[at]
     row = lax.broadcasted_iota(jnp.int32, (N, N), 0)
-    lane = lax.broadcasted_iota(jnp.int32, (N, N), 1)
 
     def work(numbers):
         each = range(len(numbers))
@@ -445,35 +474,16 @@
             return jnp.where(depth == 0, 0, lax.div(words[k][0], 8))
 
         def window(k, s):
-            r, block, shift, start, _ = words[k]
+            r, _, _, start, _ = words[k]
             here = (row >= jnp.where(depth == 0, r, 0)) & (row < jnp.where(depth == 0, N, r))
-            keep = lane >= shift
             src = pl.multiple_of(PAD + (start - base_of(k)) * 8, 8)
-            column = pl.multiple_of(block * N, N)
-            left, right = pl.ds(column, N), pl.ds(pl.multiple_of(column + N, N), N)
-            near = depth == s
             return [
-                jnp.where(
-                    here,
-                    jnp.where(
-                        keep,
-                        jnp.where(near, tile[c, :, left], other[c, :, left]),
-                        jnp.where(near, tile[c, :, right], other[c, :, right]),
-                    ),
-                    received[s, c, pl.ds(src, N), :],
-                )
+                jnp.where(here, windows[s, numbers[k], c], received[s, c, pl.ds(src, N), :])
                 for c in range(2)
             ]
 
-        def rolled(k):
-            r, _, shift, _, _ = words[k]
-            return [
-                pltpu.roll(pltpu.roll(probe[c], r, 0), jnp.where(shift == N, 0, shift), 1)
-                for c in range(2)
-            ]
-
-        probes = [rolled(k) for k in each]
-        waves = [product(p, window(k, 0)) for k, p in enumerate(probes)]
+        turned = [[probes[j, c] for c in range(2)] for j in numbers]
+        waves = [product(p, window(k, 0)) for k, p in enumerate(turned)]
         waves = propagate(waves, table, False)
         slices = [window(k, 1) for k in each]
         spectra = to_spectrum([product(w, o) for w, o in zip(waves, slices)], table)
@@ -488,7 +498,7 @@
         backs = [conj_product(o, b) for o, b in zip(slices, backs)]
         backs = propagate(backs, table, True)
         for k in each:
-            grads[0, numbers[k], 0], grads[0, numbers[k], 1] = conj_product(probes[k], backs[k])
+            grads[0, numbers[k], 0], grads[0, numbers[k], 1] = conj_product(turned[k], backs[k])
         for k in each:
             r, start = words[k][0], words[k][3]
             base = base_of(k)
@@ -600,28 +610,35 @@
         out_specs=(SMEM, VMEM, VMEM),
         compiler_params=pltpu.CompilerParams(vmem_limit_bytes=4 << 20),
     )(positions, counts, prev_positions, prev_counts, tile, measured)
-    received, other = pl.pallas_call(
+    received, windows, probes = pl.pallas_call(
         functools.partial(exchange_kernel, n_lat),
         name="exchange",
-        out_shape=(shape(2, 2, ROWS + 2 * PAD, N), shape(2, N, columns)),
-        in_specs=[VMEM, VMEM, VMEM],
-        out_specs=(VMEM, VMEM),
-        scratch_shapes=[dma((2,)), dma((2,)), dma, dma],
+        out_shape=(
+            shape(2, 2, ROWS + 2 * PAD, N),
+            shape(2, MAX_JOBS, 2, N, N),
+            shape(MAX_JOBS, 2, N, N),
+        ),
+        in_specs=[SMEM, VMEM, VMEM, VMEM, VMEM],
+        out_specs=(VMEM, VMEM, VMEM),
+        scratch_shapes=[
+            pltpu.VMEM((2, N, columns), jnp.float32),
+            dma((2,)), dma((2,)), dma, dma,
+        ],
         compiler_params=pltpu.CompilerParams(
             collective_id=0, has_side_effects=True, vmem_limit_bytes=12 << 20
         ),
-    )(ahead, behind, tile)
+    )(plan, ahead, behind, tile, probe)
 
     table = jnp.asarray(tables())
     rows_out, grads = pl.pallas_call(
         compute_kernel,
         name="compute",
         out_shape=(shape(2, 2, ROWS, N), shape(2, MAX_JOBS, 2, N, N)),
-        in_specs=[SMEM, VMEM, VMEM, VMEM, VMEM, VMEM, VMEM],
+        in_specs=[SMEM, VMEM, VMEM, VMEM, VMEM, VMEM],
         out_specs=(VMEM, VMEM),
         scratch_shapes=[pltpu.VMEM((2, N, N), jnp.float32)],
         compiler_params=pltpu.CompilerParams(vmem_limit_bytes=30 << 20),
-    )(plan, tile, other, received, measured, probe, table)
+    )(plan, windows, probes, received, measured, table)
 
     rows_back, tile = pl.pallas_call(
         functools.partial(return_kernel, n_lat),

time: 76.2 us -> 74.4 us (0.976)
  Pallas kernels: 73.3 us -> 71.6 us
    pallas_call x1, Pallas kernels: 5.95 us -> 3.83 us  [shards(): pl.pallas_call(compute_kernel, name='compute', out_shape=(shape(2, 2, ROW...]
where the time goes in v8:
time: 74.4 us; the launch traced here: 74.2 us
  Pallas kernels  71.6 us (96%)
  local copies, waits for them, and re-layouts  1.91 us (3%)
    pallas_call x1, Pallas kernels, shards(): pl.pallas_call(functools.partial(return_kernel, n_lat), name='giveback',...  26 us
    pallas_call x1, Pallas kernels, shards(): pl.pallas_call(functools.partial(exchange_kernel, n_lat), name='exchange'...  25.4 us
    pallas_call x1, Pallas kernels, shards(): pl.pallas_call(functools.partial(announce_kernel, n_lat), name='announce'...  11.4 us
    pallas_call x1, Pallas kernels, shards(): pl.pallas_call(compute_kernel, name='compute', out_shape=(shape(2, 2, ROW...  3.83 us
    pallas_call x1, Pallas kernels, shards(): pl.pallas_call(gather_kernel, name='gather', out_shape=(shape(2, N, colum...  2.61 us
    pallas_call x1, Pallas kernels, shards(): pl.pallas_call(pack_kernel, name='pack', out_shape=(jax.ShapeDtypeStruct(...  2.34 us
    unnamed x8, local copies, waits for them, and re-layouts  1.91 us

profile of v8, /device:TPU:1, one launch (start us, length us, event | category | flops | bytes accessed | tf_op | source)
XLA Modules:
  0.0 74.2 jit_solution(3574496272860502457)
XLA Ops:
  0.7 0.0 copy-start.1
  0.7 1.2 %copy-done.1 = f32[4,256,256]{2,1,0:T(8,128)S(1)} copy-done((f32[4,256,256]{2,1,0:T(8,128)S(1)}, f32[4,256,256]{2,1,0:T(8,128)}, u32[]{:S(2)}) %copy-start.1) | copy-done | bytes 1048600
  1.9 0.0 copy-start.3
  1.9 0.7 copy-done.3
  2.6 11.4 %announce.1 = (s32[2,4]{1,0:T(2,128)S(1)}, s32[2,4]{1,0:T(2,128)S(1)}, s32[1]{0:T(128)}, f32[2,256,2048]{2,1,0:T(8,128)S(1)}, f32[4,256,256]{2,1,0:T(8,128)S(1)}) custom-call(s32[2,4]{1,0:T(2,128)S(1)} %bitcast.3, s32[1]{0:T(128)S(6)} %copy.9.cnt, f32[2,256,2048]{2,1,0:T(8,128)} %bitcast.4, f32[4,256,256]{2,1,0:T(8,128)S(1)} %copy-done.1), custom_call_target="tpu_custom_call" | custom-call | tf_op jit(solution)/shard_map/announce/pallas_call | solution.py:580
  14.0 0.0 copy-start.2
  14.0 2.3 %pack.1 = (s32[80]{0:T(128)S(1)}, f32[2,384,256]{2,1,0:T(8,128)S(1)}, f32[2,384,256]{2,1,0:T(8,128)S(1)}) custom-call(s32[2,4]{1,0:T(2,128)S(1)} %get-tuple-element.21.pos, s32[1]{0:T(128)S(6)} %copy.9.cnt, s32[2,4]{1,0:T(2,128)S(1)} %get-tuple-element.22.prev_pos, s32[1]{0:T(128)} %get-tuple-element.23.prev_cnt, ...), custom_call_target="tpu_custom_call" | custom-call | tf_op jit(solution)/shard_map/pack/pallas_call | solution.py:601
  16.4 0.0 copy-start
  16.4 0.0 copy-done.2
  16.4 25.4 %exchange.1 = (f32[2,2,896,256]{3,2,1,0:T(8,128)S(1)}, f32[2,3,2,256,256]{4,3,2,1,0:T(8,128)S(1)}, f32[3,2,256,256]{3,2,1,0:T(8,128)S(1)}) custom-call(s32[80]{0:T(128)S(1)} %get-tuple-element.26.plan, f32[2,384,256]{2,1,0:T(8,128)S(1)} %get-tuple-element.27.ahead, f32[2,384,256]{2,1,0:T(8,128)S(1)} %get-tuple-element.28.behind, ...), custom_call_target="tpu_custom_call" | custom-call | tf_op jit(solution)/shard_map/exchange/pallas_call | solution.py:613
  41.8 0.0 copy-done
  41.8 3.8 %compute.1 = (f32[2,2,384,256]{3,2,1,0:T(8,128)S(1)}, f32[2,3,2,256,256]{4,3,2,1,0:T(8,128)S(1)}) custom-call(s32[80]{0:T(128)S(1)} %get-tuple-element.26.plan, f32[2,3,2,256,256]{4,3,2,1,0:T(8,128)S(1)} %get-tuple-element.29.windows, f32[3,2,256,256]{3,2,1,0:T(8,128)S(1)} %get-tuple-element.30.probes, f32[2,2,896,256]{3,2,1,0:T(8,128)S(1)} %get-tuple-element.31.received, ...), custom_call_target="tpu_custom_call" | custom-call | tf_op jit(solution)/shard_map/compute/pallas_call | solution.py:633
  45.6 26.0 %giveback.1 = (f32[2,2,448,256]{3,2,1,0:T(8,128)S(1)}, f32[2,256,2048]{2,1,0:T(8,128)S(1)}) custom-call(s32[80]{0:T(128)S(1)} %get-tuple-element.26.plan, f32[2,2,384,256]{3,2,1,0:T(8,128)S(1)} %get-tuple-element.32.rows, f32[2,3,2,256,256]{4,3,2,1,0:T(8,128)S(1)} %get-tuple-element.33.windows), custom_call_target="tpu_custom_call" | custom-call | tf_op jit(solution)/shard_map/giveback/pallas_call | solution.py:643
  71.6 2.6 %gather.1 = (f32[2,256,2048]{2,1,0:T(8,128)}, f32[2,256,2048]{2,1,0:T(8,128)S(1)}) custom-call(s32[80]{0:T(128)S(1)} %get-tuple-element.26.plan, f32[2,2,448,256]{3,2,1,0:T(8,128)S(1)} %get-tuple-element.34.rows, f32[2,256,2048]{2,1,0:T(8,128)S(1)} %get-tuple-element.35.tile_in), custom_call_target="tpu_custom_call", output_to_operand_aliasing={{1}: (2, {})} | custom-call | tf_op jit(solution)/shard_map/gather/pallas_call | solution.py:658
Async XLA Ops:
  0.7 1.2 %copy-start.1 = (f32[4,256,256]{2,1,0:T(8,128)S(1)}, f32[4,256,256]{2,1,0:T(8,128)}, u32[]{:S(2)}) copy-start(f32[4,256,256]{2,1,0:T(8,128)} %measured_hbm.1) | copy-start | bytes 3145732
  1.9 0.7 copy-start.3
  14.0 2.4 %copy-start.2 = (f32[2,256,256]{2,1,0:T(8,128)S(1)}, f32[2,256,256]{2,1,0:T(8,128)}, u32[]{:S(2)}) copy-start(f32[2,256,256]{2,1,0:T(8,128)} %probe.1) | copy-start | bytes 1572868
  16.4 25.4 %copy-start = (bf16[8,2,256,256]{3,2,1,0:T(8,128)(2,1)S(1)}, bf16[8,2,256,256]{3,2,1,0:T(8,128)(2,1)}, u32[]{:S(2)}) copy-start(bf16[8,2,256,256]{3,2,1,0:T(8,128)(2,1)} %constant.2.clone.table) | copy-start | bytes 6291460

commit v9 on v8

--- a/solution.py
+++ b/solution.py
@@ -90,8 +90,8 @@
 
 def announce_kernel(
     n_lat, pos_hbm, cnt, tile_hbm, measured_hbm,
-    pos, prev_pos, prev_cnt, tile, apart,
-    measured, spread, send, recv, local,
+    own_plan, prev_pos, prev_cnt, tile, apart,
+    measured, spread, pos, live, send, recv, local,
 ):
     depth = lax.axis_index("depth")
     lat = lax.axis_index("lat")
@@ -106,6 +106,7 @@
         pltpu.make_async_copy(measured_hbm, measured, local.at[0]),
         pltpu.make_async_copy(tile_hbm, tile, local.at[1]),
         pltpu.make_async_copy(pos_hbm, pos, local.at[2]),
+        pltpu.make_async_copy(cnt, live, local.at[3]),
     ]
     for load in loads:
         load.start()
@@ -133,23 +134,28 @@
                 apart[slot, HALF * p : HALF * p + HALF, HALF * h : HALF * h + HALF] = spread[
                     h, pl.ds(p, HALF, stride=2), :
                 ]
-    for load in loads[1:]:
+    for load in loads[2:]:
         load.wait()
+    own = choose_sides([pos[0, i] for i in range(4)], [pos[1, i] for i in range(4)], live[0])
+    for k, side in enumerate(own):
+        for w, word in enumerate(side):
+            own_plan[k * SPAN + w] = word
+    loads[1].wait()
     for copy in copies:
         copy.wait()
 
 
 def pack_kernel(
-    pos, cnt, prev_pos, prev_cnt, tile, measured, plan, ahead, behind
+    own_plan, prev_pos, prev_cnt, tile, measured, plan, ahead, behind
 ):
     depth = lax.axis_index("depth")
-    own = choose_sides([pos[0, i] for i in range(4)], [pos[1, i] for i in range(4)], cnt[0])
     prev = choose_sides(
         [prev_pos[0, i] for i in range(4)], [prev_pos[1, i] for i in range(4)], prev_cnt[0]
     )
-    for k, side in enumerate(own + prev):
+    for k, side in enumerate(prev):
         for w, word in enumerate(side):
-            plan[k * SPAN + w] = word
+            plan[k * SPAN + w] = own_plan[k * SPAN + w]
+            plan[PREV_LEFT + k * SPAN + w] = word
 
     def copy_rows(out, at, j, first, count):
         start = plan[at + 2 + 5 * j + 3]
@@ -504,17 +510,19 @@
             base = base_of(k)
             count = jnp.where(depth == 0, lax.div(r + 7, 8), 32 - lax.div(r, 8))
 
-            def step(g, carry, k=k, base=base, start=start):
-                src = pl.multiple_of((base + g) * 8, 8)
-                dst = pl.multiple_of((start + g) * 8, 8)
-                for s in range(2):
-                    for c in range(2):
-                        rows_out[s, c, pl.ds(dst, 8), :] = grads[
-                            s, numbers[k], c, pl.ds(src, 8), :
-                        ]
+            def step(g, carry, k=k, base=base, start=start, count=count):
+                for q in range(4):
+                    granule = jnp.minimum(4 * g + q, count - 1)
+                    src = pl.multiple_of((base + granule) * 8, 8)
+                    dst = pl.multiple_of((start + granule) * 8, 8)
+                    for s in range(2):
+                        for c in range(2):
+                            rows_out[s, c, pl.ds(dst, 8), :] = grads[
+                                s, numbers[k], c, pl.ds(src, 8), :
+                            ]
                 return carry
 
-            lax.fori_loop(0, count, step, 0)
+            lax.fori_loop(0, lax.div(count + 3, 4), step, 0)
 
     @pl.when(jobs >= 2)
     def _():
@@ -577,22 +585,24 @@
     tile = object_slices.reshape(object_slices.shape[1:])
     dma = pltpu.SemaphoreType.DMA
     positions = positions.T
-    positions, prev_positions, prev_counts, tile, measured = pl.pallas_call(
+    own_plan, prev_positions, prev_counts, tile, measured = pl.pallas_call(
         functools.partial(announce_kernel, n_lat),
         name="announce",
         out_shape=(
-            jax.ShapeDtypeStruct(positions.shape, jnp.int32),
+            jax.ShapeDtypeStruct((2 * SPAN,), jnp.int32),
             jax.ShapeDtypeStruct(positions.shape, jnp.int32),
             jax.ShapeDtypeStruct(counts.shape, jnp.int32),
             shape(*tile.shape),
             shape(*measured.shape),
         ),
         in_specs=[HBM, HBM, HBM, HBM],
-        out_specs=(VMEM, VMEM, VMEM, VMEM, VMEM),
+        out_specs=(SMEM, VMEM, VMEM, VMEM, VMEM),
         scratch_shapes=[
             pltpu.VMEM((4, N, N), jnp.float32),
             pltpu.VMEM((2, N, HALF), jnp.float32),
-            dma((2,)), dma((2,)), dma((3,)),
+            pltpu.SMEM((2, 4), jnp.int32),
+            pltpu.SMEM((1,), jnp.int32),
+            dma((2,)), dma((2,)), dma((4,)),
         ],
         compiler_params=pltpu.CompilerParams(
             collective_id=2, has_side_effects=True, vmem_limit_bytes=46 << 20
@@ -606,10 +616,10 @@
             shape(2, ROWS, N),
             shape(2, ROWS, N),
         ),
-        in_specs=[SMEM, SMEM, SMEM, SMEM, VMEM, VMEM],
+        in_specs=[SMEM, SMEM, SMEM, VMEM, VMEM],
         out_specs=(SMEM, VMEM, VMEM),
         compiler_params=pltpu.CompilerParams(vmem_limit_bytes=4 << 20),
-    )(positions, counts, prev_positions, prev_counts, tile, measured)
+    )(own_plan, prev_positions, prev_counts, tile, measured)
     received, windows, probes = pl.pallas_call(
         functools.partial(exchange_kernel, n_lat),
         name="exchange",

time: 74.4 us -> 74.4 us (level)
  no operation moved by 1% of the time
where the time goes in v9:
time: 74.4 us; the launch traced here: 74.3 us
  Pallas kernels  71.6 us (96%)
  local copies, waits for them, and re-layouts  1.91 us (3%)
    pallas_call x1, Pallas kernels, shards(): pl.pallas_call(functools.partial(return_kernel, n_lat), name='giveback',...  26 us
    pallas_call x1, Pallas kernels, shards(): pl.pallas_call(functools.partial(exchange_kernel, n_lat), name='exchange'...  25.4 us
    pallas_call x1, Pallas kernels, shards(): pl.pallas_call(functools.partial(announce_kernel, n_lat), name='announce'...  11.5 us
    pallas_call x1, Pallas kernels, shards(): pl.pallas_call(compute_kernel, name='compute', out_shape=(shape(2, 2, ROW...  3.85 us
    pallas_call x1, Pallas kernels, shards(): pl.pallas_call(gather_kernel, name='gather', out_shape=(shape(2, N, colum...  2.67 us
    pallas_call x1, Pallas kernels, shards(): pl.pallas_call(pack_kernel, name='pack', out_shape=(jax.ShapeDtypeStruct(...  2.24 us
    unnamed x8, local copies, waits for them, and re-layouts  1.91 us

profile of v9, /device:TPU:1, one launch (start us, length us, event | category | flops | bytes accessed | tf_op | source)
XLA Modules:
  0.0 74.3 jit_solution(9407220939785760089)
XLA Ops:
  0.7 0.0 copy-start.1
  0.7 1.2 %copy-done.1 = f32[4,256,256]{2,1,0:T(8,128)S(1)} copy-done((f32[4,256,256]{2,1,0:T(8,128)S(1)}, f32[4,256,256]{2,1,0:T(8,128)}, u32[]{:S(2)}) %copy-start.1) | copy-done | bytes 1048600
  1.9 0.0 copy-start.3
  1.9 0.7 copy-done.3
  2.6 11.5 %announce.1 = (s32[40]{0:T(128)S(1)}, s32[2,4]{1,0:T(2,128)S(1)}, s32[1]{0:T(128)}, f32[2,256,2048]{2,1,0:T(8,128)S(1)}, f32[4,256,256]{2,1,0:T(8,128)S(1)}) custom-call(s32[2,4]{1,0:T(2,128)S(1)} %bitcast.3, s32[1]{0:T(128)S(6)} %copy.9.cnt, f32[2,256,2048]{2,1,0:T(8,128)} %bitcast.4, f32[4,256,256]{2,1,0:T(8,128)S(1)} %copy-done.1), custom_call_target="tpu_custom_call" | custom-call | tf_op jit(solution)/shard_map/announce/pallas_call | solution.py:588
  14.0 0.0 copy-start.2
  14.1 2.2 %pack.1 = (s32[80]{0:T(128)S(1)}, f32[2,384,256]{2,1,0:T(8,128)S(1)}, f32[2,384,256]{2,1,0:T(8,128)S(1)}) custom-call(s32[40]{0:T(128)S(1)} %get-tuple-element.21.own_plan, s32[2,4]{1,0:T(2,128)S(1)} %get-tuple-element.22.prev_pos, s32[1]{0:T(128)} %get-tuple-element.23.prev_cnt, f32[2,256,2048]{2,1,0:T(8,128)S(1)} %get-tuple-element.24.tile, ...), custom_call_target="tpu_custom_call" | custom-call | tf_op jit(solution)/shard_map/pack/pallas_call | solution.py:611
  16.3 0.0 copy-start
  16.3 0.0 copy-done.2
  16.3 25.4 %exchange.1 = (f32[2,2,896,256]{3,2,1,0:T(8,128)S(1)}, f32[2,3,2,256,256]{4,3,2,1,0:T(8,128)S(1)}, f32[3,2,256,256]{3,2,1,0:T(8,128)S(1)}) custom-call(s32[80]{0:T(128)S(1)} %get-tuple-element.26.plan, f32[2,384,256]{2,1,0:T(8,128)S(1)} %get-tuple-element.27.ahead, f32[2,384,256]{2,1,0:T(8,128)S(1)} %get-tuple-element.28.behind, ...), custom_call_target="tpu_custom_call" | custom-call | tf_op jit(solution)/shard_map/exchange/pallas_call | solution.py:623
  41.7 0.0 copy-done
  41.7 3.8 %compute.1 = (f32[2,2,384,256]{3,2,1,0:T(8,128)S(1)}, f32[2,3,2,256,256]{4,3,2,1,0:T(8,128)S(1)}) custom-call(s32[80]{0:T(128)S(1)} %get-tuple-element.26.plan, f32[2,3,2,256,256]{4,3,2,1,0:T(8,128)S(1)} %get-tuple-element.29.windows, f32[3,2,256,256]{3,2,1,0:T(8,128)S(1)} %get-tuple-element.30.probes, f32[2,2,896,256]{3,2,1,0:T(8,128)S(1)} %get-tuple-element.31.received, ...), custom_call_target="tpu_custom_call" | custom-call | tf_op jit(solution)/shard_map/compute/pallas_call | solution.py:643
  45.6 26.0 %giveback.1 = (f32[2,2,448,256]{3,2,1,0:T(8,128)S(1)}, f32[2,256,2048]{2,1,0:T(8,128)S(1)}) custom-call(s32[80]{0:T(128)S(1)} %get-tuple-element.26.plan, f32[2,2,384,256]{3,2,1,0:T(8,128)S(1)} %get-tuple-element.32.rows, f32[2,3,2,256,256]{4,3,2,1,0:T(8,128)S(1)} %get-tuple-element.33.windows), custom_call_target="tpu_custom_call" | custom-call | tf_op jit(solution)/shard_map/giveback/pallas_call | solution.py:653
  71.6 2.7 %gather.1 = (f32[2,256,2048]{2,1,0:T(8,128)}, f32[2,256,2048]{2,1,0:T(8,128)S(1)}) custom-call(s32[80]{0:T(128)S(1)} %get-tuple-element.26.plan, f32[2,2,448,256]{3,2,1,0:T(8,128)S(1)} %get-tuple-element.34.rows, f32[2,256,2048]{2,1,0:T(8,128)S(1)} %get-tuple-element.35.tile_in), custom_call_target="tpu_custom_call", output_to_operand_aliasing={{1}: (2, {})} | custom-call | tf_op jit(solution)/shard_map/gather/pallas_call | solution.py:668
Async XLA Ops:
  0.7 1.2 %copy-start.1 = (f32[4,256,256]{2,1,0:T(8,128)S(1)}, f32[4,256,256]{2,1,0:T(8,128)}, u32[]{:S(2)}) copy-start(f32[4,256,256]{2,1,0:T(8,128)} %measured_hbm.1) | copy-start | bytes 3145732
  1.9 0.7 copy-start.3
  14.0 2.3 %copy-start.2 = (f32[2,256,256]{2,1,0:T(8,128)S(1)}, f32[2,256,256]{2,1,0:T(8,128)}, u32[]{:S(2)}) copy-start(f32[2,256,256]{2,1,0:T(8,128)} %probe.1) | copy-start | bytes 1572868
  16.3 25.4 %copy-start = (bf16[8,2,256,256]{3,2,1,0:T(8,128)(2,1)S(1)}, bf16[8,2,256,256]{3,2,1,0:T(8,128)(2,1)}, u32[]{:S(2)}) copy-start(bf16[8,2,256,256]{3,2,1,0:T(8,128)(2,1)} %constant.2.clone.table) | copy-start | bytes 6291460

commit v10 on v9

--- a/solution.py
+++ b/solution.py
@@ -122,7 +122,7 @@
     order = jnp.where(lane < HALF, 2 * lane, 2 * lane - (N - 1))
     shuffle = jnp.where(row == order, 1.0, 0.0).astype(jnp.bfloat16)
     loads[0].wait()
-    for slot in range(4):
+    def rearrange(slot, carry):
         hi, lo = halves(measured[slot])
         columns = dot(
             jnp.concatenate([hi, lo], axis=1), jnp.concatenate([shuffle, shuffle], axis=0)
@@ -134,6 +134,9 @@
                 apart[slot, HALF * p : HALF * p + HALF, HALF * h : HALF * h + HALF] = spread[
                     h, pl.ds(p, HALF, stride=2), :
                 ]
+        return carry
+
+    lax.fori_loop(0, 4, rearrange, 0)
     for load in loads[2:]:
         load.wait()
     own = choose_sides([pos[0, i] for i in range(4)], [pos[1, i] for i in range(4)], live[0])
@@ -220,11 +223,14 @@
     swap = remote(tile, other, tile_send, tile_recv, 1 - depth, lat)
     swap.start()
     at = jnp.where(depth == 0, OWN_LEFT, PREV_RIGHT)
-    for j in range(MAX_JOBS):
+    def turn(i, carry):
+        j, c = lax.div(i, 2), lax.rem(i, 2)
         shift = plan[at + 2 + 5 * j + 2]
         shift = jnp.where(shift == N, 0, shift)
-        for c in range(2):
-            probes[j, c] = pltpu.roll(pltpu.roll(probe[c], plan[at + 2 + 5 * j], 0), shift, 1)
+        probes[j, c] = pltpu.roll(pltpu.roll(probe[c], plan[at + 2 + 5 * j], 0), shift, 1)
+        return carry
+
+    lax.fori_loop(0, 2 * MAX_JOBS, turn, 0)
     pick_columns(plan, at, tile, windows, depth)
     swap.wait()
     pick_columns(plan, at, other, windows, 1 - depth)

time: 74.4 us -> 74.3 us (level)
  no operation moved by 1% of the time
where the time goes in v10:
time: 74.3 us; the launch traced here: 74.1 us
  Pallas kernels  71.5 us (96%)
  local copies, waits for them, and re-layouts  1.91 us (3%)
    pallas_call x1, Pallas kernels, shards(): pl.pallas_call(functools.partial(return_kernel, n_lat), name='giveback',...  26 us
    pallas_call x1, Pallas kernels, shards(): pl.pallas_call(functools.partial(exchange_kernel, n_lat), name='exchange'...  25.4 us
    pallas_call x1, Pallas kernels, shards(): pl.pallas_call(functools.partial(announce_kernel, n_lat), name='announce'...  11.5 us
    pallas_call x1, Pallas kernels, shards(): pl.pallas_call(compute_kernel, name='compute', out_shape=(shape(2, 2, ROW...  3.83 us
    pallas_call x1, Pallas kernels, shards(): pl.pallas_call(gather_kernel, name='gather', out_shape=(shape(2, N, colum...  2.63 us
    pallas_call x1, Pallas kernels, shards(): pl.pallas_call(pack_kernel, name='pack', out_shape=(jax.ShapeDtypeStruct(...  2.17 us
    unnamed x8, local copies, waits for them, and re-layouts  1.91 us

profile of v10, /device:TPU:1, one launch (start us, length us, event | category | flops | bytes accessed | tf_op | source)
XLA Modules:
  0.0 74.1 jit_solution(12818414360333355806)
XLA Ops:
  0.7 0.0 copy-start.1
  0.7 1.2 %copy-done.1 = f32[4,256,256]{2,1,0:T(8,128)S(1)} copy-done((f32[4,256,256]{2,1,0:T(8,128)S(1)}, f32[4,256,256]{2,1,0:T(8,128)}, u32[]{:S(2)}) %copy-start.1) | copy-done | bytes 1048600
  1.9 0.0 copy-start.3
  1.9 0.7 copy-done.3
  2.6 11.5 %announce.1 = (s32[40]{0:T(128)S(1)}, s32[2,4]{1,0:T(2,128)S(1)}, s32[1]{0:T(128)}, f32[2,256,2048]{2,1,0:T(8,128)S(1)}, f32[4,256,256]{2,1,0:T(8,128)S(1)}) custom-call(s32[2,4]{1,0:T(2,128)S(1)} %bitcast.3, s32[1]{0:T(128)S(6)} %copy.9.cnt, f32[2,256,2048]{2,1,0:T(8,128)} %bitcast.4, f32[4,256,256]{2,1,0:T(8,128)S(1)} %copy-done.1), custom_call_target="tpu_custom_call" | custom-call | tf_op jit(solution)/shard_map/announce/pallas_call | solution.py:594
  14.0 0.0 copy-start.2
  14.1 2.2 %pack.1 = (s32[80]{0:T(128)S(1)}, f32[2,384,256]{2,1,0:T(8,128)S(1)}, f32[2,384,256]{2,1,0:T(8,128)S(1)}) custom-call(s32[40]{0:T(128)S(1)} %get-tuple-element.21.own_plan, s32[2,4]{1,0:T(2,128)S(1)} %get-tuple-element.22.prev_pos, s32[1]{0:T(128)} %get-tuple-element.23.prev_cnt, f32[2,256,2048]{2,1,0:T(8,128)S(1)} %get-tuple-element.24.tile, ...), custom_call_target="tpu_custom_call" | custom-call | tf_op jit(solution)/shard_map/pack/pallas_call | solution.py:617
  16.2 0.0 copy-start
  16.2 0.0 copy-done.2
  16.3 25.4 %exchange.1 = (f32[2,2,896,256]{3,2,1,0:T(8,128)S(1)}, f32[2,3,2,256,256]{4,3,2,1,0:T(8,128)S(1)}, f32[3,2,256,256]{3,2,1,0:T(8,128)S(1)}) custom-call(s32[80]{0:T(128)S(1)} %get-tuple-element.26.plan, f32[2,384,256]{2,1,0:T(8,128)S(1)} %get-tuple-element.27.ahead, f32[2,384,256]{2,1,0:T(8,128)S(1)} %get-tuple-element.28.behind, ...), custom_call_target="tpu_custom_call" | custom-call | tf_op jit(solution)/shard_map/exchange/pallas_call | solution.py:629
  41.6 0.0 copy-done
  41.7 3.8 %compute.1 = (f32[2,2,384,256]{3,2,1,0:T(8,128)S(1)}, f32[2,3,2,256,256]{4,3,2,1,0:T(8,128)S(1)}) custom-call(s32[80]{0:T(128)S(1)} %get-tuple-element.26.plan, f32[2,3,2,256,256]{4,3,2,1,0:T(8,128)S(1)} %get-tuple-element.29.windows, f32[3,2,256,256]{3,2,1,0:T(8,128)S(1)} %get-tuple-element.30.probes, f32[2,2,896,256]{3,2,1,0:T(8,128)S(1)} %get-tuple-element.31.received, ...), custom_call_target="tpu_custom_call" | custom-call | tf_op jit(solution)/shard_map/compute/pallas_call | solution.py:649
  45.5 26.0 %giveback.1 = (f32[2,2,448,256]{3,2,1,0:T(8,128)S(1)}, f32[2,256,2048]{2,1,0:T(8,128)S(1)}) custom-call(s32[80]{0:T(128)S(1)} %get-tuple-element.26.plan, f32[2,2,384,256]{3,2,1,0:T(8,128)S(1)} %get-tuple-element.32.rows, f32[2,3,2,256,256]{4,3,2,1,0:T(8,128)S(1)} %get-tuple-element.33.windows), custom_call_target="tpu_custom_call" | custom-call | tf_op jit(solution)/shard_map/giveback/pallas_call | solution.py:659
  71.5 2.6 %gather.1 = (f32[2,256,2048]{2,1,0:T(8,128)}, f32[2,256,2048]{2,1,0:T(8,128)S(1)}) custom-call(s32[80]{0:T(128)S(1)} %get-tuple-element.26.plan, f32[2,2,448,256]{3,2,1,0:T(8,128)S(1)} %get-tuple-element.34.rows, f32[2,256,2048]{2,1,0:T(8,128)S(1)} %get-tuple-element.35.tile_in), custom_call_target="tpu_custom_call", output_to_operand_aliasing={{1}: (2, {})} | custom-call | tf_op jit(solution)/shard_map/gather/pallas_call | solution.py:674
Async XLA Ops:
  0.7 1.2 %copy-start.1 = (f32[4,256,256]{2,1,0:T(8,128)S(1)}, f32[4,256,256]{2,1,0:T(8,128)}, u32[]{:S(2)}) copy-start(f32[4,256,256]{2,1,0:T(8,128)} %measured_hbm.1) | copy-start | bytes 3145732
  1.9 0.7 copy-start.3
  14.0 2.2 %copy-start.2 = (f32[2,256,256]{2,1,0:T(8,128)S(1)}, f32[2,256,256]{2,1,0:T(8,128)}, u32[]{:S(2)}) copy-start(f32[2,256,256]{2,1,0:T(8,128)} %probe.1) | copy-start | bytes 1572868
  16.2 25.4 %copy-start = (bf16[8,2,256,256]{3,2,1,0:T(8,128)(2,1)S(1)}, bf16[8,2,256,256]{3,2,1,0:T(8,128)(2,1)}, u32[]{:S(2)}) copy-start(bf16[8,2,256,256]{3,2,1,0:T(8,128)(2,1)} %constant.2.clone.table) | copy-start | bytes 6291460

commit v11 on v10

--- a/solution.py
+++ b/solution.py
@@ -98,10 +98,9 @@
     after = lax.rem(lat + 1, n_lat)
     before = lax.rem(lat + n_lat - 1, n_lat)
     barrier = pltpu.get_barrier_semaphore()
-    for other in (after, before):
-        pl.semaphore_signal(
-            barrier, inc=1, device_id=(depth, other), device_id_type=pl.DeviceIdType.MESH
-        )
+    pl.semaphore_signal(
+        barrier, inc=1, device_id=(depth, before), device_id_type=pl.DeviceIdType.MESH
+    )
     loads = [
         pltpu.make_async_copy(measured_hbm, measured, local.at[0]),
         pltpu.make_async_copy(tile_hbm, tile, local.at[1]),
@@ -110,7 +109,7 @@
     ]
     for load in loads:
         load.start()
-    pl.semaphore_wait(barrier, 2)
+    pl.semaphore_wait(barrier, 1)
     copies = [
         remote(pos_hbm, prev_pos, send.at[0], recv.at[0], depth, after),
         remote(cnt, prev_cnt, send.at[1], recv.at[1], depth, after),
@@ -208,8 +207,8 @@
     lat = lax.axis_index("lat")
     after = lax.rem(lat + 1, n_lat)
     before = lax.rem(lat + n_lat - 1, n_lat)
-    greet(depth, lat, after, before)
-    pl.semaphore_wait(pltpu.get_barrier_semaphore(), 4)
+    origin = jnp.where(depth == 0, after, before)
+    greet([(0, origin), (1, origin), (1 - depth, lat)])
 
     def slot(s):
         return received.at[s, :, pl.ds(PAD, ROWS), :]
@@ -273,18 +272,13 @@
     )
 
 
-def greet(depth, lat, after, before):
+def greet(sources):
     barrier = pltpu.get_barrier_semaphore()
-    partners = [
-        (depth, after),
-        (depth, before),
-        (1 - depth, jnp.where(depth == 0, after, before)),
-        (1 - depth, lat),
-    ]
-    for partner in partners:
+    for source in sources:
         pl.semaphore_signal(
-            barrier, inc=1, device_id=partner, device_id_type=pl.DeviceIdType.MESH
+            barrier, inc=1, device_id=source, device_id_type=pl.DeviceIdType.MESH
         )
+    pl.semaphore_wait(barrier, 3)
 
 
 def return_kernel(
@@ -295,8 +289,7 @@
     lat = lax.axis_index("lat")
     after = lax.rem(lat + 1, n_lat)
     before = lax.rem(lat + n_lat - 1, n_lat)
-    greet(depth, lat, after, before)
-    pl.semaphore_wait(pltpu.get_barrier_semaphore(), 4)
+    greet([(0, before), (1, after), (1 - depth, lat)])
     target = jnp.where(depth == 0, after, before)
 
     def part(c):

time: 74.3 us -> 73.8 us (level)
  no operation moved by 1% of the time
where the time goes in v11:
time: 73.8 us; the launch traced here: 73.7 us
  Pallas kernels  71 us (96%)
  local copies, waits for them, and re-layouts  1.91 us (3%)
    pallas_call x1, Pallas kernels, shards(): pl.pallas_call(functools.partial(return_kernel, n_lat), name='giveback',...  26 us
    pallas_call x1, Pallas kernels, shards(): pl.pallas_call(functools.partial(exchange_kernel, n_lat), name='exchange'...  25.4 us
    pallas_call x1, Pallas kernels, shards(): pl.pallas_call(functools.partial(announce_kernel, n_lat), name='announce'...  11 us
    pallas_call x1, Pallas kernels, shards(): pl.pallas_call(compute_kernel, name='compute', out_shape=(shape(2, 2, ROW...  3.85 us
    pallas_call x1, Pallas kernels, shards(): pl.pallas_call(gather_kernel, name='gather', out_shape=(shape(2, N, colum...  2.63 us
    pallas_call x1, Pallas kernels, shards(): pl.pallas_call(pack_kernel, name='pack', out_shape=(jax.ShapeDtypeStruct(...  2.17 us
    unnamed x8, local copies, waits for them, and re-layouts  1.91 us

profile of v11, /device:TPU:1, one launch (start us, length us, event | category | flops | bytes accessed | tf_op | source)
XLA Modules:
  0.0 73.7 jit_solution(2313116980779526814)
XLA Ops:
  0.7 0.0 copy-start.1
  0.7 1.2 %copy-done.1 = f32[4,256,256]{2,1,0:T(8,128)S(1)} copy-done((f32[4,256,256]{2,1,0:T(8,128)S(1)}, f32[4,256,256]{2,1,0:T(8,128)}, u32[]{:S(2)}) %copy-start.1) | copy-done | bytes 1048600
  1.9 0.0 copy-start.3
  1.9 0.7 copy-done.3
  2.6 11.0 %announce.1 = (s32[40]{0:T(128)S(1)}, s32[2,4]{1,0:T(2,128)S(1)}, s32[1]{0:T(128)}, f32[2,256,2048]{2,1,0:T(8,128)S(1)}, f32[4,256,256]{2,1,0:T(8,128)S(1)}) custom-call(s32[2,4]{1,0:T(2,128)S(1)} %bitcast.3, s32[1]{0:T(128)S(6)} %copy.9.cnt, f32[2,256,2048]{2,1,0:T(8,128)} %bitcast.4, f32[4,256,256]{2,1,0:T(8,128)S(1)} %copy-done.1), custom_call_target="tpu_custom_call" | custom-call | tf_op jit(solution)/shard_map/announce/pallas_call | solution.py:587
  13.6 0.0 copy-start.2
  13.6 2.2 %pack.1 = (s32[80]{0:T(128)S(1)}, f32[2,384,256]{2,1,0:T(8,128)S(1)}, f32[2,384,256]{2,1,0:T(8,128)S(1)}) custom-call(s32[40]{0:T(128)S(1)} %get-tuple-element.21.own_plan, s32[2,4]{1,0:T(2,128)S(1)} %get-tuple-element.22.prev_pos, s32[1]{0:T(128)} %get-tuple-element.23.prev_cnt, f32[2,256,2048]{2,1,0:T(8,128)S(1)} %get-tuple-element.24.tile, ...), custom_call_target="tpu_custom_call" | custom-call | tf_op jit(solution)/shard_map/pack/pallas_call | solution.py:610
  15.8 0.0 copy-start
  15.8 0.0 copy-done.2
  15.8 25.4 %exchange.1 = (f32[2,2,896,256]{3,2,1,0:T(8,128)S(1)}, f32[2,3,2,256,256]{4,3,2,1,0:T(8,128)S(1)}, f32[3,2,256,256]{3,2,1,0:T(8,128)S(1)}) custom-call(s32[80]{0:T(128)S(1)} %get-tuple-element.26.plan, f32[2,384,256]{2,1,0:T(8,128)S(1)} %get-tuple-element.27.ahead, f32[2,384,256]{2,1,0:T(8,128)S(1)} %get-tuple-element.28.behind, ...), custom_call_target="tpu_custom_call" | custom-call | tf_op jit(solution)/shard_map/exchange/pallas_call | solution.py:622
  41.2 0.0 copy-done
  41.2 3.9 %compute.1 = (f32[2,2,384,256]{3,2,1,0:T(8,128)S(1)}, f32[2,3,2,256,256]{4,3,2,1,0:T(8,128)S(1)}) custom-call(s32[80]{0:T(128)S(1)} %get-tuple-element.26.plan, f32[2,3,2,256,256]{4,3,2,1,0:T(8,128)S(1)} %get-tuple-element.29.windows, f32[3,2,256,256]{3,2,1,0:T(8,128)S(1)} %get-tuple-element.30.probes, f32[2,2,896,256]{3,2,1,0:T(8,128)S(1)} %get-tuple-element.31.received, ...), custom_call_target="tpu_custom_call" | custom-call | tf_op jit(solution)/shard_map/compute/pallas_call | solution.py:642
  45.1 26.0 %giveback.1 = (f32[2,2,448,256]{3,2,1,0:T(8,128)S(1)}, f32[2,256,2048]{2,1,0:T(8,128)S(1)}) custom-call(s32[80]{0:T(128)S(1)} %get-tuple-element.26.plan, f32[2,2,384,256]{3,2,1,0:T(8,128)S(1)} %get-tuple-element.32.rows, f32[2,3,2,256,256]{4,3,2,1,0:T(8,128)S(1)} %get-tuple-element.33.windows), custom_call_target="tpu_custom_call" | custom-call | tf_op jit(solution)/shard_map/giveback/pallas_call | solution.py:652
  71.0 2.6 %gather.1 = (f32[2,256,2048]{2,1,0:T(8,128)}, f32[2,256,2048]{2,1,0:T(8,128)S(1)}) custom-call(s32[80]{0:T(128)S(1)} %get-tuple-element.26.plan, f32[2,2,448,256]{3,2,1,0:T(8,128)S(1)} %get-tuple-element.34.rows, f32[2,256,2048]{2,1,0:T(8,128)S(1)} %get-tuple-element.35.tile_in), custom_call_target="tpu_custom_call", output_to_operand_aliasing={{1}: (2, {})} | custom-call | tf_op jit(solution)/shard_map/gather/pallas_call | solution.py:667
Async XLA Ops:
  0.7 1.2 %copy-start.1 = (f32[4,256,256]{2,1,0:T(8,128)S(1)}, f32[4,256,256]{2,1,0:T(8,128)}, u32[]{:S(2)}) copy-start(f32[4,256,256]{2,1,0:T(8,128)} %measured_hbm.1) | copy-start | bytes 3145732
  1.9 0.7 copy-start.3
  13.6 2.2 %copy-start.2 = (f32[2,256,256]{2,1,0:T(8,128)S(1)}, f32[2,256,256]{2,1,0:T(8,128)}, u32[]{:S(2)}) copy-start(f32[2,256,256]{2,1,0:T(8,128)} %probe.1) | copy-start | bytes 1572868
  15.8 25.4 %copy-start = (bf16[8,2,256,256]{3,2,1,0:T(8,128)(2,1)S(1)}, bf16[8,2,256,256]{3,2,1,0:T(8,128)(2,1)}, u32[]{:S(2)}) copy-start(bf16[8,2,256,256]{3,2,1,0:T(8,128)(2,1)} %constant.2.clone.table) | copy-start | bytes 6291460

commit v12 on v11

--- a/solution.py
+++ b/solution.py
@@ -89,9 +89,9 @@
 
 
 def announce_kernel(
-    n_lat, pos_hbm, cnt, tile_hbm, measured_hbm,
-    own_plan, prev_pos, prev_cnt, tile, apart,
-    measured, spread, pos, live, send, recv, local,
+    n_lat, pos_hbm, cnt, tile_hbm,
+    own_plan, prev_pos, prev_cnt, tile,
+    pos, live, send, recv, local,
 ):
     depth = lax.axis_index("depth")
     lat = lax.axis_index("lat")
@@ -102,10 +102,9 @@
         barrier, inc=1, device_id=(depth, before), device_id_type=pl.DeviceIdType.MESH
     )
     loads = [
-        pltpu.make_async_copy(measured_hbm, measured, local.at[0]),
-        pltpu.make_async_copy(tile_hbm, tile, local.at[1]),
-        pltpu.make_async_copy(pos_hbm, pos, local.at[2]),
-        pltpu.make_async_copy(cnt, live, local.at[3]),
+        pltpu.make_async_copy(tile_hbm, tile, local.at[0]),
+        pltpu.make_async_copy(pos_hbm, pos, local.at[1]),
+        pltpu.make_async_copy(cnt, live, local.at[2]),
     ]
     for load in loads:
         load.start()
@@ -116,33 +115,13 @@
     ]
     for copy in copies:
         copy.start()
-    row = lax.broadcasted_iota(jnp.int32, (N, N), 0)
-    lane = lax.broadcasted_iota(jnp.int32, (N, N), 1)
-    order = jnp.where(lane < HALF, 2 * lane, 2 * lane - (N - 1))
-    shuffle = jnp.where(row == order, 1.0, 0.0).astype(jnp.bfloat16)
-    loads[0].wait()
-    def rearrange(slot, carry):
-        hi, lo = halves(measured[slot])
-        columns = dot(
-            jnp.concatenate([hi, lo], axis=1), jnp.concatenate([shuffle, shuffle], axis=0)
-        )
-        for h in range(2):
-            spread[h] = columns[:, HALF * h : HALF * h + HALF]
-        for p in range(2):
-            for h in range(2):
-                apart[slot, HALF * p : HALF * p + HALF, HALF * h : HALF * h + HALF] = spread[
-                    h, pl.ds(p, HALF, stride=2), :
-                ]
-        return carry
-
-    lax.fori_loop(0, 4, rearrange, 0)
-    for load in loads[2:]:
+    for load in loads[1:]:
         load.wait()
     own = choose_sides([pos[0, i] for i in range(4)], [pos[1, i] for i in range(4)], live[0])
     for k, side in enumerate(own):
         for w, word in enumerate(side):
             own_plan[k * SPAN + w] = word
-    loads[1].wait()
+    loads[0].wait()
     for copy in copies:
         copy.wait()
 
@@ -448,12 +427,15 @@
 def compute_kernel(
     plan, windows, probes, received, measured, table,
     rows_out, grads,
-    amplitude,
+    amplitude, spread,
 ):
     depth = lax.axis_index("depth")
     at = jnp.where(depth == 0, OWN_LEFT, PREV_RIGHT)
     jobs = plan[at]
     row = lax.broadcasted_iota(jnp.int32, (N, N), 0)
+    lane = lax.broadcasted_iota(jnp.int32, (N, N), 1)
+    order = jnp.where(lane < HALF, 2 * lane, 2 * lane - (N - 1))
+    shuffle = jnp.where(row == order, 1.0, 0.0).astype(jnp.bfloat16)
 
     def work(numbers):
         each = range(len(numbers))
@@ -494,8 +476,24 @@
         spectra = to_spectrum([product(w, o) for w, o in zip(waves, slices)], table)
         backs = []
         for k in each:
+            hi, lo = halves(amplitude[k])
+            apart = dot(
+                jnp.concatenate([hi, lo], axis=1), jnp.concatenate([shuffle, shuffle], axis=0)
+            )
+            for h in range(2):
+                spread[k, h] = apart[:, HALF * h : HALF * h + HALF]
+        for k in each:
+            apart = jnp.concatenate(
+                [
+                    jnp.concatenate(
+                        [spread[k, h, pl.ds(p, HALF, stride=2), :] for h in range(2)], axis=1
+                    )
+                    for p in range(2)
+                ],
+                axis=0,
+            )
             re, im = spectra[k]
-            factor = 1.0 - amplitude[k] * lax.rsqrt(re * re + im * im + 1.0)
+            factor = 1.0 - apart * lax.rsqrt(re * re + im * im + 1.0)
             backs.append((re * factor, im * factor))
         backs = from_spectrum(backs, table)
         for k in each:
@@ -584,7 +582,7 @@
     tile = object_slices.reshape(object_slices.shape[1:])
     dma = pltpu.SemaphoreType.DMA
     positions = positions.T
-    own_plan, prev_positions, prev_counts, tile, measured = pl.pallas_call(
+    own_plan, prev_positions, prev_counts, tile = pl.pallas_call(
         functools.partial(announce_kernel, n_lat),
         name="announce",
         out_shape=(
@@ -592,21 +590,18 @@
             jax.ShapeDtypeStruct(positions.shape, jnp.int32),
             jax.ShapeDtypeStruct(counts.shape, jnp.int32),
             shape(*tile.shape),
-            shape(*measured.shape),
         ),
-        in_specs=[HBM, HBM, HBM, HBM],
-        out_specs=(SMEM, VMEM, VMEM, VMEM, VMEM),
+        in_specs=[HBM, HBM, HBM],
+        out_specs=(SMEM, VMEM, VMEM, VMEM),
         scratch_shapes=[
-            pltpu.VMEM((4, N, N), jnp.float32),
-            pltpu.VMEM((2, N, HALF), jnp.float32),
             pltpu.SMEM((2, 4), jnp.int32),
             pltpu.SMEM((1,), jnp.int32),
-            dma((2,)), dma((2,)), dma((4,)),
+            dma((2,)), dma((2,)), dma((3,)),
         ],
         compiler_params=pltpu.CompilerParams(
             collective_id=2, has_side_effects=True, vmem_limit_bytes=46 << 20
         ),
-    )(positions, counts, tile, measured)
+    )(positions, counts, tile)
     plan, ahead, behind = pl.pallas_call(
         pack_kernel,
         name="pack",
@@ -645,7 +640,10 @@
         out_shape=(shape(2, 2, ROWS, N), shape(2, MAX_JOBS, 2, N, N)),
         in_specs=[SMEM, VMEM, VMEM, VMEM, VMEM, VMEM],
         out_specs=(VMEM, VMEM),
-        scratch_shapes=[pltpu.VMEM((2, N, N), jnp.float32)],
+        scratch_shapes=[
+            pltpu.VMEM((2, N, N), jnp.float32),
+            pltpu.VMEM((2, 2, N, HALF), jnp.float32),
+        ],
         compiler_params=pltpu.CompilerParams(vmem_limit_bytes=30 << 20),
     )(plan, windows, probes, received, measured, table)
 

time: 73.8 us -> 73.5 us (level); the launches traced: 73.7 us -> 72.6 us
  local copies, waits for them, and re-layouts: 1.91 us -> 0.69 us
    unnamed x8, local copies, waits for them, and re-layouts: 1.91 us -> 0.69 us
where the time goes in v12:
time: 73.5 us; the launch traced here: 72.6 us
  Pallas kernels  71.1 us (97%)
  between operations  0.83 us (1%)
    pallas_call x1, Pallas kernels, shards(): pl.pallas_call(functools.partial(return_kernel, n_lat), name='giveback',...  26 us
    pallas_call x1, Pallas kernels, shards(): pl.pallas_call(functools.partial(exchange_kernel, n_lat), name='exchange'...  25.4 us
    pallas_call x1, Pallas kernels, shards(): pl.pallas_call(functools.partial(announce_kernel, n_lat), name='announce'...  10.9 us
    pallas_call x1, Pallas kernels, shards(): pl.pallas_call(compute_kernel, name='compute', out_shape=(shape(2, 2, ROW...  4.08 us
    pallas_call x1, Pallas kernels, shards(): pl.pallas_call(gather_kernel, name='gather', out_shape=(shape(2, N, colum...  2.61 us
    pallas_call x1, Pallas kernels, shards(): pl.pallas_call(pack_kernel, name='pack', out_shape=(jax.ShapeDtypeStruct(...  2.12 us

profile of v12, /device:TPU:1, one launch (start us, length us, event | category | flops | bytes accessed | tf_op | source)
XLA Modules:
  0.0 72.6 jit_solution(13963726455266650151)
XLA Ops:
  0.0 0.0 copy-start
  0.7 0.0 copy-start.3
  0.8 0.7 copy-done.3
  1.4 10.9 %announce.1 = (s32[40]{0:T(128)S(1)}, s32[2,4]{1,0:T(2,128)S(1)}, s32[1]{0:T(128)}, f32[2,256,2048]{2,1,0:T(8,128)S(1)}) custom-call(s32[2,4]{1,0:T(2,128)S(1)} %bitcast.3, s32[1]{0:T(128)S(6)} %copy.9.cnt, f32[2,256,2048]{2,1,0:T(8,128)} %bitcast.4), custom_call_target="tpu_custom_call" | custom-call | tf_op jit(solution)/shard_map/announce/pallas_call | solution.py:585
  12.3 0.0 copy-start.2
  12.4 0.0 copy-done
  12.4 2.1 %pack.1 = (s32[80]{0:T(128)S(1)}, f32[2,384,256]{2,1,0:T(8,128)S(1)}, f32[2,384,256]{2,1,0:T(8,128)S(1)}) custom-call(s32[40]{0:T(128)S(1)} %get-tuple-element.20.own_plan, s32[2,4]{1,0:T(2,128)S(1)} %get-tuple-element.21.prev_pos, s32[1]{0:T(128)} %get-tuple-element.22.prev_cnt, f32[2,256,2048]{2,1,0:T(8,128)S(1)} %get-tuple-element.23.tile, ...), custom_call_target="tpu_custom_call" | custom-call | tf_op jit(solution)/shard_map/pack/pallas_call | solution.py:605
  14.5 0.0 copy-start.1
  14.5 0.0 copy-done.2
  14.5 25.4 %exchange.1 = (f32[2,2,896,256]{3,2,1,0:T(8,128)S(1)}, f32[2,3,2,256,256]{4,3,2,1,0:T(8,128)S(1)}, f32[3,2,256,256]{3,2,1,0:T(8,128)S(1)}) custom-call(s32[80]{0:T(128)S(1)} %get-tuple-element.24.plan, f32[2,384,256]{2,1,0:T(8,128)S(1)} %get-tuple-element.25.ahead, f32[2,384,256]{2,1,0:T(8,128)S(1)} %get-tuple-element.26.behind, ...), custom_call_target="tpu_custom_call" | custom-call | tf_op jit(solution)/shard_map/exchange/pallas_call | solution.py:617
  39.9 0.0 copy-done.1
  39.9 4.1 %compute.1 = (f32[2,2,384,256]{3,2,1,0:T(8,128)S(1)}, f32[2,3,2,256,256]{4,3,2,1,0:T(8,128)S(1)}) custom-call(s32[80]{0:T(128)S(1)} %get-tuple-element.24.plan, f32[2,3,2,256,256]{4,3,2,1,0:T(8,128)S(1)} %get-tuple-element.27.windows, f32[3,2,256,256]{3,2,1,0:T(8,128)S(1)} %get-tuple-element.28.probes, f32[2,2,896,256]{3,2,1,0:T(8,128)S(1)} %get-tuple-element.29.received, ...), custom_call_target="tpu_custom_call" | custom-call | tf_op jit(solution)/shard_map/compute/pallas_call | solution.py:637
  44.0 26.0 %giveback.1 = (f32[2,2,448,256]{3,2,1,0:T(8,128)S(1)}, f32[2,256,2048]{2,1,0:T(8,128)S(1)}) custom-call(s32[80]{0:T(128)S(1)} %get-tuple-element.24.plan, f32[2,2,384,256]{3,2,1,0:T(8,128)S(1)} %get-tuple-element.30.rows, f32[2,3,2,256,256]{4,3,2,1,0:T(8,128)S(1)} %get-tuple-element.31.windows), custom_call_target="tpu_custom_call" | custom-call | tf_op jit(solution)/shard_map/giveback/pallas_call | solution.py:650
  70.0 2.6 %gather.1 = (f32[2,256,2048]{2,1,0:T(8,128)}, f32[2,256,2048]{2,1,0:T(8,128)S(1)}) custom-call(s32[80]{0:T(128)S(1)} %get-tuple-element.24.plan, f32[2,2,448,256]{3,2,1,0:T(8,128)S(1)} %get-tuple-element.32.rows, f32[2,256,2048]{2,1,0:T(8,128)S(1)} %get-tuple-element.33.tile_in), custom_call_target="tpu_custom_call", output_to_operand_aliasing={{1}: (2, {})} | custom-call | tf_op jit(solution)/shard_map/gather/pallas_call | solution.py:665
Async XLA Ops:
  0.0 12.4 %copy-start = (f32[4,256,256]{2,1,0:T(8,128)S(1)}, f32[4,256,256]{2,1,0:T(8,128)}, u32[]{:S(2)}) copy-start(f32[4,256,256]{2,1,0:T(8,128)} %measured.3) | copy-start | bytes 3145732
  0.7 0.7 copy-start.3
  12.3 2.2 %copy-start.2 = (f32[2,256,256]{2,1,0:T(8,128)S(1)}, f32[2,256,256]{2,1,0:T(8,128)}, u32[]{:S(2)}) copy-start(f32[2,256,256]{2,1,0:T(8,128)} %probe.1) | copy-start | bytes 1572868
  14.5 25.4 %copy-start.1 = (bf16[8,2,256,256]{3,2,1,0:T(8,128)(2,1)S(1)}, bf16[8,2,256,256]{3,2,1,0:T(8,128)(2,1)}, u32[]{:S(2)}) copy-start(bf16[8,2,256,256]{3,2,1,0:T(8,128)(2,1)} %constant.2.clone.table) | copy-start | bytes 6291460

commit v13 on v12

--- a/solution.py
+++ b/solution.py
@@ -534,6 +534,14 @@
     row = lax.broadcasted_iota(jnp.int32, (CHUNK, N), 0)
     lane = lax.broadcasted_iota(jnp.int32, (CHUNK, N), 1)
 
+    def stores(c):
+        return [
+            pltpu.make_async_copy(
+                tile.at[c, pl.ds(64 * q, 64)], out.at[c, pl.ds(64 * q, 64)], out_sems.at[c, q]
+            )
+            for q in range(N // 64)
+        ]
+
     def add(at, j, c, lower):
         r = plan[at + 2 + 5 * j]
         start = plan[at + 2 + 5 * j + 3]
@@ -563,9 +571,11 @@
                 return carry
 
             lax.fori_loop(0, plan[at], step, 0)
-        pltpu.make_async_copy(tile.at[c], out.at[c], out_sems.at[c]).start()
+        for copy in stores(c):
+            copy.start()
     for c in range(2):
-        pltpu.make_async_copy(tile.at[c], out.at[c], out_sems.at[c]).wait()
+        for copy in stores(c):
+            copy.wait()
 
 
 SMEM = pl.BlockSpec(memory_space=pltpu.SMEM)
@@ -668,7 +678,7 @@
         out_shape=(shape(2, N, columns), shape(2, N, columns)),
         in_specs=[SMEM, VMEM, VMEM],
         out_specs=(HBM, VMEM),
-        scratch_shapes=[dma((2,))],
+        scratch_shapes=[dma((2, N // 64))],
         input_output_aliases={2: 1},
         compiler_params=pltpu.CompilerParams(vmem_limit_bytes=12 << 20),
     )(plan, rows_back, tile)

time: 73.5 us -> 73 us (level); the launches traced: 72.6 us -> 72.8 us
  no operation moved by 1% of the time
where the time goes in v13:
time: 73 us; the launch traced here: 72.8 us
  Pallas kernels  71.3 us (98%)
  between operations  0.83 us (1%)
    pallas_call x1, Pallas kernels, shards(): pl.pallas_call(functools.partial(return_kernel, n_lat), name='giveback',...  26 us
    pallas_call x1, Pallas kernels, shards(): pl.pallas_call(functools.partial(exchange_kernel, n_lat), name='exchange'...  25.4 us
    pallas_call x1, Pallas kernels, shards(): pl.pallas_call(functools.partial(announce_kernel, n_lat), name='announce'...  10.9 us
    pallas_call x1, Pallas kernels, shards(): pl.pallas_call(compute_kernel, name='compute', out_shape=(shape(2, 2, ROW...  4.14 us
    pallas_call x1, Pallas kernels, shards(): pl.pallas_call(gather_kernel, name='gather', out_shape=(shape(2, N, colum...  2.7 us
    pallas_call x1, Pallas kernels, shards(): pl.pallas_call(pack_kernel, name='pack', out_shape=(jax.ShapeDtypeStruct(...  2.21 us

profile of v13, /device:TPU:1, one launch (start us, length us, event | category | flops | bytes accessed | tf_op | source)
XLA Modules:
  0.0 72.8 jit_solution(15221155782754029759)
XLA Ops:
  0.0 0.0 copy-start
  0.7 0.0 copy-start.3
  0.8 0.7 copy-done.3
  1.4 10.9 %announce.1 = (s32[40]{0:T(128)S(1)}, s32[2,4]{1,0:T(2,128)S(1)}, s32[1]{0:T(128)}, f32[2,256,2048]{2,1,0:T(8,128)S(1)}) custom-call(s32[2,4]{1,0:T(2,128)S(1)} %bitcast.3, s32[1]{0:T(128)S(6)} %copy.9.cnt, f32[2,256,2048]{2,1,0:T(8,128)} %bitcast.4), custom_call_target="tpu_custom_call" | custom-call | tf_op jit(solution)/shard_map/announce/pallas_call | solution.py:595
  12.3 0.0 copy-start.2
  12.4 0.0 copy-done
  12.4 2.2 %pack.1 = (s32[80]{0:T(128)S(1)}, f32[2,384,256]{2,1,0:T(8,128)S(1)}, f32[2,384,256]{2,1,0:T(8,128)S(1)}) custom-call(s32[40]{0:T(128)S(1)} %get-tuple-element.20.own_plan, s32[2,4]{1,0:T(2,128)S(1)} %get-tuple-element.21.prev_pos, s32[1]{0:T(128)} %get-tuple-element.22.prev_cnt, f32[2,256,2048]{2,1,0:T(8,128)S(1)} %get-tuple-element.23.tile, ...), custom_call_target="tpu_custom_call" | custom-call | tf_op jit(solution)/shard_map/pack/pallas_call | solution.py:615
  14.6 0.0 copy-start.1
  14.6 0.0 copy-done.2
  14.6 25.4 %exchange.1 = (f32[2,2,896,256]{3,2,1,0:T(8,128)S(1)}, f32[2,3,2,256,256]{4,3,2,1,0:T(8,128)S(1)}, f32[3,2,256,256]{3,2,1,0:T(8,128)S(1)}) custom-call(s32[80]{0:T(128)S(1)} %get-tuple-element.24.plan, f32[2,384,256]{2,1,0:T(8,128)S(1)} %get-tuple-element.25.ahead, f32[2,384,256]{2,1,0:T(8,128)S(1)} %get-tuple-element.26.behind, ...), custom_call_target="tpu_custom_call" | custom-call | tf_op jit(solution)/shard_map/exchange/pallas_call | solution.py:627
  40.0 0.0 copy-done.1
  40.0 4.1 %compute.1 = (f32[2,2,384,256]{3,2,1,0:T(8,128)S(1)}, f32[2,3,2,256,256]{4,3,2,1,0:T(8,128)S(1)}) custom-call(s32[80]{0:T(128)S(1)} %get-tuple-element.24.plan, f32[2,3,2,256,256]{4,3,2,1,0:T(8,128)S(1)} %get-tuple-element.27.windows, f32[3,2,256,256]{3,2,1,0:T(8,128)S(1)} %get-tuple-element.28.probes, f32[2,2,896,256]{3,2,1,0:T(8,128)S(1)} %get-tuple-element.29.received, ...), custom_call_target="tpu_custom_call" | custom-call | tf_op jit(solution)/shard_map/compute/pallas_call | solution.py:647
  44.2 26.0 %giveback.1 = (f32[2,2,448,256]{3,2,1,0:T(8,128)S(1)}, f32[2,256,2048]{2,1,0:T(8,128)S(1)}) custom-call(s32[80]{0:T(128)S(1)} %get-tuple-element.24.plan, f32[2,2,384,256]{3,2,1,0:T(8,128)S(1)} %get-tuple-element.30.rows, f32[2,3,2,256,256]{4,3,2,1,0:T(8,128)S(1)} %get-tuple-element.31.windows), custom_call_target="tpu_custom_call" | custom-call | tf_op jit(solution)/shard_map/giveback/pallas_call | solution.py:660
  70.1 2.7 %gather.1 = (f32[2,256,2048]{2,1,0:T(8,128)}, f32[2,256,2048]{2,1,0:T(8,128)S(1)}) custom-call(s32[80]{0:T(128)S(1)} %get-tuple-element.24.plan, f32[2,2,448,256]{3,2,1,0:T(8,128)S(1)} %get-tuple-element.32.rows, f32[2,256,2048]{2,1,0:T(8,128)S(1)} %get-tuple-element.33.tile_in), custom_call_target="tpu_custom_call", output_to_operand_aliasing={{1}: (2, {})} | custom-call | tf_op jit(solution)/shard_map/gather/pallas_call | solution.py:675
Async XLA Ops:
  0.0 12.4 %copy-start = (f32[4,256,256]{2,1,0:T(8,128)S(1)}, f32[4,256,256]{2,1,0:T(8,128)}, u32[]{:S(2)}) copy-start(f32[4,256,256]{2,1,0:T(8,128)} %measured.3) | copy-start | bytes 3145732
  0.7 0.7 copy-start.3
  12.3 2.3 %copy-start.2 = (f32[2,256,256]{2,1,0:T(8,128)S(1)}, f32[2,256,256]{2,1,0:T(8,128)}, u32[]{:S(2)}) copy-start(f32[2,256,256]{2,1,0:T(8,128)} %probe.1) | copy-start | bytes 1572868
  14.6 25.4 %copy-start.1 = (bf16[8,2,256,256]{3,2,1,0:T(8,128)(2,1)S(1)}, bf16[8,2,256,256]{3,2,1,0:T(8,128)(2,1)}, u32[]{:S(2)}) copy-start(bf16[8,2,256,256]{3,2,1,0:T(8,128)(2,1)} %constant.2.clone.table) | copy-start | bytes 6291460

commit v14 on v12

--- a/solution.py
+++ b/solution.py
@@ -102,9 +102,16 @@
         barrier, inc=1, device_id=(depth, before), device_id_type=pl.DeviceIdType.MESH
     )
     loads = [
-        pltpu.make_async_copy(tile_hbm, tile, local.at[0]),
-        pltpu.make_async_copy(pos_hbm, pos, local.at[1]),
-        pltpu.make_async_copy(cnt, live, local.at[2]),
+        pltpu.make_async_copy(pos_hbm, pos, local.at[0]),
+        pltpu.make_async_copy(cnt, live, local.at[1]),
+    ] + [
+        pltpu.make_async_copy(
+            tile_hbm.at[c, pl.ds(HALF * h, HALF)],
+            tile.at[c, pl.ds(HALF * h, HALF)],
+            local.at[2 + 2 * c + h],
+        )
+        for c in range(2)
+        for h in range(2)
     ]
     for load in loads:
         load.start()
@@ -115,13 +122,14 @@
     ]
     for copy in copies:
         copy.start()
-    for load in loads[1:]:
+    for load in loads[:2]:
         load.wait()
     own = choose_sides([pos[0, i] for i in range(4)], [pos[1, i] for i in range(4)], live[0])
     for k, side in enumerate(own):
         for w, word in enumerate(side):
             own_plan[k * SPAN + w] = word
-    loads[0].wait()
+    for load in loads[2:]:
+        load.wait()
     for copy in copies:
         copy.wait()
 
@@ -596,7 +604,7 @@
         scratch_shapes=[
             pltpu.SMEM((2, 4), jnp.int32),
             pltpu.SMEM((1,), jnp.int32),
-            dma((2,)), dma((2,)), dma((3,)),
+            dma((2,)), dma((2,)), dma((6,)),
         ],
         compiler_params=pltpu.CompilerParams(
             collective_id=2, has_side_effects=True, vmem_limit_bytes=46 << 20

time: 73.5 us -> 72.9 us (level)
  no operation moved by 1% of the time
where the time goes in v14:
time: 72.9 us; the launch traced here: 72.5 us
  Pallas kernels  71 us (97%)
  between operations  0.83 us (1%)
    pallas_call x1, Pallas kernels, shards(): pl.pallas_call(functools.partial(return_kernel, n_lat), name='giveback',...  26 us
    pallas_call x1, Pallas kernels, shards(): pl.pallas_call(functools.partial(exchange_kernel, n_lat), name='exchange'...  25.4 us
    pallas_call x1, Pallas kernels, shards(): pl.pallas_call(functools.partial(announce_kernel, n_lat), name='announce'...  10.9 us
    pallas_call x1, Pallas kernels, shards(): pl.pallas_call(compute_kernel, name='compute', out_shape=(shape(2, 2, ROW...  4.06 us
    pallas_call x1, Pallas kernels, shards(): pl.pallas_call(gather_kernel, name='gather', out_shape=(shape(2, N, colum...  2.58 us
    pallas_call x1, Pallas kernels, shards(): pl.pallas_call(pack_kernel, name='pack', out_shape=(jax.ShapeDtypeStruct(...  2.06 us

profile of v14, /device:TPU:1, one launch (start us, length us, event | category | flops | bytes accessed | tf_op | source)
XLA Modules:
  0.0 72.5 jit_solution(7802147397586381581)
XLA Ops:
  0.0 0.0 copy-start
  0.7 0.0 copy-start.3
  0.8 0.7 copy-done.3
  1.4 10.9 %announce.1 = (s32[40]{0:T(128)S(1)}, s32[2,4]{1,0:T(2,128)S(1)}, s32[1]{0:T(128)}, f32[2,256,2048]{2,1,0:T(8,128)S(1)}) custom-call(s32[2,4]{1,0:T(2,128)S(1)} %bitcast.3, s32[1]{0:T(128)S(6)} %copy.9.cnt, f32[2,256,2048]{2,1,0:T(8,128)} %bitcast.4), custom_call_target="tpu_custom_call" | custom-call | tf_op jit(solution)/shard_map/announce/pallas_call | solution.py:593
  12.4 0.0 copy-start.2
  12.4 0.0 copy-done
  12.4 2.1 %pack.1 = (s32[80]{0:T(128)S(1)}, f32[2,384,256]{2,1,0:T(8,128)S(1)}, f32[2,384,256]{2,1,0:T(8,128)S(1)}) custom-call(s32[40]{0:T(128)S(1)} %get-tuple-element.20.own_plan, s32[2,4]{1,0:T(2,128)S(1)} %get-tuple-element.21.prev_pos, s32[1]{0:T(128)} %get-tuple-element.22.prev_cnt, f32[2,256,2048]{2,1,0:T(8,128)S(1)} %get-tuple-element.23.tile, ...), custom_call_target="tpu_custom_call" | custom-call | tf_op jit(solution)/shard_map/pack/pallas_call | solution.py:613
  14.5 0.0 copy-start.1
  14.5 0.0 copy-done.2
  14.5 25.4 %exchange.1 = (f32[2,2,896,256]{3,2,1,0:T(8,128)S(1)}, f32[2,3,2,256,256]{4,3,2,1,0:T(8,128)S(1)}, f32[3,2,256,256]{3,2,1,0:T(8,128)S(1)}) custom-call(s32[80]{0:T(128)S(1)} %get-tuple-element.24.plan, f32[2,384,256]{2,1,0:T(8,128)S(1)} %get-tuple-element.25.ahead, f32[2,384,256]{2,1,0:T(8,128)S(1)} %get-tuple-element.26.behind, ...), custom_call_target="tpu_custom_call" | custom-call | tf_op jit(solution)/shard_map/exchange/pallas_call | solution.py:625
  39.9 0.0 copy-done.1
  39.9 4.1 %compute.1 = (f32[2,2,384,256]{3,2,1,0:T(8,128)S(1)}, f32[2,3,2,256,256]{4,3,2,1,0:T(8,128)S(1)}) custom-call(s32[80]{0:T(128)S(1)} %get-tuple-element.24.plan, f32[2,3,2,256,256]{4,3,2,1,0:T(8,128)S(1)} %get-tuple-element.27.windows, f32[3,2,256,256]{3,2,1,0:T(8,128)S(1)} %get-tuple-element.28.probes, f32[2,2,896,256]{3,2,1,0:T(8,128)S(1)} %get-tuple-element.29.received, ...), custom_call_target="tpu_custom_call" | custom-call | tf_op jit(solution)/shard_map/compute/pallas_call | solution.py:645
  44.0 26.0 %giveback.1 = (f32[2,2,448,256]{3,2,1,0:T(8,128)S(1)}, f32[2,256,2048]{2,1,0:T(8,128)S(1)}) custom-call(s32[80]{0:T(128)S(1)} %get-tuple-element.24.plan, f32[2,2,384,256]{3,2,1,0:T(8,128)S(1)} %get-tuple-element.30.rows, f32[2,3,2,256,256]{4,3,2,1,0:T(8,128)S(1)} %get-tuple-element.31.windows), custom_call_target="tpu_custom_call" | custom-call | tf_op jit(solution)/shard_map/giveback/pallas_call | solution.py:658
  70.0 2.6 %gather.1 = (f32[2,256,2048]{2,1,0:T(8,128)}, f32[2,256,2048]{2,1,0:T(8,128)S(1)}) custom-call(s32[80]{0:T(128)S(1)} %get-tuple-element.24.plan, f32[2,2,448,256]{3,2,1,0:T(8,128)S(1)} %get-tuple-element.32.rows, f32[2,256,2048]{2,1,0:T(8,128)S(1)} %get-tuple-element.33.tile_in), custom_call_target="tpu_custom_call", output_to_operand_aliasing={{1}: (2, {})} | custom-call | tf_op jit(solution)/shard_map/gather/pallas_call | solution.py:673
Async XLA Ops:
  0.0 12.4 %copy-start = (f32[4,256,256]{2,1,0:T(8,128)S(1)}, f32[4,256,256]{2,1,0:T(8,128)}, u32[]{:S(2)}) copy-start(f32[4,256,256]{2,1,0:T(8,128)} %measured.3) | copy-start | bytes 3145732
  0.7 0.7 copy-start.3
  12.4 2.1 %copy-start.2 = (f32[2,256,256]{2,1,0:T(8,128)S(1)}, f32[2,256,256]{2,1,0:T(8,128)}, u32[]{:S(2)}) copy-start(f32[2,256,256]{2,1,0:T(8,128)} %probe.1) | copy-start | bytes 1572868
  14.5 25.4 %copy-start.1 = (bf16[8,2,256,256]{3,2,1,0:T(8,128)(2,1)S(1)}, bf16[8,2,256,256]{3,2,1,0:T(8,128)(2,1)}, u32[]{:S(2)}) copy-start(bf16[8,2,256,256]{3,2,1,0:T(8,128)(2,1)} %constant.2.clone.table) | copy-start | bytes 6291460
